TPU v7x, 32 devices: a whole 2x2x4 slice. The times are simulated.
32 devices in a mesh: dp: 4 (over y, x), ctx: 8 (over z, core).
Axes of the slice: x: 2, y: 2, z: 4, core: 2. Of those that a mesh axis runs over, the one named last changes fastest.
Arguments:
- block_input: bfloat16 [4, 2048, 768], P('dp', 'ctx'), may hold values from -6 to 6
- doc_ids: int32 [4, 2048], P('dp', 'ctx'), may hold values from 0 to 7, never falling along the last dimension, each value on 1 to 1536 neighbouring positions
- out_grad: bfloat16 [4, 2048, 768], P('dp', 'ctx'), may hold values from -6 to 6
- ln1_gain: bfloat16 [2, 768], P(None, ('dp', 'ctx')), may hold values from 0.5 to 1.5
- ln1_bias: bfloat16 [2, 768], P(None, ('dp', 'ctx')), may hold values from -3 to 3
- w_qkv: bfloat16 [2, 768, 2304], P(None, ('dp', 'ctx')), may hold values from -0.21875 to 0.21875
- b_query: bfloat16 [2, 768], P(None, ('dp', 'ctx')), may hold values from -3 to 3
- b_value: bfloat16 [2, 768], P(None, ('dp', 'ctx')), may hold values from -3 to 3
- w_out: bfloat16 [2, 768, 768], P(None, ('dp', 'ctx')), may hold values from -0.875 to 0.875
- b_out: bfloat16 [2, 768], P(None, ('dp', 'ctx')), may hold values from -3 to 3
- ln2_gain: bfloat16 [2, 768], P(None, ('dp', 'ctx')), may hold values from 0.5 to 1.5
- ln2_bias: bfloat16 [2, 768], P(None, ('dp', 'ctx')), may hold values from -3 to 3
- w_fc: bfloat16 [2, 768, 3072], P(None, ('dp', 'ctx')), may hold values from -0.21875 to 0.21875
- b_fc: bfloat16 [2, 3072], P(None, ('dp', 'ctx')), may hold values from -3 to 3
- w_proj: bfloat16 [2, 3072, 768], P(None, ('dp', 'ctx')), may hold values from -0.109375 to 0.109375
- b_proj: bfloat16 [2, 768], P(None, ('dp', 'ctx')), may hold values from -3 to 3
Outputs:
- block_output: bfloat16 [4, 2048, 768], P('dp', 'ctx')
- grad_input: bfloat16 [4, 2048, 768], P('dp', 'ctx')
- grad_ln1_gain: float32 [2, 768], P(None, ('dp', 'ctx'))
- grad_ln1_bias: float32 [2, 768], P(None, ('dp', 'ctx'))
- grad_w_qkv: float32 [2, 768, 2304], P(None, ('dp', 'ctx'))
- grad_b_query: float32 [2, 768], P(None, ('dp', 'ctx'))
- grad_b_value: float32 [2, 768], P(None, ('dp', 'ctx'))
- grad_w_out: float32 [2, 768, 768], P(None, ('dp', 'ctx'))
- grad_b_out: float32 [2, 768], P(None, ('dp', 'ctx'))
- grad_ln2_gain: float32 [2, 768], P(None, ('dp', 'ctx'))
- grad_ln2_bias: float32 [2, 768], P(None, ('dp', 'ctx'))
- grad_w_fc: float32 [2, 768, 3072], P(None, ('dp', 'ctx'))
- grad_b_fc: float32 [2, 3072], P(None, ('dp', 'ctx'))
- grad_w_proj: float32 [2, 3072, 768], P(None, ('dp', 'ctx'))
- grad_b_proj: float32 [2, 768], P(None, ('dp', 'ctx'))
Inputs may be any that keep to these rules, and one draw needn't show every extreme that they name: `doc_ids`: along each sequence the document numbers never fall; a document covers 1 to 1536 positions, and one covers exactly 1536.
All inputs are finite; a program needn't handle non-finite values.
Results may differ from a plain program's by a relative error of at most 0.03.
Values may be sent and summed in bfloat16 or wider, within the bound.
A program may use at most 256 MiB of HBM per device.

v0:
```python
import jax
import jax.numpy as jnp
from jax import lax
from jax.sharding import PartitionSpec as P

HEAD = 64
LAYERS = 2


norm_eps = 1e-05
masked_value = -1e30
gelu_coeff = 0.7978845608028654
cubic_coeff = 0.044715
key_block = 512


def layer_norm(residual, norm_gain, norm_bias):
    row_mean = jnp.mean(residual, axis=-1, keepdims=True)
    centered = residual - row_mean
    variance = jnp.mean(centered * centered, axis=-1, keepdims=True)
    inv_std = lax.rsqrt(variance + norm_eps)
    normed = centered * inv_std
    return (normed * norm_gain + norm_bias, normed, inv_std)


def norm_back(grad_norm, normed, inv_std, norm_gain):
    scaled = grad_norm * norm_gain
    return inv_std * (
        scaled
        - jnp.mean(scaled, axis=-1, keepdims=True)
        - normed * jnp.mean(scaled * normed, axis=-1, keepdims=True)
    )


def gelu_value(values_in):
    inner_arg = gelu_coeff * (values_in + cubic_coeff * values_in * values_in * values_in)
    return 0.5 * values_in * (1.0 + jnp.tanh(inner_arg))


def gelu_slope(values_in):
    tanh_val = jnp.tanh(gelu_coeff * (values_in + cubic_coeff * values_in * values_in * values_in))
    return 0.5 * (1.0 + tanh_val) + 0.5 * values_in * (1.0 - tanh_val * tanh_val) * gelu_coeff * (
        1.0 + 3.0 * cubic_coeff * values_in * values_in
    )


def forward_layer(residual, layer_params, attend_fwd):
    (
        norm1_gain,
        norm1_bias,
        qkv_weight,
        query_bias,
        value_bias,
        out_weight,
        out_bias,
        norm2_gain,
        norm2_bias,
        fc_weight,
        fc_bias,
        proj_weight,
        proj_bias,
    ) = layer_params
    model_width = residual.shape[1]
    normed_in, normed1, inv_std1 = layer_norm(
        residual, norm1_gain.astype(jnp.float32), norm1_bias.astype(jnp.float32)
    )
    attn_in = normed_in.astype(jnp.bfloat16)
    projected = jnp.dot(attn_in, qkv_weight, preferred_element_type=jnp.float32)
    queries = (projected[:, :model_width] + query_bias.astype(jnp.float32)).astype(jnp.bfloat16)
    keys = projected[:, model_width : 2 * model_width].astype(jnp.bfloat16)
    values = (projected[:, 2 * model_width :] + value_bias.astype(jnp.float32)).astype(jnp.bfloat16)
    mixed_rows, log_total = attend_fwd(queries, keys, values)
    middle = (
        residual
        + jnp.dot(mixed_rows, out_weight, preferred_element_type=jnp.float32)
        + out_bias.astype(jnp.float32)
    )
    normed_mid, normed2, inv_std2 = layer_norm(
        middle, norm2_gain.astype(jnp.float32), norm2_bias.astype(jnp.float32)
    )
    ffn_in = normed_mid.astype(jnp.bfloat16)
    pre_act = jnp.dot(ffn_in, fc_weight, preferred_element_type=jnp.float32) + fc_bias.astype(
        jnp.float32
    )
    hidden = gelu_value(pre_act).astype(jnp.bfloat16)
    result = (
        middle
        + jnp.dot(hidden, proj_weight, preferred_element_type=jnp.float32)
        + proj_bias.astype(jnp.float32)
    )
    return (
        result,
        (
            normed1,
            inv_std1,
            attn_in,
            queries,
            keys,
            values,
            mixed_rows,
            log_total,
            normed2,
            inv_std2,
            ffn_in,
            pre_act,
            hidden,
        ),
    )


def backward_layer(grad_residual, saved_rows, layer_params, attend_back):
    (
        normed1,
        inv_std1,
        attn_in,
        queries,
        keys,
        values,
        mixed_rows,
        log_total,
        normed2,
        inv_std2,
        ffn_in,
        pre_act,
        hidden,
    ) = saved_rows
    (
        norm1_gain,
        norm1_bias,
        qkv_weight,
        query_bias,
        value_bias,
        out_weight,
        out_bias,
        norm2_gain,
        norm2_bias,
        fc_weight,
        fc_bias,
        proj_weight,
        proj_bias,
    ) = layer_params
    grad_narrow = grad_residual.astype(jnp.bfloat16)
    grad_proj_w = jnp.dot(hidden.T, grad_narrow, preferred_element_type=jnp.float32)
    grad_proj_b = jnp.sum(grad_residual, axis=0)
    grad_hidden = jnp.dot(grad_narrow, proj_weight.T, preferred_element_type=jnp.float32)
    grad_pre = grad_hidden * gelu_slope(pre_act)
    pre_narrow = grad_pre.astype(jnp.bfloat16)
    grad_fc_w = jnp.dot(ffn_in.T, pre_narrow, preferred_element_type=jnp.float32)
    grad_fc_b = jnp.sum(grad_pre, axis=0)
    grad_norm2 = jnp.dot(pre_narrow, fc_weight.T, preferred_element_type=jnp.float32)
    grad_gain2 = jnp.sum(grad_norm2 * normed2, axis=0)
    grad_bias2 = jnp.sum(grad_norm2, axis=0)
    grad_middle = grad_residual + norm_back(
        grad_norm2, normed2, inv_std2, norm2_gain.astype(jnp.float32)
    )
    middle_narrow = grad_middle.astype(jnp.bfloat16)
    grad_out_w = jnp.dot(mixed_rows.T, middle_narrow, preferred_element_type=jnp.float32)
    grad_out_b = jnp.sum(grad_middle, axis=0)
    grad_mixed = jnp.dot(middle_narrow, out_weight.T, preferred_element_type=jnp.float32).astype(
        jnp.bfloat16
    )
    grad_queries, grad_keys, grad_values = attend_back(
        queries, keys, values, mixed_rows, grad_mixed, log_total
    )
    proj_narrow = jnp.concatenate([grad_queries, grad_keys, grad_values], axis=1).astype(
        jnp.bfloat16
    )
    grad_qkv_w = jnp.dot(attn_in.T, proj_narrow, preferred_element_type=jnp.float32)
    grad_query_b = jnp.sum(grad_queries, axis=0)
    grad_value_b = jnp.sum(grad_values, axis=0)
    grad_norm1 = jnp.dot(proj_narrow, qkv_weight.T, preferred_element_type=jnp.float32)
    grad_gain1 = jnp.sum(grad_norm1 * normed1, axis=0)
    grad_bias1 = jnp.sum(grad_norm1, axis=0)
    grad_before = grad_middle + norm_back(
        grad_norm1, normed1, inv_std1, norm1_gain.astype(jnp.float32)
    )
    return (
        grad_before,
        (
            grad_gain1,
            grad_bias1,
            grad_qkv_w,
            grad_query_b,
            grad_value_b,
            grad_out_w,
            grad_out_b,
            grad_gain2,
            grad_bias2,
            grad_fc_w,
            grad_fc_b,
            grad_proj_w,
            grad_proj_b,
        ),
    )


def visible(key_ids, key_places, query_ids, query_places):
    same_doc = key_ids[:, None, :] == query_ids[:, :, None]
    causal = key_places[None, :] <= query_places[:, None]
    return (same_doc & causal[None])[:, None]


def shards(
    block_input,
    doc_ids,
    out_grad,
    ln1_gain,
    ln1_bias,
    w_qkv,
    b_query,
    b_value,
    w_out,
    b_out,
    ln2_gain,
    ln2_bias,
    w_fc,
    b_fc,
    w_proj,
    b_proj,
):
    seq_count, local_len, model_width = block_input.shape
    head_count = model_width // HEAD
    row_count = seq_count * local_len
    score_scale = HEAD ** (-0.5)
    ctx_rank = lax.axis_index("ctx")
    all_ids = lax.all_gather(doc_ids, "ctx", axis=1, tiled=True)
    seq_length = all_ids.shape[1]
    query_pos = ctx_rank * local_len + jnp.arange(local_len, dtype=jnp.int32)

    def split_heads(three_dim):
        return three_dim.reshape(three_dim.shape[0], three_dim.shape[1], head_count, HEAD)

    def as_seqs(flat_rows):
        return flat_rows.reshape(seq_count, local_len, model_width)

    def attend_fwd(queries, keys, values):
        query_heads = split_heads(as_seqs(queries))
        running_max = jnp.full((seq_count, head_count, local_len), masked_value, jnp.float32)
        key_piece = lax.all_gather(as_seqs(keys), "ctx", axis=1, tiled=True)
        value_piece = lax.all_gather(as_seqs(values), "ctx", axis=1, tiled=True)
        piece_len = key_piece.shape[1]
        key_heads = split_heads(key_piece)
        value_heads = split_heads(value_piece)
        key_places = jnp.arange(piece_len, dtype=jnp.int32)
        allowed = visible(all_ids, key_places, doc_ids, query_pos)
        scores = (
            jnp.einsum(
                "sqhd,skhd->shqk", query_heads, key_heads, preferred_element_type=jnp.float32
            )
            * score_scale
        )
        scores = jnp.where(allowed, scores, masked_value)
        new_max = jnp.maximum(running_max, jnp.max(scores, axis=-1))
        weights = jnp.where(allowed, jnp.exp(scores - new_max[..., None]), 0.0)
        weight_sum = jnp.sum(weights, axis=-1)
        accumulated = jnp.einsum(
            "shqk,skhd->shqd",
            weights.astype(jnp.bfloat16),
            value_heads,
            preferred_element_type=jnp.float32,
        )
        running_max, weight_sum, accumulated = (new_max, weight_sum, accumulated)
        mixed_heads = accumulated / weight_sum[..., None]
        mixed_rows = (
            jnp.transpose(mixed_heads, (0, 2, 1, 3))
            .reshape(row_count, model_width)
            .astype(jnp.bfloat16)
        )
        return (mixed_rows, running_max + jnp.log(weight_sum))

    def attend_back(queries, keys, values, mixed_rows, grad_mixed, log_total):
        query_rows = as_seqs(queries)
        grad_rows = as_seqs(grad_mixed)
        query_heads = split_heads(query_rows)
        grad_heads = split_heads(grad_rows)
        row_delta = jnp.transpose(
            jnp.sum(
                grad_heads.astype(jnp.float32)
                * split_heads(as_seqs(mixed_rows)).astype(jnp.float32),
                axis=-1,
            ),
            (0, 2, 1),
        )
        key_all, value_all = (
            lax.all_gather(as_seqs(keys), "ctx", axis=1, tiled=True),
            lax.all_gather(as_seqs(values), "ctx", axis=1, tiled=True),
        )
        block_count = seq_length // key_block

        def block_terms(offset):
            key_heads = split_heads(lax.dynamic_slice_in_dim(key_all, offset, key_block, 1))
            value_heads = split_heads(lax.dynamic_slice_in_dim(value_all, offset, key_block, 1))
            key_ids = lax.dynamic_slice_in_dim(all_ids, offset, key_block, 1)
            key_places = offset + jnp.arange(key_block, dtype=jnp.int32)
            allowed = visible(key_ids, key_places, doc_ids, query_pos)
            scores = (
                jnp.einsum(
                    "sqhd,skhd->shqk", query_heads, key_heads, preferred_element_type=jnp.float32
                )
                * score_scale
            )
            scores = jnp.where(allowed, scores, masked_value)
            probabilities = jnp.where(allowed, jnp.exp(scores - log_total[..., None]), 0.0)
            grad_probs = jnp.einsum(
                "sqhd,skhd->shqk", grad_heads, value_heads, preferred_element_type=jnp.float32
            )
            grad_narrow = (probabilities * (grad_probs - row_delta[..., None])).astype(jnp.bfloat16)
            grad_queries = (
                jnp.einsum(
                    "shqk,skhd->sqhd", grad_narrow, key_heads, preferred_element_type=jnp.float32
                )
                * score_scale
            )
            return (probabilities, grad_narrow, grad_queries)

        zero_query = jnp.zeros((seq_count, local_len, head_count, HEAD), jnp.float32)

        def full_step(block_index, running):
            grad_q, grad_k, grad_v = running
            offset = block_index * key_block
            probabilities, grad_narrow, grad_queries = block_terms(offset)
            part_keys = (
                jnp.einsum(
                    "shqk,sqhd->skhd", grad_narrow, query_heads, preferred_element_type=jnp.float32
                )
                * score_scale
            ).reshape(seq_count, key_block, model_width)
            part_values = jnp.einsum(
                "shqk,sqhd->skhd",
                probabilities.astype(jnp.bfloat16),
                grad_heads,
                preferred_element_type=jnp.float32,
            ).reshape(seq_count, key_block, model_width)
            grad_k = lax.dynamic_update_slice_in_dim(grad_k, part_keys, offset, 1)
            grad_v = lax.dynamic_update_slice_in_dim(grad_v, part_values, offset, 1)
            return (grad_q + grad_queries, grad_k, grad_v)

        zero_keys = jnp.zeros((seq_count, seq_length, model_width), jnp.float32)
        grad_q, grad_k, grad_v = lax.fori_loop(
            0, block_count, full_step, (zero_query, zero_keys, zero_keys)
        )
        grad_k, grad_v = (
            lax.psum_scatter(
                grad_k.astype(jnp.bfloat16), "ctx", scatter_dimension=1, tiled=True
            ).astype(jnp.float32),
            lax.psum_scatter(
                grad_v.astype(jnp.bfloat16), "ctx", scatter_dimension=1, tiled=True
            ).astype(jnp.float32),
        )
        return (
            grad_q.reshape(row_count, model_width),
            grad_k.reshape(row_count, model_width),
            grad_v.reshape(row_count, model_width),
        )

    residual = block_input.reshape(row_count, model_width).astype(jnp.float32)
    kept_params = []
    saved_list = []
    for layer_idx in range(LAYERS):
        layer_params = (
            lax.all_gather(ln1_gain[layer_idx], ("dp", "ctx"), axis=0, tiled=True),
            lax.all_gather(ln1_bias[layer_idx], ("dp", "ctx"), axis=0, tiled=True),
            lax.all_gather(w_qkv[layer_idx], ("dp", "ctx"), axis=0, tiled=True),
            lax.all_gather(b_query[layer_idx], ("dp", "ctx"), axis=0, tiled=True),
            lax.all_gather(b_value[layer_idx], ("dp", "ctx"), axis=0, tiled=True),
            lax.all_gather(w_out[layer_idx], ("dp", "ctx"), axis=0, tiled=True),
            lax.all_gather(b_out[layer_idx], ("dp", "ctx"), axis=0, tiled=True),
            lax.all_gather(ln2_gain[layer_idx], ("dp", "ctx"), axis=0, tiled=True),
            lax.all_gather(ln2_bias[layer_idx], ("dp", "ctx"), axis=0, tiled=True),
            lax.all_gather(w_fc[layer_idx], ("dp", "ctx"), axis=0, tiled=True),
            lax.all_gather(b_fc[layer_idx], ("dp", "ctx"), axis=0, tiled=True),
            lax.all_gather(w_proj[layer_idx], ("dp", "ctx"), axis=0, tiled=True),
            lax.all_gather(b_proj[layer_idx], ("dp", "ctx"), axis=0, tiled=True),
        )
        residual, saved_rows = forward_layer(residual, layer_params, attend_fwd)
        kept_params.append(layer_params)
        saved_list.append(saved_rows)
    output_rows = residual.astype(jnp.bfloat16).reshape(seq_count, local_len, model_width)
    grad_residual = out_grad.reshape(row_count, model_width).astype(jnp.float32)
    reduced = [None] * LAYERS
    for layer_idx in reversed(range(LAYERS)):
        layer_params = (
            lax.all_gather(ln1_gain[layer_idx], ("dp", "ctx"), axis=0, tiled=True),
            lax.all_gather(ln1_bias[layer_idx], ("dp", "ctx"), axis=0, tiled=True),
            lax.all_gather(w_qkv[layer_idx], ("dp", "ctx"), axis=0, tiled=True),
            lax.all_gather(b_query[layer_idx], ("dp", "ctx"), axis=0, tiled=True),
            lax.all_gather(b_value[layer_idx], ("dp", "ctx"), axis=0, tiled=True),
            lax.all_gather(w_out[layer_idx], ("dp", "ctx"), axis=0, tiled=True),
            lax.all_gather(b_out[layer_idx], ("dp", "ctx"), axis=0, tiled=True),
            lax.all_gather(ln2_gain[layer_idx], ("dp", "ctx"), axis=0, tiled=True),
            lax.all_gather(ln2_bias[layer_idx], ("dp", "ctx"), axis=0, tiled=True),
            lax.all_gather(w_fc[layer_idx], ("dp", "ctx"), axis=0, tiled=True),
            lax.all_gather(b_fc[layer_idx], ("dp", "ctx"), axis=0, tiled=True),
            lax.all_gather(w_proj[layer_idx], ("dp", "ctx"), axis=0, tiled=True),
            lax.all_gather(b_proj[layer_idx], ("dp", "ctx"), axis=0, tiled=True),
        )
        grad_residual, layer_grads = backward_layer(
            grad_residual, saved_list[layer_idx], layer_params, attend_back
        )
        reduced[layer_idx] = (
            lax.psum_scatter(layer_grads[0], ("dp", "ctx"), scatter_dimension=0, tiled=True),
            lax.psum_scatter(layer_grads[1], ("dp", "ctx"), scatter_dimension=0, tiled=True),
            lax.psum_scatter(layer_grads[2], ("dp", "ctx"), scatter_dimension=0, tiled=True),
            lax.psum_scatter(layer_grads[3], ("dp", "ctx"), scatter_dimension=0, tiled=True),
            lax.psum_scatter(layer_grads[4], ("dp", "ctx"), scatter_dimension=0, tiled=True),
            lax.psum_scatter(layer_grads[5], ("dp", "ctx"), scatter_dimension=0, tiled=True),
            lax.psum_scatter(layer_grads[6], ("dp", "ctx"), scatter_dimension=0, tiled=True),
            lax.psum_scatter(layer_grads[7], ("dp", "ctx"), scatter_dimension=0, tiled=True),
            lax.psum_scatter(layer_grads[8], ("dp", "ctx"), scatter_dimension=0, tiled=True),
            lax.psum_scatter(layer_grads[9], ("dp", "ctx"), scatter_dimension=0, tiled=True),
            lax.psum_scatter(layer_grads[10], ("dp", "ctx"), scatter_dimension=0, tiled=True),
            lax.psum_scatter(layer_grads[11], ("dp", "ctx"), scatter_dimension=0, tiled=True),
            lax.psum_scatter(layer_grads[12], ("dp", "ctx"), scatter_dimension=0, tiled=True),
        )
    grad_rows = grad_residual.astype(jnp.bfloat16).reshape(seq_count, local_len, model_width)
    stacked = tuple(
        (
            jnp.stack([reduced[layer_idx][member] for layer_idx in range(LAYERS)])
            for member in range(13)
        )
    )
    return (output_rows, grad_rows) + stacked


def solution(mesh):
    return jax.shard_map(
        shards,
        mesh=mesh,
        in_specs=(
            P("dp", "ctx", None),
            P("dp", "ctx"),
            P("dp", "ctx", None),
            P(None, ("dp", "ctx")),
            P(None, ("dp", "ctx")),
            P(None, ("dp", "ctx"), None),
            P(None, ("dp", "ctx")),
            P(None, ("dp", "ctx")),
            P(None, ("dp", "ctx"), None),
            P(None, ("dp", "ctx")),
            P(None, ("dp", "ctx")),
            P(None, ("dp", "ctx")),
            P(None, ("dp", "ctx"), None),
            P(None, ("dp", "ctx")),
            P(None, ("dp", "ctx"), None),
            P(None, ("dp", "ctx")),
        ),
        out_specs=(
            P("dp", "ctx", None),
            P("dp", "ctx", None),
            P(None, ("dp", "ctx")),
            P(None, ("dp", "ctx")),
            P(None, ("dp", "ctx"), None),
            P(None, ("dp", "ctx")),
            P(None, ("dp", "ctx")),
            P(None, ("dp", "ctx"), None),
            P(None, ("dp", "ctx")),
            P(None, ("dp", "ctx")),
            P(None, ("dp", "ctx")),
            P(None, ("dp", "ctx"), None),
            P(None, ("dp", "ctx")),
            P(None, ("dp", "ctx"), None),
            P(None, ("dp", "ctx")),
        ),
        check_vma=False,
    )
```

profile of v0, /device:TPU:0, one launch (start us, length us, event | category | flops | bytes accessed | tf_op | source)
XLA Modules:
  0.0 2258.5 jit_solution(16489377935709036343)
XLA Ops:
  31.1 43.9 %all-reduce.37 = (bf16[768]{0:T(1024)(128)(2,1)S(1)}, bf16[768]{0:T(1024)(128)(2,1)S(1)}, bf16[768]{0:T(1024)(128)(2,1)S(1)}, bf16[768]{0:T(1024)(128)(2,1)S(1)}...) all-reduce(bf16[768]{0:T(1024)(128)(2,1)S(1)} %dynamic-update-slice, ...), channel_id=3, replica_groups=mesh['dp'=4,'ctx'=8] {'dp','ctx'}, use_global_device_ids=true, to_apply=%add.1 | all-reduce | flops 18432 | bytes 73728
  85.8 11.0 all_gather.111
  97.8 22.0 all-gather.45.cloned.1.call-done
  119.8 4.8 copy.78
  124.6 12.6 fusion.40
  137.2 21.9 all-gather.47.cloned.1.call-done
  159.2 4.8 copy.79
  164.0 12.1 fusion.42
  176.1 11.9 fusion.127
  188.0 27.1 %all-gather.49.cloned.1.call-done = bf16[1,768,768]{2,1,0:T(8,128)(2,1)} async-done(((bf16[1,24,768]{2,1,0:T(8,128)(2,1)}), bf16[1,768,768]{2,1,0:T(8,128)(2,1)}) %all-gather.49.cloned.1.call-update) | async-done | bytes 1179664 | tf_op jit(solution)/shard_map/all_gather | solution.py:366
  217.2 63.3 %all-gather.51.cloned.1.call-done = bf16[1,768,3072]{2,1,0:T(8,128)(2,1)} async-done(((bf16[1,24,3072]{2,1,0:T(8,128)(2,1)}), bf16[1,768,3072]{2,1,0:T(8,128)(2,1)}) %all-gather.51.cloned.1.call-update) | async-done | bytes 4718608 | tf_op jit(solution)/shard_map/all_gather | solution.py:370
  280.5 5.4 fusion.74
  286.0 60.0 %all-gather.53.cloned.1.call-done = bf16[1,3072,768]{2,1,0:T(8,128)(2,1)} async-done(((bf16[1,96,768]{2,1,0:T(8,128)(2,1)}), bf16[1,3072,768]{2,1,0:T(8,128)(2,1)}) %all-gather.53.cloned.1.call-update) | async-done | bytes 4718608 | tf_op jit(solution)/shard_map/all_gather | solution.py:372
  345.9 5.3 fusion.198
  351.5 55.8 %all-gather.55.cloned.1.call-done = bf16[1,768,2304]{2,1,0:T(8,128)(2,1)} async-done(((bf16[1,24,2304]{2,1,0:T(8,128)(2,1)}), bf16[1,768,2304]{2,1,0:T(8,128)(2,1)}) %all-gather.55.cloned.1.call-update) | async-done | bytes 3538960 | tf_op jit(solution)/shard_map/all_gather | solution.py:363
  417.3 32.6 %all-gather.57.cloned.1.call-done = bf16[2048,768]{1,0:T(8,128)(2,1)} async-done(((bf16[256,768]{1,0:T(8,128)(2,1)}), bf16[2048,768]{1,0:T(8,128)(2,1)}) %all-gather.57.cloned.1.call-update) | async-done | bytes 3145744 | tf_op jit(solution)/shard_map/all_gather | solution.py:239
  449.9 5.0 copy.81
  454.9 34.4 %all-gather.59.cloned.1.call-done = bf16[2048,768]{1,0:T(8,128)(2,1)} async-done(((bf16[256,768]{1,0:T(8,128)(2,1)}), bf16[2048,768]{1,0:T(8,128)(2,1)}) %all-gather.59.cloned.1.call-update) | async-done | bytes 3145744 | tf_op jit(solution)/shard_map/all_gather | solution.py:240
  489.3 4.8 copy.82
  494.0 12.5 fusion.41
  506.6 12.1 fusion.44
  518.7 11.6 fusion.133
  530.3 14.9 all-gather.61.cloned.1.call-done
  547.9 62.8 %all-gather.63.cloned.1.call-done = bf16[1,768,3072]{2,1,0:T(8,128)(2,1)} async-done(((bf16[1,24,3072]{2,1,0:T(8,128)(2,1)}), bf16[1,768,3072]{2,1,0:T(8,128)(2,1)}) %all-gather.63.cloned.1.call-update) | async-done | bytes 4718608 | tf_op jit(solution)/shard_map/all_gather | solution.py:370
  610.7 5.5 fusion.77
  616.2 59.9 %all-gather.65.cloned.1.call-done = bf16[1,3072,768]{2,1,0:T(8,128)(2,1)} async-done(((bf16[1,96,768]{2,1,0:T(8,128)(2,1)}), bf16[1,3072,768]{2,1,0:T(8,128)(2,1)}) %all-gather.65.cloned.1.call-update) | async-done | bytes 4718608 | tf_op jit(solution)/shard_map/all_gather | solution.py:372
  676.1 7.7 fusion.200
  695.3 94.5 %while.36 = (s32[]{:T(128)}, f32[1,256,12,64]{1,3,2,0:T(8,128)}, bf16[1,2048,768]{1,2,0:T(8,128)(2,1)}, bf16[1,2048,768]{1,2,0:T(8,128)(2,1)}, bf16[1,2048,768]{...) while((s32[]{:T(128)}, f32[1,256,12,64]{1,3,2,0:T(8,128)}, ...), condition=%wide.region_16.17_spmd.clone, body=%wide.region_15.16_spmd.clone.sunk | while | flops 1027277568 | bytes 48940324 | solution.py:339
  703.7 5.4 fusion.265
  710.2 4.5 fusion.267
  727.2 5.4 fusion.265
  733.6 4.5 fusion.267
  750.9 5.4 fusion.265
  757.4 4.5 fusion.267
  774.6 5.4 fusion.265
  781.1 4.5 fusion.267
  792.1 36.6 %reduce-scatter.13.cloned.1.call-done = bf16[1,256,768]{1,2,0:T(8,128)(2,1)} async-done(((bf16[1,2048,768]{1,2,0:T(8,128)(2,1)}), bf16[1,256,768]{1,2,0:T(8,128)(2,1)}) %reduce-scatter.13.cloned.1.call-update) | async-done | bytes 393232 | tf_op jit(solution)/shard_map/reduce_scatter | solution.py:343
  828.7 41.8 %reduce-scatter.15.cloned.1.call-done = bf16[1,256,768]{1,2,0:T(8,128)(2,1)} async-done(((bf16[1,2048,768]{1,2,0:T(8,128)(2,1)}), bf16[1,256,768]{1,2,0:T(8,128)(2,1)}) %reduce-scatter.15.cloned.1.call-update) | async-done | bytes 393232 | tf_op jit(solution)/shard_map/reduce_scatter | solution.py:346
  876.8 5.7 fusion.201
  893.8 95.0 %while.37 = (s32[]{:T(128)}, f32[1,256,12,64]{1,3,2,0:T(8,128)}, bf16[1,2048,768]{1,2,0:T(8,128)(2,1)}, bf16[1,2048,768]{1,2,0:T(8,128)(2,1)}, bf16[1,2048,768]{...) while((s32[]{:T(128)}, f32[1,256,12,64]{1,3,2,0:T(8,128)}, ...), condition=%wide.region_25.26_spmd.clone, body=%wide.region_24.25_spmd.clone.sunk | while | flops 1027277568 | bytes 48940324 | solution.py:339
  902.5 5.4 fusion.279
  909.0 4.5 fusion.281
  926.0 5.4 fusion.279
  949.8 5.4 fusion.279
  973.5 5.4 fusion.279
  980.0 4.5 fusion.281
  996.4 32.1 %reduce-scatter.19.cloned.1.call-done = bf16[1,256,768]{1,2,0:T(8,128)(2,1)} async-done(((bf16[1,2048,768]{1,2,0:T(8,128)(2,1)}), bf16[1,256,768]{1,2,0:T(8,128)(2,1)}) %reduce-scatter.19.cloned.1.call-update) | async-done | bytes 393232 | tf_op jit(solution)/shard_map/reduce_scatter | solution.py:346
  1030.3 40.0 %reduce-scatter.17.cloned.1.call-done = bf16[1,256,768]{1,2,0:T(8,128)(2,1)} async-done(((bf16[1,2048,768]{1,2,0:T(8,128)(2,1)}), bf16[1,256,768]{1,2,0:T(8,128)(2,1)}) %reduce-scatter.17.cloned.1.call-update) | async-done | bytes 393232 | tf_op jit(solution)/shard_map/reduce_scatter | solution.py:343
  1070.3 5.0 fusion.149
  1075.4 7.8 fusion.164
  1084.3 7.8 fusion.170
  1093.3 6.7 fusion.158
  1101.1 6.7 fusion.155
  1109.1 5.1 fusion.162
  1120.3 6.4 fusion.116
  1126.7 47.7 %reduce-scatter.27.cloned.1.call-done = f32[24,768]{1,0:T(8,128)} async-done(((f32[768,768]{1,0:T(8,128)}), f32[24,768]{1,0:T(8,128)}) %reduce-scatter.27.cloned.1.call-update) | async-done | bytes 73744 | tf_op jit(solution)/shard_map/reduce_scatter | solution.py:406
  1174.5 103.8 %reduce-scatter.25.cloned.1.call-done = f32[24,768]{1,0:T(8,128)} async-done(((f32[768,768]{1,0:T(8,128)}), f32[24,768]{1,0:T(8,128)}) %reduce-scatter.25.cloned.1.call-update) | async-done | bytes 73744 | tf_op jit(solution)/shard_map/reduce_scatter | solution.py:406
  1280.9 153.4 %all-reduce.40.cloned.1.call-done = (f32[768]{0:T(1024)}, f32[768]{0:T(1024)}, f32[768]{0:T(1024)}, f32[768]{0:T(1024)}, f32[768]{0:T(1024)}, /*index=5*/f32[768...) async-done(((f32[768]{0:T(1024)}, f32[768]{0:T(1024)}, ...) | async-done | bytes 73744
  1453.1 125.2 %reduce-scatter.35.cloned.1.call-done = f32[96,768]{1,0:T(8,128)} async-done(((f32[3072,768]{1,0:T(8,128)}), f32[96,768]{1,0:T(8,128)}) %reduce-scatter.35.cloned.1.call-update) | async-done | bytes 294928 | tf_op jit(solution)/shard_map/reduce_scatter | solution.py:412
  1578.2 141.1 %reduce-scatter.33.cloned.1.call-done = f32[96,768]{1,0:T(8,128)} async-done(((f32[3072,768]{1,0:T(8,128)}), f32[96,768]{1,0:T(8,128)}) %reduce-scatter.33.cloned.1.call-update) | async-done | bytes 294928 | tf_op jit(solution)/shard_map/reduce_scatter | solution.py:412
  1721.2 139.1 %reduce-scatter.31.cloned.1.call-done = f32[24,3072]{1,0:T(8,128)} async-done(((f32[768,3072]{1,0:T(8,128)}), f32[24,3072]{1,0:T(8,128)}) %reduce-scatter.31.cloned.1.call-update) | async-done | bytes 294928 | tf_op jit(solution)/shard_map/reduce_scatter | solution.py:410
  1860.4 141.1 %reduce-scatter.29.cloned.1.call-done = f32[24,3072]{1,0:T(8,128)} async-done(((f32[768,3072]{1,0:T(8,128)}), f32[24,3072]{1,0:T(8,128)}) %reduce-scatter.29.cloned.1.call-update) | async-done | bytes 294928 | tf_op jit(solution)/shard_map/reduce_scatter | solution.py:410
  2003.4 122.2 %reduce-scatter.23.cloned.1.call-done = f32[24,2304]{1,0:T(8,128)} async-done(((f32[768,2304]{1,0:T(8,128)}), f32[24,2304]{1,0:T(8,128)}) %reduce-scatter.23.cloned.1.call-update) | async-done | bytes 221200 | tf_op jit(solution)/shard_map/reduce_scatter | solution.py:403
  2125.5 124.2 %reduce-scatter.21.cloned.1.call-done = f32[24,2304]{1,0:T(8,128)} async-done(((f32[768,2304]{1,0:T(8,128)}), f32[24,2304]{1,0:T(8,128)}) %reduce-scatter.21.cloned.1.call-update) | async-done | bytes 221200 | tf_op jit(solution)/shard_map/reduce_scatter | solution.py:403
  (534 shorter events, 246.9 us)
Async XLA Ops:
  7.2 70.3 %all-gather.43.cloned.1.call-start = ((), (), s32[]{:S(2)}) async-start(), calls=%async_computation.24 | async-start | bytes 3649536 | tf_op jit(solution)/shard_map/all_gather | solution.py:363
  8.9 110.9 %all-gather.45.cloned.1.call-start = ((), (), s32[]{:S(2)}) async-start(), calls=%async_computation.25 | async-start | bytes 3538944 | tf_op jit(solution)/shard_map/all_gather | solution.py:239
  75.0 5.8 copy-start.62
  81.7 77.5 %all-gather.47.cloned.1.call-start = ((), (), s32[]{:S(2)}) async-start(), calls=%async_computation.26 | async-start | bytes 3538944 | tf_op jit(solution)/shard_map/all_gather | solution.py:240
  82.6 132.5 %all-gather.49.cloned.1.call-start = ((), (), s32[]{:S(2)}) async-start(), calls=%async_computation.27 | async-start | bytes 1216512 | tf_op jit(solution)/shard_map/all_gather | solution.py:366
  83.3 197.2 %all-gather.51.cloned.1.call-start = ((), (), s32[]{:S(2)}) async-start(), calls=%async_computation.28 | async-start | bytes 4866048 | tf_op jit(solution)/shard_map/all_gather | solution.py:370
  84.1 261.8 %all-gather.53.cloned.1.call-start = ((), (), s32[]{:S(2)}) async-start(), calls=%async_computation.29 | async-start | bytes 4866048 | tf_op jit(solution)/shard_map/all_gather | solution.py:372
  85.0 322.3 %all-gather.55.cloned.1.call-start = ((), (), s32[]{:S(2)}) async-start(), calls=%async_computation.30 | async-start | bytes 3649536 | tf_op jit(solution)/shard_map/all_gather | solution.py:363
  85.7 364.2 %all-gather.57.cloned.1.call-start = ((), (), s32[]{:S(2)}) async-start(), calls=%async_computation.31 | async-start | bytes 3538944 | tf_op jit(solution)/shard_map/all_gather | solution.py:239
  96.8 183.7 %copy-start.55 = (f32[768]{0:T(1024)}, f32[768]{0:T(1024)S(1)}, u32[]{:S(2)}) copy-start(f32[768]{0:T(1024)S(1)} %convert_element_type.340) | copy-start | bytes 9220
  96.8 183.7 %copy-start.64 = (f32[768]{0:T(1024)}, f32[768]{0:T(1024)S(1)}, u32[]{:S(2)}) copy-start(f32[768]{0:T(1024)S(1)} %convert_element_type.341) | copy-start | bytes 9220
  96.9 310.4 %copy-start.53 = (f32[768]{0:T(1024)}, f32[768]{0:T(1024)S(1)}, u32[]{:S(2)}) copy-start(f32[768]{0:T(1024)S(1)} %convert_element_type.345) | copy-start | bytes 9220
  97.8 26.8 %copy-start.2 = (bf16[256,768]{0,1:T(8,128)(2,1)}, bf16[256,768]{0,1:T(8,128)(2,1)S(1)}, u32[]{:S(2)}) copy-start(bf16[256,768]{0,1:T(8,128)(2,1)S(1)} %copy.77) | copy-start | bytes 1179652
  137.2 26.7 %copy-start.60 = (f32[12,256]{1,0:T(8,128)}, f32[12,256]{1,0:T(8,128)S(1)}, u32[]{:S(2)}) copy-start(f32[12,256]{1,0:T(8,128)S(1)} %get-tuple-element.770) | copy-start | bytes 36868
  164.0 12.1 copy-start.35
  176.1 11.9 copy-start.69
  176.1 39.0 %copy-start.19 = (bf16[1,256,768]{2,1,0:T(8,128)(2,1)S(1)}, bf16[1,256,768]{2,1,0:T(8,128)(2,1)}, u32[]{:S(2)}) copy-start(bf16[1,256,768]{2,1,0:T(8,128)(2,1)} %param.20) | copy-start | bytes 1179652
  188.0 98.0 %copy-start.27 = (bf16[12,256,64]{1,2,0:T(8,128)(2,1)}, bf16[12,256,64]{1,2,0:T(8,128)(2,1)S(1)}, u32[]{:S(2)}) copy-start(bf16[12,256,64]{1,2,0:T(8,128)(2,1)S(1)} %fusion.127) | copy-start | bytes 1179652
  217.0 128.9 %copy-start.14 = (f32[256,768]{1,0:T(8,128)}, f32[256,768]{1,0:T(8,128)S(1)}, u32[]{:S(2)}) copy-start(f32[256,768]{1,0:T(8,128)S(1)} %get-tuple-element.773) | copy-start | bytes 2359300
  217.0 69.0 %copy-start.78 = (f32[256]{0:T(256)}, f32[256]{0:T(256)S(1)}, u32[]{:S(2)}) copy-start(f32[256]{0:T(256)S(1)} %broadcast_multiply_fusion.10) | copy-start | bytes 3076
  217.2 68.7 %copy-start.88 = (f32[256]{0:T(256)}, f32[256]{0:T(256)S(1)}, u32[]{:S(2)}) copy-start(f32[256]{0:T(256)S(1)} %add_rsqrt_fusion.2) | copy-start | bytes 3076
  351.2 193.9 %copy-start.6 = (f32[256,768]{1,0:T(8,128)}, f32[256,768]{1,0:T(8,128)S(1)}, u32[]{:S(2)}) copy-start(f32[256,768]{1,0:T(8,128)S(1)} %get-tuple-element.775) | copy-start | bytes 2359300
  351.3 59.2 %copy-start.71 = (f32[256]{0:T(256)}, f32[256]{0:T(256)S(1)}, u32[]{:S(2)}) copy-start(f32[256]{0:T(256)S(1)} %broadcast_multiply_fusion.9) | copy-start | bytes 3076
  351.5 59.0 %copy-start.81 = (f32[256]{0:T(256)}, f32[256]{0:T(256)S(1)}, u32[]{:S(2)}) copy-start(f32[256]{0:T(256)S(1)} %add_rsqrt_fusion.1) | copy-start | bytes 3076
  412.7 76.5 %all-gather.59.cloned.1.call-start = ((), (), s32[]{:S(2)}) async-start(), calls=%async_computation.32 | async-start | bytes 3538944 | tf_op jit(solution)/shard_map/all_gather | solution.py:240
  415.1 130.1 %all-gather.61.cloned.1.call-start = ((), (), s32[]{:S(2)}) async-start(), calls=%async_computation.33 | async-start | bytes 1216512 | tf_op jit(solution)/shard_map/all_gather | solution.py:366
  415.7 195.1 %all-gather.63.cloned.1.call-start = ((), (), s32[]{:S(2)}) async-start(), calls=%async_computation.34 | async-start | bytes 4866048 | tf_op jit(solution)/shard_map/all_gather | solution.py:370
  416.4 259.7 %all-gather.65.cloned.1.call-start = ((), (), s32[]{:S(2)}) async-start(), calls=%async_computation.35 | async-start | bytes 4866048 | tf_op jit(solution)/shard_map/all_gather | solution.py:372
  417.0 411.7 %reduce-scatter.13.cloned.1.call-start = ((), (), s32[]{:S(2)}) async-start(), calls=%async_computation.12 | async-start | bytes 3538944 | tf_op jit(solution)/shard_map/reduce_scatter | solution.py:343
  417.1 269.0 %copy-start.58 = (f32[768]{0:T(1024)}, f32[768]{0:T(1024)S(1)}, u32[]{:S(2)}) copy-start(f32[768]{0:T(1024)S(1)} %convert_element_type.349) | copy-start | bytes 9220
  417.1 193.7 %copy-start.66 = (f32[768]{0:T(1024)}, f32[768]{0:T(1024)S(1)}, u32[]{:S(2)}) copy-start(f32[768]{0:T(1024)S(1)} %convert_element_type.350) | copy-start | bytes 9220
  506.5 12.1 copy-start.34
  530.3 159.1 %copy-start.30 = (bf16[12,256,64]{1,2,0:T(8,128)(2,1)}, bf16[12,256,64]{1,2,0:T(8,128)(2,1)S(1)}, u32[]{:S(2)}) copy-start(bf16[12,256,64]{1,2,0:T(8,128)(2,1)S(1)} %fusion.133) | copy-start | bytes 1179652
  547.0 139.0 %copy-start.17 = (f32[256,768]{1,0:T(8,128)}, f32[256,768]{1,0:T(8,128)S(1)}, u32[]{:S(2)}) copy-start(f32[256,768]{1,0:T(8,128)S(1)} %get-tuple-element.779) | copy-start | bytes 2359300
  547.0 139.0 %copy-start.83 = (f32[256]{0:T(256)}, f32[256]{0:T(256)S(1)}, u32[]{:S(2)}) copy-start(f32[256]{0:T(256)S(1)} %broadcast_multiply_fusion.8) | copy-start | bytes 3076
  547.3 138.8 %copy-start.91 = (f32[256]{0:T(256)}, f32[256]{0:T(256)S(1)}, u32[]{:S(2)}) copy-start(f32[256]{0:T(256)S(1)} %add_rsqrt_fusion) | copy-start | bytes 3076
  547.9 128.2 %copy-start.44 = (bf16[1,256,768]{2,1,0:T(8,128)(2,1)S(1)}, bf16[1,256,768]{2,1,0:T(8,128)(2,1)}, u32[]{:S(2)}) copy-start(bf16[1,256,768]{2,1,0:T(8,128)(2,1)} %param.22) | copy-start | bytes 1179652
  676.1 7.7 copy-start.96
  789.8 80.6 %copy-start.7 = (f32[256,768]{1,0:T(8,128)S(1)}, f32[256,768]{1,0:T(8,128)}, u32[]{:S(2)}) copy-start(f32[256,768]{1,0:T(8,128)} %copy-done.6) | copy-start | bytes 2359300
  789.9 80.6 %copy-start.72 = (f32[256]{0:T(256)S(1)}, f32[256]{0:T(256)}, u32[]{:S(2)}) copy-start(f32[256]{0:T(256)} %copy-done.71) | copy-start | bytes 3076
  789.9 80.6 %copy-start.82 = (f32[256]{0:T(256)S(1)}, f32[256]{0:T(256)}, u32[]{:S(2)}) copy-start(f32[256]{0:T(256)} %copy-done.81) | copy-start | bytes 3076
  789.9 80.6 %reduce-scatter.15.cloned.1.call-start = ((), (), s32[]{:S(2)}) async-start(), calls=%async_computation.13 | async-start | bytes 3538944 | tf_op jit(solution)/shard_map/reduce_scatter | solution.py:346
  790.5 238.1 %reduce-scatter.19.cloned.1.call-start = ((), (), s32[]{:S(2)}) async-start(), calls=%async_computation.15 | async-start | bytes 3538944 | tf_op jit(solution)/shard_map/reduce_scatter | solution.py:346
  792.1 82.7 %copy-start.37 = (bf16[1,256,12,64]{1,3,2,0:T(8,128)(2,1)}, bf16[1,256,12,64]{1,3,2,0:T(8,128)(2,1)S(1)}, u32[]{:S(2)}) copy-start(bf16[1,256,12,64]{1,3,2,0:T(8,128)(2,1)S(1)} %get-tuple-element.742) | copy-start | bytes 1179652
  870.5 12.0 slice-start
  875.8 8.9 copy-start.22
  988.9 81.4 %reduce-scatter.17.cloned.1.call-start = ((), (), s32[]{:S(2)}) async-start(), calls=%async_computation.14 | async-start | bytes 3538944 | tf_op jit(solution)/shard_map/reduce_scatter | solution.py:343
  989.5 185.0 %reduce-scatter.27.cloned.1.call-start = ((), (), s32[]{:S(2)}) async-start(), calls=%async_computation.19 | async-start | bytes 2433024 | tf_op jit(solution)/shard_map/reduce_scatter | solution.py:406
  992.0 78.3 %copy-start.20 = (bf16[1,256,768]{2,1,0:T(8,128)(2,1)S(1)}, bf16[1,256,768]{2,1,0:T(8,128)(2,1)}, u32[]{:S(2)}) copy-start(bf16[1,256,768]{2,1,0:T(8,128)(2,1)} %param.20) | copy-start | bytes 1179652
  992.0 78.3 %copy-start.52 = (f32[768]{0:T(1024)S(1)}, f32[768]{0:T(1024)}, u32[]{:S(2)}) copy-start(f32[768]{0:T(1024)} %copy-done.51) | copy-start | bytes 9220
  992.0 78.3 %copy-start.76 = (f32[256]{0:T(256)S(1)}, f32[256]{0:T(256)}, u32[]{:S(2)}) copy-start(f32[256]{0:T(256)} %copy-done.75) | copy-start | bytes 3076
  992.0 78.3 %copy-start.86 = (f32[256]{0:T(256)S(1)}, f32[256]{0:T(256)}, u32[]{:S(2)}) copy-start(f32[256]{0:T(256)} %copy-done.85) | copy-start | bytes 3076
  992.0 286.2 %reduce-scatter.25.cloned.1.call-start = ((), (), s32[]{:S(2)}) async-start(), calls=%async_computation.18 | async-start | bytes 2433024 | tf_op jit(solution)/shard_map/reduce_scatter | solution.py:406
  994.0 440.4 %all-reduce.40.cloned.1.call-start = ((), (), s32[]{:S(2)}) async-start(), calls=%async_computation.36 | async-start | bytes 180224
  994.9 80.4 %copy-start.42 = (bf16[1,256,12,64]{1,3,2,0:T(8,128)(2,1)}, bf16[1,256,12,64]{1,3,2,0:T(8,128)(2,1)S(1)}, u32[]{:S(2)}) copy-start(bf16[1,256,12,64]{1,3,2,0:T(8,128)(2,1)S(1)} %get-tuple-element.740) | copy-start | bytes 1179652
  1075.4 502.9 %reduce-scatter.35.cloned.1.call-start = ((), (), s32[]{:S(2)}) async-start(), calls=%async_computation.23 | async-start | bytes 9732096 | tf_op jit(solution)/shard_map/reduce_scatter | solution.py:412
  1083.2 636.1 %reduce-scatter.33.cloned.1.call-start = ((), (), s32[]{:S(2)}) async-start(), calls=%async_computation.22 | async-start | bytes 9732096 | tf_op jit(solution)/shard_map/reduce_scatter | solution.py:412
  1092.2 768.2 %reduce-scatter.31.cloned.1.call-start = ((), (), s32[]{:S(2)}) async-start(), calls=%async_computation.21 | async-start | bytes 9732096 | tf_op jit(solution)/shard_map/reduce_scatter | solution.py:410
  1100.0 901.5 %reduce-scatter.29.cloned.1.call-start = ((), (), s32[]{:S(2)}) async-start(), calls=%async_computation.20 | async-start | bytes 9732096 | tf_op jit(solution)/shard_map/reduce_scatter | solution.py:410
  1107.9 1017.7 %reduce-scatter.23.cloned.1.call-start = ((), (), s32[]{:S(2)}) async-start(), calls=%async_computation.17 | async-start | bytes 7299072 | tf_op jit(solution)/shard_map/reduce_scatter | solution.py:403
  1114.3 1135.5 %reduce-scatter.21.cloned.1.call-start = ((), (), s32[]{:S(2)}) async-start(), calls=%async_computation.16 | async-start | bytes 7299072 | tf_op jit(solution)/shard_map/reduce_scatter | solution.py:403
  1120.3 159.5 %copy-start.95 = (f32[256]{0:T(256)S(1)}, f32[256]{0:T(256)}, u32[]{:S(2)}) copy-start(f32[256]{0:T(256)} %get-tuple-element.628) | copy-start | bytes 3076
  1120.3 159.5 %copy-start.94 = (f32[256]{0:T(256)S(1)}, f32[256]{0:T(256)}, u32[]{:S(2)}) copy-start(f32[256]{0:T(256)} %get-tuple-element.629) | copy-start | bytes 3076
  1120.3 159.5 %copy-start.46 = (f32[256,768]{1,0:T(8,128)S(1)}, f32[256,768]{1,0:T(8,128)}, u32[]{:S(2)}) copy-start(f32[256,768]{1,0:T(8,128)} %get-tuple-element.783) | copy-start | bytes 2359300
  (72 other events, 168.3 us)
Sparse Core Ops, SparseCore 0:
  11.6 63.0 all-gather.42
  81.8 38.0 all-gather.44
  122.1 37.0 all-gather.46
  162.1 53.0 all-gather.48
  218.0 62.4 all-gather.50
  284.0 61.9 all-gather.52
  348.9 58.3 all-gather.54
  412.9 36.9 all-gather.56
  452.1 37.1 all-gather.58
  492.1 53.0 all-gather.60
  548.2 62.4 all-gather.62
  614.2 61.9 all-gather.64
  790.0 38.6 reduce-scatter.12
  830.9 39.5 reduce-scatter.14
  989.0 39.5 reduce-scatter.18
  1030.7 39.5 reduce-scatter.16
  1075.4 98.9 reduce-scatter.26
  1179.6 98.6 reduce-scatter.24
  1285.8 148.5 all-reduce.39
  1440.1 138.0 reduce-scatter.34
  1584.2 135.1 reduce-scatter.32
  1725.2 135.0 reduce-scatter.30
  1866.3 135.1 reduce-scatter.28
  2007.0 118.4 reduce-scatter.22
  2131.2 118.4 reduce-scatter.20
where the time goes:
time: 2270 us; the launch traced here: 2260 us
  waiting for transfers between devices  1710 us (75%)
  matrix products  292 us (13%)
  local copies, waits for them, and re-layouts  125 us (6%)
  other arithmetic  62.5 us (3%)
  blocking collectives  55 us (2%)
    reduce_scatter x2, waiting for transfers between devices, shards(): lax.psum_scatter(layer_grads[9], ('dp', 'ctx'), scatter_dimension=0, tile...  280 us
    reduce_scatter x2, waiting for transfers between devices, shards(): lax.psum_scatter(layer_grads[11], ('dp', 'ctx'), scatter_dimension=0, til...  266 us
    reduce_scatter x2, waiting for transfers between devices, shards(): lax.psum_scatter(layer_grads[2], ('dp', 'ctx'), scatter_dimension=0, tile...  246 us
    unnamed x26, waiting for transfers between devices  157 us
    reduce_scatter x2, waiting for transfers between devices, shards(): lax.psum_scatter(layer_grads[5], ('dp', 'ctx'), scatter_dimension=0, tile...  152 us
    all_gather x2, waiting for transfers between devices, shards(): lax.all_gather(w_fc[layer_idx], ('dp', 'ctx'), axis=0, tiled=True)  126 us
    all_gather x2, waiting for transfers between devices, shards(): lax.all_gather(w_proj[layer_idx], ('dp', 'ctx'), axis=0, tiled=True)  120 us
    reduce_scatter x2, waiting for transfers between devices, attend_back(): lax.psum_scatter(grad_k.astype(jnp.bfloat16), 'ctx', scatter_dimension=1,...  76.5 us
  transfers between devices with their start and end apart: 25, of which 24 were waited for; matrix products, arithmetic and copies ran while one was open for 10% of the time, Pallas kernels for 0%

commit v1 on v0

--- a/solution.py
+++ b/solution.py
@@ -1,6 +1,10 @@
+import functools
+
 import jax
 import jax.numpy as jnp
 from jax import lax
+from jax.experimental import pallas as pl
+from jax.experimental.pallas import tpu as pltpu
 from jax.sharding import PartitionSpec as P
 
 HEAD = 64
@@ -12,6 +16,143 @@
 gelu_coeff = 0.7978845608028654
 cubic_coeff = 0.044715
 key_block = 512
+
+def swap(value, dp_bits, ctx_bits):
+    dp_size, ctx_size = lax.axis_size("dp"), lax.axis_size("ctx")
+    pairs = [
+        (i, ((i // ctx_size) ^ dp_bits) * ctx_size + ((i % ctx_size) ^ ctx_bits))
+        for i in range(dp_size * ctx_size)
+    ]
+    return lax.ppermute(value, ("dp", "ctx"), pairs)
+
+
+def place_kernel(dp_size, chips, *refs):
+    pieces, whole, held, in_sem, out_sem = refs[: 2 * dp_size], *refs[2 * dp_size :]
+    half = held.shape[-1]
+    dp_rank, ctx_rank = lax.axis_index("dp"), lax.axis_index("ctx")
+    chip, core = ctx_rank // 2, ctx_rank % 2
+    arrivals = []
+    for n, piece in enumerate(pieces):
+        for k in range(chips):
+            copy = pltpu.make_async_copy(piece.at[k], held.at[n, k], in_sem.at[n, k])
+            copy.start()
+            arrivals.append((n, k, copy))
+    leaving = []
+    for n, k, copy in arrivals:
+        copy.wait()
+        side, move = n // dp_size, n % dp_size
+        row = (dp_rank ^ move) * chips + (chip ^ k)
+        column = pl.multiple_of((core ^ side) * half, half)
+        out = pltpu.make_async_copy(
+            held.at[n, k], whole.at[row, :, pl.ds(column, half)], out_sem.at[n, k]
+        )
+        out.start()
+        leaving.append(out)
+    for out in leaving:
+        out.wait()
+
+
+def gather_rows(shard, order):
+    dp_size, chips = lax.axis_size("dp"), lax.axis_size("ctx") // 2
+    rows, columns = shard.shape
+    half = columns // 2
+    core = lax.axis_index("ctx") % 2
+    kept = lax.dynamic_slice_in_dim(shard, core * half, half, 1)
+    given = lax.dynamic_slice_in_dim(shard, (1 - core) * half, half, 1)
+    got = swap(given, 0, 1)
+    own = jnp.where(core == 0, jnp.concatenate([kept, got]), jnp.concatenate([got, kept]))
+    line = jnp.stack([own] + [swap(own, 0, 2 * k) for k in range(1, chips)])
+    pieces = {0: line}
+    for bit in order:
+        for place in list(pieces):
+            pieces[place ^ bit] = swap(pieces[place], bit, 0)
+    near = [pieces[place] for place in range(dp_size)]
+    far = [swap(piece, 0, 1) for piece in near]
+    whole = pl.pallas_call(
+        functools.partial(place_kernel, dp_size, chips),
+        out_shape=jax.ShapeDtypeStruct((dp_size * chips, 2 * rows, columns), shard.dtype),
+        in_specs=[pl.BlockSpec(memory_space=pl.ANY)] * (2 * dp_size),
+        out_specs=pl.BlockSpec(memory_space=pl.ANY),
+        scratch_shapes=[
+            pltpu.VMEM((2 * dp_size, chips, 2 * rows, half), shard.dtype),
+            pltpu.SemaphoreType.DMA((2 * dp_size, chips)),
+            pltpu.SemaphoreType.DMA((2 * dp_size, chips)),
+        ],
+        cost_estimate=pl.CostEstimate(
+            flops=0, transcendentals=0, bytes_accessed=4 * dp_size * chips * rows * columns * 2
+        ),
+    )(*near, *far)
+    return whole.reshape(dp_size * chips * 2 * rows, columns)
+
+
+def pick(value, place, axis):
+    return lax.dynamic_index_in_dim(value, place, axis, keepdims=False)
+
+
+def reduce_rows(left, right, order):
+    dp_size, chips = lax.axis_size("dp"), lax.axis_size("ctx") // 2
+    dp_rank, ctx_rank = lax.axis_index("dp"), lax.axis_index("ctx")
+    chip, core = ctx_rank // 2, ctx_rank % 2
+    rows, columns = left.shape[1] // (dp_size * chips * 2), right.shape[1]
+    half = columns // 2
+    own_side = lax.dynamic_slice_in_dim(right, core * half, half, 1)
+    far_side = lax.dynamic_slice_in_dim(right, (1 - core) * half, half, 1)
+    far = jnp.dot(left.T, far_side, preferred_element_type=jnp.float32).astype(jnp.bfloat16)
+    got = swap(far, 0, 1)
+    part = (
+        jnp.dot(left.T, own_side, preferred_element_type=jnp.float32) + got.astype(jnp.float32)
+    ).astype(jnp.bfloat16)
+    bits = [1 << n for n in reversed(range(dp_size.bit_length() - 1))]
+    part = part.reshape([2] * len(bits) + [chips, 2 * rows, half])
+    for bit in order:
+        axis = bits.index(bit)
+        bits.remove(bit)
+        side = (dp_rank // bit) % 2
+        got = swap(pick(part, 1 - side, axis), bit, 0)
+        part = (pick(part, side, axis).astype(jnp.float32) + got.astype(jnp.float32)).astype(
+            jnp.bfloat16
+        )
+    total = pick(part, chip, 0).astype(jnp.float32)
+    for k in range(1, chips):
+        total = total + swap(pick(part, chip ^ k, 0), 0, 2 * k).astype(jnp.float32)
+    total = total.reshape(2, rows, half)
+    got = swap(pick(total, 1 - core, 0), 0, 1)
+    kept = pick(total, core, 0)
+    return jnp.where(
+        core == 0,
+        jnp.concatenate([kept, got], axis=1),
+        jnp.concatenate([got, kept], axis=1),
+    )
+
+
+def gather_small(packed):
+    dp_size, ctx_size = lax.axis_size("dp"), lax.axis_size("ctx")
+    mine = lax.axis_index("dp") * ctx_size + lax.axis_index("ctx")
+    held = packed.reshape(1, 8, -1)
+    held = jnp.concatenate([held] + [swap(held, 0, k) for k in range(1, ctx_size)])
+    bit = 1
+    while bit < dp_size:
+        held = jnp.concatenate([held, swap(held, bit, 0)])
+        bit *= 2
+    devices = dp_size * ctx_size
+    held = held.reshape(devices, -1)
+    source = mine ^ jnp.arange(devices, dtype=jnp.int32)
+    chosen = (source[:, None] == jnp.arange(devices, dtype=jnp.int32)[None, :]).astype(held.dtype)
+    return jnp.dot(chosen, held, preferred_element_type=jnp.float32).astype(held.dtype)
+
+
+def reduce_small(terms):
+    dp_size, ctx_size = lax.axis_size("dp"), lax.axis_size("ctx")
+    dp_rank, ctx_rank = lax.axis_index("dp"), lax.axis_index("ctx")
+    width = terms.shape[1]
+    part = terms.reshape(dp_size, ctx_size, 8, width // 8)
+    total = pick(part, dp_rank, 0)
+    for k in range(1, dp_size):
+        total = total + swap(pick(part, dp_rank ^ k, 0), k, 0)
+    row = pick(total, ctx_rank, 0)
+    for k in range(1, ctx_size):
+        row = row + swap(pick(total, ctx_rank ^ k, 0), 0, k)
+    return row.reshape(width)
 
 
 def layer_norm(residual, norm_gain, norm_bias):
@@ -108,7 +249,7 @@
     )
 
 
-def backward_layer(grad_residual, saved_rows, layer_params, attend_back):
+def backward_layer(grad_residual, saved_rows, layer_params, attend_back, orders):
     (
         normed1,
         inv_std1,
@@ -140,12 +281,12 @@
         proj_bias,
     ) = layer_params
     grad_narrow = grad_residual.astype(jnp.bfloat16)
-    grad_proj_w = jnp.dot(hidden.T, grad_narrow, preferred_element_type=jnp.float32)
+    grad_proj_w = reduce_rows(hidden, grad_narrow, orders[2])
     grad_proj_b = jnp.sum(grad_residual, axis=0)
     grad_hidden = jnp.dot(grad_narrow, proj_weight.T, preferred_element_type=jnp.float32)
     grad_pre = grad_hidden * gelu_slope(pre_act)
     pre_narrow = grad_pre.astype(jnp.bfloat16)
-    grad_fc_w = jnp.dot(ffn_in.T, pre_narrow, preferred_element_type=jnp.float32)
+    grad_fc_w = reduce_rows(ffn_in, pre_narrow, orders[1])
     grad_fc_b = jnp.sum(grad_pre, axis=0)
     grad_norm2 = jnp.dot(pre_narrow, fc_weight.T, preferred_element_type=jnp.float32)
     grad_gain2 = jnp.sum(grad_norm2 * normed2, axis=0)
@@ -154,7 +295,7 @@
         grad_norm2, normed2, inv_std2, norm2_gain.astype(jnp.float32)
     )
     middle_narrow = grad_middle.astype(jnp.bfloat16)
-    grad_out_w = jnp.dot(mixed_rows.T, middle_narrow, preferred_element_type=jnp.float32)
+    grad_out_w = reduce_rows(mixed_rows, middle_narrow, orders[1])
     grad_out_b = jnp.sum(grad_middle, axis=0)
     grad_mixed = jnp.dot(middle_narrow, out_weight.T, preferred_element_type=jnp.float32).astype(
         jnp.bfloat16
@@ -165,7 +306,7 @@
     proj_narrow = jnp.concatenate([grad_queries, grad_keys, grad_values], axis=1).astype(
         jnp.bfloat16
     )
-    grad_qkv_w = jnp.dot(attn_in.T, proj_narrow, preferred_element_type=jnp.float32)
+    grad_qkv_w = reduce_rows(attn_in, proj_narrow, orders[0])
     grad_query_b = jnp.sum(grad_queries, axis=0)
     grad_value_b = jnp.sum(grad_values, axis=0)
     grad_norm1 = jnp.dot(proj_narrow, qkv_weight.T, preferred_element_type=jnp.float32)
@@ -353,24 +494,53 @@
             grad_v.reshape(row_count, model_width),
         )
 
+    dp_size, ctx_size = lax.axis_size("dp"), lax.axis_size("ctx")
+    devices = dp_size * ctx_size
+    rising = [1 << n for n in range(dp_size.bit_length() - 1)]
+    falling = rising[::-1]
+    narrow_list = (ln1_gain, ln1_bias, b_query, b_value, b_out, ln2_gain, ln2_bias, b_proj)
+    narrow_count = LAYERS * len(narrow_list)
+    slot = narrow_list[0].shape[1]
+    fc_slot = b_fc.shape[1]
+    used = narrow_count * slot + LAYERS * fc_slot
+    packed_size = -(-used // 1024) * 1024
+    packed = jnp.concatenate(
+        [jnp.stack(narrow_list, 1).reshape(-1), b_fc.reshape(-1)]
+        + [jnp.zeros((packed_size - used,), jnp.bfloat16)]
+    )
+    small = gather_small(packed)
+    narrow_all = jnp.transpose(
+        small[:, : narrow_count * slot].reshape(devices, narrow_count, slot), (1, 0, 2)
+    ).reshape(LAYERS, len(narrow_list), devices * slot)
+    fc_all = jnp.transpose(
+        small[:, narrow_count * slot : used].reshape(devices, LAYERS, fc_slot), (1, 0, 2)
+    ).reshape(LAYERS, devices * fc_slot)
+
     residual = block_input.reshape(row_count, model_width).astype(jnp.float32)
     kept_params = []
     saved_list = []
     for layer_idx in range(LAYERS):
+        ways = (rising, falling) if layer_idx % 2 == 0 else (falling, rising)
+        first = gather_rows(
+            jnp.concatenate([w_qkv[layer_idx], w_out[layer_idx]], axis=1), ways[0]
+        )
+        fc_weight = gather_rows(w_fc[layer_idx], ways[1])
+        proj_weight = gather_rows(w_proj[layer_idx], ways[0])
+        narrow = narrow_all[layer_idx]
         layer_params = (
-            lax.all_gather(ln1_gain[layer_idx], ("dp", "ctx"), axis=0, tiled=True),
-            lax.all_gather(ln1_bias[layer_idx], ("dp", "ctx"), axis=0, tiled=True),
-            lax.all_gather(w_qkv[layer_idx], ("dp", "ctx"), axis=0, tiled=True),
-            lax.all_gather(b_query[layer_idx], ("dp", "ctx"), axis=0, tiled=True),
-            lax.all_gather(b_value[layer_idx], ("dp", "ctx"), axis=0, tiled=True),
-            lax.all_gather(w_out[layer_idx], ("dp", "ctx"), axis=0, tiled=True),
-            lax.all_gather(b_out[layer_idx], ("dp", "ctx"), axis=0, tiled=True),
-            lax.all_gather(ln2_gain[layer_idx], ("dp", "ctx"), axis=0, tiled=True),
-            lax.all_gather(ln2_bias[layer_idx], ("dp", "ctx"), axis=0, tiled=True),
-            lax.all_gather(w_fc[layer_idx], ("dp", "ctx"), axis=0, tiled=True),
-            lax.all_gather(b_fc[layer_idx], ("dp", "ctx"), axis=0, tiled=True),
-            lax.all_gather(w_proj[layer_idx], ("dp", "ctx"), axis=0, tiled=True),
-            lax.all_gather(b_proj[layer_idx], ("dp", "ctx"), axis=0, tiled=True),
+            narrow[0],
+            narrow[1],
+            first[:, : 3 * model_width],
+            narrow[2],
+            narrow[3],
+            first[:, 3 * model_width :],
+            narrow[4],
+            narrow[5],
+            narrow[6],
+            fc_weight,
+            fc_all[layer_idx],
+            proj_weight,
+            narrow[7],
         )
         residual, saved_rows = forward_layer(residual, layer_params, attend_fwd)
         kept_params.append(layer_params)
@@ -379,47 +549,38 @@
     grad_residual = out_grad.reshape(row_count, model_width).astype(jnp.float32)
     reduced = [None] * LAYERS
     for layer_idx in reversed(range(LAYERS)):
-        layer_params = (
-            lax.all_gather(ln1_gain[layer_idx], ("dp", "ctx"), axis=0, tiled=True),
-            lax.all_gather(ln1_bias[layer_idx], ("dp", "ctx"), axis=0, tiled=True),
-            lax.all_gather(w_qkv[layer_idx], ("dp", "ctx"), axis=0, tiled=True),
-            lax.all_gather(b_query[layer_idx], ("dp", "ctx"), axis=0, tiled=True),
-            lax.all_gather(b_value[layer_idx], ("dp", "ctx"), axis=0, tiled=True),
-            lax.all_gather(w_out[layer_idx], ("dp", "ctx"), axis=0, tiled=True),
-            lax.all_gather(b_out[layer_idx], ("dp", "ctx"), axis=0, tiled=True),
-            lax.all_gather(ln2_gain[layer_idx], ("dp", "ctx"), axis=0, tiled=True),
-            lax.all_gather(ln2_bias[layer_idx], ("dp", "ctx"), axis=0, tiled=True),
-            lax.all_gather(w_fc[layer_idx], ("dp", "ctx"), axis=0, tiled=True),
-            lax.all_gather(b_fc[layer_idx], ("dp", "ctx"), axis=0, tiled=True),
-            lax.all_gather(w_proj[layer_idx], ("dp", "ctx"), axis=0, tiled=True),
-            lax.all_gather(b_proj[layer_idx], ("dp", "ctx"), axis=0, tiled=True),
-        )
-        grad_residual, layer_grads = backward_layer(
-            grad_residual, saved_list[layer_idx], layer_params, attend_back
-        )
-        reduced[layer_idx] = (
-            lax.psum_scatter(layer_grads[0], ("dp", "ctx"), scatter_dimension=0, tiled=True),
-            lax.psum_scatter(layer_grads[1], ("dp", "ctx"), scatter_dimension=0, tiled=True),
-            lax.psum_scatter(layer_grads[2], ("dp", "ctx"), scatter_dimension=0, tiled=True),
-            lax.psum_scatter(layer_grads[3], ("dp", "ctx"), scatter_dimension=0, tiled=True),
-            lax.psum_scatter(layer_grads[4], ("dp", "ctx"), scatter_dimension=0, tiled=True),
-            lax.psum_scatter(layer_grads[5], ("dp", "ctx"), scatter_dimension=0, tiled=True),
-            lax.psum_scatter(layer_grads[6], ("dp", "ctx"), scatter_dimension=0, tiled=True),
-            lax.psum_scatter(layer_grads[7], ("dp", "ctx"), scatter_dimension=0, tiled=True),
-            lax.psum_scatter(layer_grads[8], ("dp", "ctx"), scatter_dimension=0, tiled=True),
-            lax.psum_scatter(layer_grads[9], ("dp", "ctx"), scatter_dimension=0, tiled=True),
-            lax.psum_scatter(layer_grads[10], ("dp", "ctx"), scatter_dimension=0, tiled=True),
-            lax.psum_scatter(layer_grads[11], ("dp", "ctx"), scatter_dimension=0, tiled=True),
-            lax.psum_scatter(layer_grads[12], ("dp", "ctx"), scatter_dimension=0, tiled=True),
+        orders = (rising, falling, rising) if layer_idx % 2 == 0 else (falling, rising, falling)
+        grad_residual, reduced[layer_idx] = backward_layer(
+            grad_residual, saved_list[layer_idx], kept_params[layer_idx], attend_back, orders
         )
     grad_rows = grad_residual.astype(jnp.bfloat16).reshape(seq_count, local_len, model_width)
-    stacked = tuple(
-        (
-            jnp.stack([reduced[layer_idx][member] for layer_idx in range(LAYERS)])
-            for member in range(13)
-        )
-    )
-    return (output_rows, grad_rows) + stacked
+    narrow_members = (0, 1, 3, 4, 6, 7, 8, 12)
+    narrow_terms = jnp.stack([grads[member] for grads in reduced for member in narrow_members])
+    fc_terms = jnp.stack([grads[10] for grads in reduced])
+    terms = jnp.concatenate(
+        [
+            jnp.transpose(narrow_terms.reshape(narrow_count, devices, slot), (1, 0, 2)).reshape(
+                devices, -1
+            ),
+            jnp.transpose(fc_terms.reshape(LAYERS, devices, fc_slot), (1, 0, 2)).reshape(
+                devices, -1
+            ),
+            jnp.zeros((devices, packed_size - used), jnp.float32),
+        ],
+        axis=1,
+    )
+    sums = reduce_small(terms)
+    narrow_sums = sums[: narrow_count * slot].reshape(LAYERS, len(narrow_list), slot)
+    fc_sums = sums[narrow_count * slot : used].reshape(LAYERS, fc_slot)
+    stacked = []
+    for member in range(13):
+        if member in narrow_members:
+            stacked.append(narrow_sums[:, narrow_members.index(member)])
+        elif member == 10:
+            stacked.append(fc_sums)
+        else:
+            stacked.append(jnp.stack([grads[member] for grads in reduced]))
+    return (output_rows, grad_rows, *stacked)
 
 
 def solution(mesh):

time: 2270 us -> 1040 us (0.46)
  waiting for transfers between devices: 1710 us -> 319 us
  starting transfers between devices: 1.44 us -> 163 us
  blocking collectives: 55 us -> 17.7 us
  Pallas kernels: 0 us -> 29.8 us
    reduce_scatter x8 -> x0, waiting for transfers between devices: 944 us -> none  [the longest x2 280 us: shards(): lax.psum_scatter(layer_grads[9], ('dp', 'ctx'), scatter_dimension=0, tile...]
    all_gather x8 -> x0, waiting for transfers between devices: 344 us -> none  [the longest x2 126 us: shards(): lax.all_gather(w_fc[layer_idx], ('dp', 'ctx'), axis=0, tiled=True)]
    ppermute x0 -> x141, waiting for transfers between devices: none -> 316 us  [swap(): return lax.ppermute(value, ('dp', 'ctx'), pairs)]
    ppermute x0 -> x141, starting transfers between devices: none -> 162 us  [swap(): return lax.ppermute(value, ('dp', 'ctx'), pairs)]
    unnamed x26 -> x8, waiting for transfers between devices: 157 us -> 0.64 us
    reduce_scatter x2, waiting for transfers between devices: 76.5 us -> 0.01 us  [attend_back(): lax.psum_scatter(grad_k.astype(jnp.bfloat16), 'ctx', scatter_dimension=1,...]
    reduce_scatter x2, waiting for transfers between devices: 73.9 us -> 2.82 us  [attend_back(): lax.psum_scatter(grad_v.astype(jnp.bfloat16), 'ctx', scatter_dimension=1,...]
    all_gather x2, waiting for transfers between devices: 56.3 us -> 0.02 us  [attend_fwd(): value_piece = lax.all_gather(as_seqs(values), 'ctx', axis=1, tiled=True)]
  transfers between devices with their start and end apart: 25 -> 149, of which waited for: 24 -> 47; matrix products, arithmetic and copies ran while one was open for 10% -> 28% of each run, Pallas kernels for 0% -> 2%
where the time goes in v1:
time: 1040 us; the launch traced here: 1030 us
  waiting for transfers between devices  319 us (31%)
  matrix products  274 us (26%)
  starting transfers between devices  163 us (16%)
  local copies, waits for them, and re-layouts  129 us (12%)
  other arithmetic  79.2 us (8%)
  Pallas kernels  29.8 us (3%)
  between operations  18.1 us (2%)
  blocking collectives  17.7 us (2%)
    ppermute x141, waiting for transfers between devices, swap(): return lax.ppermute(value, ('dp', 'ctx'), pairs)  316 us
    ppermute x141, starting transfers between devices, swap(): return lax.ppermute(value, ('dp', 'ctx'), pairs)  162 us
    dot_general x8, matrix products, block_terms(): jnp.einsum('sqhd,skhd->shqk', grad_heads, value_heads, preferred_element_...  43.2 us
    dot_general x8, matrix products, full_step(): jnp.einsum('shqk,sqhd->skhd', probabilities.astype(jnp.bfloat16), grad_he...  36.3 us
    pallas_call x6, Pallas kernels, gather_rows(): pl.pallas_call(functools.partial(place_kernel, dp_size, chips), out_shape...  29.8 us
    dot_general x8, matrix products, block_terms(): jnp.einsum('sqhd,skhd->shqk', query_heads, key_heads, preferred_element_t...  29.3 us
    dot_general x2, matrix products, attend_fwd(): jnp.einsum('shqk,skhd->shqd', weights.astype(jnp.bfloat16), value_heads,...  25.1 us
    dot_general x2, matrix products, attend_fwd(): jnp.einsum('sqhd,skhd->shqk', query_heads, key_heads, preferred_element_t...  25 us
  transfers between devices with their start and end apart: 149, of which 47 were waited for; matrix products, arithmetic and copies ran while one was open for 28% of the time, Pallas kernels for 2%

profile of v1, /device:TPU:0, one launch (start us, length us, event | category | flops | bytes accessed | tf_op | source)
XLA Modules:
  0.0 1030.5 jit_solution(14607420291428129264)
XLA Ops:
  24.4 4.8 collective-permute-done.10
  53.1 7.9 collective-permute-done.14.refs_2_
  60.9 11.3 %collective-permute-done.15.refs_3_ = bf16[4,48,1536]{2,1,0:T(8,128)(2,1)S(1)} collective-permute-done((bf16[4,48,1536]{2,1,0:T(8,128)(2,1)S(1)}, bf16[4,48,1536]{2,1,0:T(8,128)(2,1)S(1)}, u32[]{:S(2)}, u32[]{:S(2)}) %collective-permute-start.15) | collective-permute-done | bytes 589856 | tf_op jit(solution)/shard_map/ppermute | solution.py:26
  78.2 4.9 shard_map.271
  95.3 7.8 collective-permute-done.21
  103.1 9.7 collective-permute-done.22
  115.0 9.3 collective-permute-start.32
  127.8 6.2 collective-permute-done.32
  134.0 8.2 collective-permute-done.33
  143.9 10.9 %collective-permute-done.44 = bf16[48,1536]{1,0:T(8,128)(2,1)S(1)} collective-permute-done((bf16[48,1536]{1,0:T(8,128)(2,1)S(1)}, bf16[48,1536]{1,0:T(8,128)(2,1)S(1)}, u32[]{:S(2)}, u32[]{:S(2)}) %collective-permute-start.44) | collective-permute-done | bytes 147488 | tf_op jit(solution)/shard_map/ppermute | solution.py:26
  162.7 9.1 collective-permute-done.35.refs_1_
  173.0 9.9 collective-permute-done.47.refs_2_
  184.5 11.7 %collective-permute-done.26.refs_3_ = bf16[4,48,1536]{2,1,0:T(8,128)(2,1)} collective-permute-done((bf16[4,48,1536]{2,1,0:T(8,128)(2,1)S(1)}, bf16[4,48,1536]{2,1,0:T(8,128)(2,1)}, u32[]{:S(2)}, u32[]{:S(2)}) %collective-permute-start.26) | collective-permute-done | bytes 589856 | tf_op jit(solution)/shard_map/ppermute | solution.py:26
  198.9 13.3 %collective-permute-done.48.refs_3_ = bf16[4,48,1536]{2,1,0:T(8,128)(2,1)} collective-permute-done((bf16[4,48,1536]{2,1,0:T(8,128)(2,1)}, bf16[4,48,1536]{2,1,0:T(8,128)(2,1)}, u32[]{:S(2)}, u32[]{:S(2)}) %collective-permute-start.48) | collective-permute-done | bytes 589856 | tf_op jit(solution)/shard_map/ppermute | solution.py:26
  212.8 17.7 %all_gather.21 = s32[1,2048]{1,0:T(1,128)S(1)} all-gather(s32[1,256]{1,0:T(1,128)S(1)} %copy-done.82), channel_id=1, replica_groups=mesh['dp'=4,'ctx'=8] {'ctx'}, dimensions={1}, use_global_device_ids=true | all-gather | bytes 9216 | tf_op jit(solution)/shard_map/all_gather | solution.py:367
  237.8 5.1 shard_map.272
  242.9 4.9 shard_map.273
  247.9 4.9 shard_map.274
  252.9 4.7 copy.59
  257.6 12.5 %fusion.40 = (f32[12,256]{1,0:T(8,128)S(1)}, f32[12,256,2048]{2,1,0:T(8,128)}) fusion(pred[256,2048]{1,0:T(8,128)(4,1)S(1)} %fusion.75, bf16[256,12,64]{0,2,1:T(8,128)(2,1)S(1)} %bitcast.705, bf16[2048,12,64]{0,2,1:T(8,128)(2,1)} %bitcast.709), kind=kOutput, calls=%fused_computation.64 | convolution fusion | flops 824177664 | bytes 29241344 | tf_op jit(solution)/shard_map/sqhd,skhd->shqk/dot_general | solution.py:388
  270.1 11.9 %fusion.42 = f32[12,256]{1,0:T(8,128)S(1)} fusion(f32[12,256,2048]{2,1,0:T(8,128)} %get-tuple-element.801, f32[12,256]{1,0:T(8,128)S(1)} %broadcast_maximum_fusion.1, pred[256,2048]{1,0:T(8,128)(4,1)S(1)} %fusion.75), kind=kLoop, calls=%fused_computation.66 | loop fusion | flops 31454208 | bytes 25714688 | tf_op jit(solution)/shard_map/reduce_sum | solution.py:396
  282.1 4.7 copy.60
  286.8 12.7 %fusion.96 = bf16[12,256,64]{1,2,0:T(8,128)(2,1)S(1)} fusion(bf16[2048,12,64]{0,2,1:T(8,128)(2,1)} %bitcast.762, f32[12,256,2048]{2,1,0:T(8,128)} %get-tuple-element.801, f32[12,256]{1,0:T(8,128)S(1)} %broadcast_maximum_fusion.1, pred[256,2048]{1,0:T(8,128)(4,1)S(1)} %fusion.75, f32[12,256]{1,0:T(8,128)S(1)} %fusion.42), kind=kOutput, calls=%fused_computation.170 | convolution fusion | flops 837156864 | bytes 29253632 | tf_op jit(solution)/shard_map/shqk,skhd->shqd/dot_general | solution.py:397
  326.5 6.7 collective-permute-done.55
  337.5 23.1 %collective-permute-done.66 = bf16[192,384]{1,0:T(8,128)(2,1)S(1)} collective-permute-done((bf16[192,384]{1,0:T(8,128)(2,1)}, bf16[192,384]{1,0:T(8,128)(2,1)S(1)}, u32[]{:S(2)}, u32[]{:S(2)}) %collective-permute-start.66) | collective-permute-done | bytes 147488 | tf_op jit(solution)/shard_map/ppermute | solution.py:26
  365.6 13.2 %collective-permute-done.69.refs_2_ = bf16[4,192,384]{2,1,0:T(8,128)(2,1)} collective-permute-done((bf16[4,192,384]{2,1,0:T(8,128)(2,1)S(1)}, bf16[4,192,384]{2,1,0:T(8,128)(2,1)}, u32[]{:S(2)}, u32[]{:S(2)}) %collective-permute-start.69) | collective-permute-done | bytes 589856 | tf_op jit(solution)/shard_map/ppermute | solution.py:26
  379.4 7.8 collective-permute-done.59.refs_3_
  391.1 5.0 shard_map.275
  396.2 4.9 shard_map.276
  401.3 4.9 copy.62
  406.2 12.5 %fusion.41 = (f32[12,256]{1,0:T(8,128)S(1)}, f32[12,256,2048]{2,1,0:T(8,128)}) fusion(pred[256,2048]{1,0:T(8,128)(4,1)S(1)} %fusion.75, bf16[256,12,64]{0,2,1:T(8,128)(2,1)S(1)} %bitcast.707, bf16[2048,12,64]{0,2,1:T(8,128)(2,1)} %bitcast.710), kind=kOutput, calls=%fused_computation.65 | convolution fusion | flops 824177664 | bytes 29241344 | tf_op jit(solution)/shard_map/sqhd,skhd->shqk/dot_general | solution.py:388
  418.7 11.9 %fusion.44 = f32[12,256]{1,0:T(8,128)S(1)} fusion(f32[12,256,2048]{2,1,0:T(8,128)} %get-tuple-element.807, f32[12,256]{1,0:T(8,128)S(1)} %broadcast_maximum_fusion, pred[256,2048]{1,0:T(8,128)(4,1)S(1)} %fusion.75), kind=kLoop, calls=%fused_computation.68 | loop fusion | flops 31454208 | bytes 25714688 | tf_op jit(solution)/shard_map/reduce_sum | solution.py:396
  431.3 4.7 copy.63
  436.0 12.3 %fusion.102 = bf16[12,256,64]{1,2,0:T(8,128)(2,1)S(1)} fusion(bf16[2048,12,64]{0,2,1:T(8,128)(2,1)} %bitcast.761, f32[12,256,2048]{2,1,0:T(8,128)} %get-tuple-element.807, f32[12,256]{1,0:T(8,128)S(1)} %broadcast_maximum_fusion, pred[256,2048]{1,0:T(8,128)(4,1)S(1)} %fusion.75, f32[12,256]{1,0:T(8,128)S(1)} %fusion.44), kind=kOutput, calls=%fused_computation.172 | convolution fusion | flops 837156864 | bytes 29253632 | tf_op jit(solution)/shard_map/shqk,skhd->shqd/dot_general | solution.py:397
  471.1 94.5 %while.36 = (s32[]{:T(128)}, f32[1,256,12,64]{1,3,2,0:T(8,128)}, bf16[1,2048,768]{1,2,0:T(8,128)(2,1)}, bf16[1,2048,768]{1,2,0:T(8,128)(2,1)}, bf16[1,2048,768]{...) while((s32[]{:T(128)}, f32[1,256,12,64]{1,3,2,0:T(8,128)}, ...), condition=%wide.region_16.17_spmd.clone, body=%wide.region_15.16_spmd.clone.sunk | while | flops 1027277568 | bytes 48940324 | solution.py:480
  479.5 5.4 fusion.344
  486.0 4.5 fusion.346
  502.9 5.4 fusion.344
  526.6 5.4 fusion.344
  550.3 5.4 fusion.344
  566.7 4.8 convolution_convert_fusion
  580.5 6.4 fusion.83
  600.8 7.8 collective-permute-start.109
  616.1 7.0 collective-permute-done.135
  633.9 6.0 collective-permute-done.136
  641.7 7.8 collective-permute-start.137
  677.9 94.3 %while.37 = (s32[]{:T(128)}, f32[1,256,12,64]{1,3,2,0:T(8,128)}, bf16[1,2048,768]{1,2,0:T(8,128)(2,1)}, bf16[1,2048,768]{1,2,0:T(8,128)(2,1)}, bf16[1,2048,768]{...) while((s32[]{:T(128)}, f32[1,256,12,64]{1,3,2,0:T(8,128)}, ...), condition=%wide.region_25.26_spmd.clone, body=%wide.region_24.25_spmd.clone.sunk | while | flops 1027277568 | bytes 48940324 | solution.py:480
  686.3 5.4 fusion.358
  709.7 5.4 fusion.358
  733.3 5.4 fusion.358
  757.0 5.4 fusion.358
  780.7 11.6 %collective-permute-done.124 = bf16[48,1536]{1,0:T(8,128)(2,1)S(1)} collective-permute-done((bf16[48,1536]{1,0:T(8,128)(2,1)S(1)}, bf16[48,1536]{1,0:T(8,128)(2,1)S(1)}, u32[]{:S(2)}, u32[]{:S(2)}) %collective-permute-start.124) | collective-permute-done | bytes 147488 | tf_op jit(solution)/shard_map/ppermute | solution.py:26
  809.1 5.1 collective-permute-done.100
  823.0 6.3 collective-permute-start.102
  853.9 12.1 %collective-permute-done.93 = bf16[2,4,48,1152]{3,2,1,0:T(8,128)(2,1)} collective-permute-done((bf16[2,4,48,1152]{3,2,1,0:T(8,128)(2,1)}, bf16[2,4,48,1152]{3,2,1,0:T(8,128)(2,1)}, u32[]{:S(2)}, u32[]{:S(2)}) %collective-permute-start.93) | collective-permute-done | bytes 884768 | tf_op jit(solution)/shard_map/ppermute | solution.py:26
  873.5 16.2 %collective-permute-done.94 = bf16[4,48,1152]{2,1,0:T(8,128)(2,1)S(1)} collective-permute-done((bf16[4,48,1152]{2,1,0:T(8,128)(2,1)S(1)}, bf16[4,48,1152]{2,1,0:T(8,128)(2,1)S(1)}, u32[]{:S(2)}, u32[]{:S(2)}) %collective-permute-start.94) | collective-permute-done | bytes 442400 | tf_op jit(solution)/shard_map/ppermute | solution.py:26
  895.5 5.8 collective-permute-done.96
  905.6 11.9 %collective-permute-done.129 = bf16[4,192,384]{2,1,0:T(8,128)(2,1)S(1)} collective-permute-done((bf16[4,192,384]{2,1,0:T(8,128)(2,1)S(1)}, bf16[4,192,384]{2,1,0:T(8,128)(2,1)S(1)}, u32[]{:S(2)}, u32[]{:S(2)}) %collective-permute-start.129) | collective-permute-done | bytes 589856 | tf_op jit(solution)/shard_map/ppermute | solution.py:26
  927.4 6.1 collective-permute-done.131
  933.7 12.0 %collective-permute-done.117 = bf16[48,1536]{1,0:T(8,128)(2,1)S(1)} collective-permute-done((bf16[48,1536]{1,0:T(8,128)(2,1)S(1)}, bf16[48,1536]{1,0:T(8,128)(2,1)S(1)}, u32[]{:S(2)}, u32[]{:S(2)}) %collective-permute-start.117) | collective-permute-done | bytes 147488 | tf_op jit(solution)/shard_map/ppermute | solution.py:26
  949.4 5.0 fusion.120
  974.2 17.1 %collective-permute-done.86 = bf16[2,4,48,1152]{3,2,1,0:T(8,128)(2,1)} collective-permute-done((bf16[2,4,48,1152]{3,2,1,0:T(8,128)(2,1)}, bf16[2,4,48,1152]{3,2,1,0:T(8,128)(2,1)}, u32[]{:S(2)}, u32[]{:S(2)}) %collective-permute-start.86) | collective-permute-done | bytes 884768 | tf_op jit(solution)/shard_map/ppermute | solution.py:26
  999.1 4.7 collective-permute-done.87
  1015.3 5.6 collective-permute-done.89
  (1054 shorter events, 493.5 us)
Async XLA Ops:
  7.2 245.7 %all-gather.9.cloned.1.call-start = ((), (), s32[]{:S(2)}) async-start(), calls=%async_computation.8 | async-start | bytes 3538944 | tf_op jit(solution)/shard_map/all_gather | solution.py:380
  13.5 23.1 %collective-permute-start = (bf16[1,8,128]{2,1,0:T(8,128)(2,1)S(1)}, bf16[1,8,128]{2,1,0:T(8,128)(2,1)S(1)}, u32[]{:S(2)}, u32[]{:S(2)}) collective-permute-start(bf16[1,8,128]{2,1,0:T(8,128)(2,1)S(1)} %get-tuple-element.784), channel_id=1, source_target_pairs={{0,1},{1,0},{2,3},{3,2},{4,5},{5,4},{6,7},{7,6},{8,9},{9,8},{10,11... | collective-permute-start | bytes 6152 | tf_op jit(solution)/shard_map/ppermute | solution.py:26
  14.0 26.4 %collective-permute-start.1 = (bf16[1,8,128]{2,1,0:T(8,128)(2,1)S(1)}, bf16[1,8,128]{2,1,0:T(8,128)(2,1)S(1)}, u32[]{:S(2)}, u32[]{:S(2)}) collective-permute-start(bf16[1,8,128]{2,1,0:T(8,128)(2,1)S(1)} %get-tuple-element.784), channel_id=1, source_target_pairs={{0,2},{1,3},{2,0},{3,1},{4,6},{5,7},{6,4},{7,5},{8,10},{9,11},{10,... | collective-permute-start | bytes 6152 | tf_op jit(solution)/shard_map/ppermute | solution.py:26
  49.4 22.8 %collective-permute-start.15 = (bf16[4,48,1536]{2,1,0:T(8,128)(2,1)S(1)}, bf16[4,48,1536]{2,1,0:T(8,128)(2,1)S(1)}, u32[]{:S(2)}, u32[]{:S(2)}) collective-permute-start(bf16[4,48,1536]{2,1,0:T(8,128)(2,1)S(1)} %collective-permute-done.13.refs_1_), channel_id=1, source_target_pairs={{0,16},{1,17},{2,18},{3,19},{4,20},{5,21},{6,22},{7,23},{8,24},{9,... | collective-permute-start | bytes 1769480 | tf_op jit(solution)/shard_map/ppermute | solution.py:26
  51.0 21.2 %collective-permute-start.7 = (bf16[8,8,128]{2,1,0:T(8,128)(2,1)S(1)}, bf16[8,8,128]{2,1,0:T(8,128)(2,1)S(1)}, u32[]{:S(2)}, u32[]{:S(2)}) collective-permute-start(bf16[8,8,128]{2,1,0:T(8,128)(2,1)S(1)} %get-tuple-element.787), channel_id=1, source_target_pairs={{0,8},{1,9},{2,10},{3,11},{4,12},{5,13},{6,14},{7,15},{8,0},{9,1},... | collective-permute-start | bytes 49160 | tf_op jit(solution)/shard_map/ppermute | solution.py:26
  52.6 25.6 %collective-permute-start.16 = (bf16[4,48,1536]{2,1,0:T(8,128)(2,1)S(1)}, bf16[4,48,1536]{2,1,0:T(8,128)(2,1)}, u32[]{:S(2)}, u32[]{:S(2)}) collective-permute-start(bf16[4,48,1536]{2,1,0:T(8,128)(2,1)S(1)} %pad_maximum_fusion.2.refs_0_), channel_id=1, source_target_pairs={{0,1},{1,0},{2,3},{3,2},{4,5},{5,4},{6,7},{7,6},{8,9},{9,8},{10,11... | collective-permute-start | bytes 1769480 | tf_op jit(solution)/shard_map/ppermute | solution.py:26
  52.6 25.6 %collective-permute-start.17 = (bf16[4,48,1536]{2,1,0:T(8,128)(2,1)S(1)}, bf16[4,48,1536]{2,1,0:T(8,128)(2,1)}, u32[]{:S(2)}, u32[]{:S(2)}) collective-permute-start(bf16[4,48,1536]{2,1,0:T(8,128)(2,1)S(1)} %collective-permute-done.13.refs_1_), channel_id=1, source_target_pairs={{0,1},{1,0},{2,3},{3,2},{4,5},{5,4},{6,7},{7,6},{8,9},{9,8},{10,11... | collective-permute-start | bytes 1769480 | tf_op jit(solution)/shard_map/ppermute | solution.py:26
  88.7 193.4 %all-gather.11.cloned.1.call-start = ((), (), s32[]{:S(2)}) async-start(), calls=%async_computation.9 | async-start | bytes 3538944 | tf_op jit(solution)/shard_map/all_gather | solution.py:381
  90.3 24.6 %collective-permute-start.31 = (bf16[96,384]{1,0:T(8,128)(2,1)S(1)}, bf16[96,384]{1,0:T(8,128)(2,1)S(1)}, u32[]{:S(2)}, u32[]{:S(2)}) collective-permute-start(bf16[96,384]{1,0:T(8,128)(2,1)S(1)} %get-tuple-element.755), channel_id=1, source_target_pairs={{0,1},{1,0},{2,3},{3,2},{4,5},{5,4},{6,7},{7,6},{8,9},{9,8},{10,11... | collective-permute-start | bytes 221192 | tf_op jit(solution)/shard_map/ppermute | solution.py:26
  90.9 21.9 %collective-permute-start.22 = (bf16[48,1536]{1,0:T(8,128)(2,1)S(1)}, bf16[48,1536]{1,0:T(8,128)(2,1)S(1)}, u32[]{:S(2)}, u32[]{:S(2)}) collective-permute-start(bf16[48,1536]{1,0:T(8,128)(2,1)S(1)} %maximum_select_fusion.9), channel_id=1, source_target_pairs={{0,4},{1,5},{2,6},{3,7},{4,0},{5,1},{6,2},{7,3},{8,12},{9,13},{10,... | collective-permute-start | bytes 442376 | tf_op jit(solution)/shard_map/ppermute | solution.py:26
  92.4 20.5 %collective-permute-start.23 = (bf16[48,1536]{1,0:T(8,128)(2,1)S(1)}, bf16[48,1536]{1,0:T(8,128)(2,1)S(1)}, u32[]{:S(2)}, u32[]{:S(2)}) collective-permute-start(bf16[48,1536]{1,0:T(8,128)(2,1)S(1)} %maximum_select_fusion.9), channel_id=1, source_target_pairs={{0,6},{1,7},{2,4},{3,5},{4,2},{5,3},{6,0},{7,1},{8,14},{9,15},{10,... | collective-permute-start | bytes 442376 | tf_op jit(solution)/shard_map/ppermute | solution.py:26
  112.9 44.0 %collective-permute-start.25 = (bf16[4,48,1536]{2,1,0:T(8,128)(2,1)S(1)}, bf16[4,48,1536]{2,1,0:T(8,128)(2,1)S(1)}, u32[]{:S(2)}, u32[]{:S(2)}) collective-permute-start(bf16[4,48,1536]{2,1,0:T(8,128)(2,1)S(1)} %pad_maximum_fusion.3.refs_0_), channel_id=1, source_target_pairs={{0,16},{1,17},{2,18},{3,19},{4,20},{5,21},{6,22},{7,23},{8,24},{9,... | collective-permute-start | bytes 1769480 | tf_op jit(solution)/shard_map/ppermute | solution.py:26
  115.0 19.1 %collective-permute-start.32 = (bf16[192,384]{1,0:T(8,128)(2,1)S(1)}, bf16[192,384]{1,0:T(8,128)(2,1)S(1)}, u32[]{:S(2)}, u32[]{:S(2)}) collective-permute-start(bf16[192,384]{1,0:T(8,128)(2,1)S(1)} %maximum_select_fusion.11), channel_id=1, source_target_pairs={{0,2},{1,3},{2,0},{3,1},{4,6},{5,7},{6,4},{7,5},{8,10},{9,11},{10,... | collective-permute-start | bytes 442376 | tf_op jit(solution)/shard_map/ppermute | solution.py:26
  124.2 19.0 %collective-permute-start.34 = (bf16[192,384]{1,0:T(8,128)(2,1)S(1)}, bf16[192,384]{1,0:T(8,128)(2,1)S(1)}, u32[]{:S(2)}, u32[]{:S(2)}) collective-permute-start(bf16[192,384]{1,0:T(8,128)(2,1)S(1)} %maximum_select_fusion.11), channel_id=1, source_target_pairs={{0,6},{1,7},{2,4},{3,5},{4,2},{5,3},{6,0},{7,1},{8,14},{9,15},{10,... | collective-permute-start | bytes 442376 | tf_op jit(solution)/shard_map/ppermute | solution.py:26
  134.0 20.8 %collective-permute-start.44 = (bf16[48,1536]{1,0:T(8,128)(2,1)S(1)}, bf16[48,1536]{1,0:T(8,128)(2,1)S(1)}, u32[]{:S(2)}, u32[]{:S(2)}) collective-permute-start(bf16[48,1536]{1,0:T(8,128)(2,1)S(1)} %maximum_select_fusion.13), channel_id=1, source_target_pairs={{0,4},{1,5},{2,6},{3,7},{4,0},{5,1},{6,2},{7,3},{8,12},{9,13},{10,... | collective-permute-start | bytes 442376 | tf_op jit(solution)/shard_map/ppermute | solution.py:26
  159.4 241.9 %all-gather.13.cloned.1.call-start = ((), (), s32[]{:S(2)}) async-start(), calls=%async_computation.10 | async-start | bytes 3538944 | tf_op jit(solution)/shard_map/all_gather | solution.py:380
  160.7 22.2 %collective-permute-start.47 = (bf16[4,48,1536]{2,1,0:T(8,128)(2,1)S(1)}, bf16[4,48,1536]{2,1,0:T(8,128)(2,1)}, u32[]{:S(2)}, u32[]{:S(2)}) collective-permute-start(bf16[4,48,1536]{2,1,0:T(8,128)(2,1)S(1)} %pad_maximum_fusion.5.refs_0_), channel_id=1, source_target_pairs={{0,16},{1,17},{2,18},{3,19},{4,20},{5,21},{6,22},{7,23},{8,24},{9,... | collective-permute-start | bytes 1769480 | tf_op jit(solution)/shard_map/ppermute | solution.py:26
  161.3 23.2 %collective-permute-start.46 = (bf16[4,48,1536]{2,1,0:T(8,128)(2,1)S(1)}, bf16[4,48,1536]{2,1,0:T(8,128)(2,1)S(1)}, u32[]{:S(2)}, u32[]{:S(2)}) collective-permute-start(bf16[4,48,1536]{2,1,0:T(8,128)(2,1)S(1)} %pad_maximum_fusion.5.refs_0_), channel_id=1, source_target_pairs={{0,8},{1,9},{2,10},{3,11},{4,12},{5,13},{6,14},{7,15},{8,0},{9,1},... | collective-permute-start | bytes 1769480 | tf_op jit(solution)/shard_map/ppermute | solution.py:26
  171.8 24.4 %collective-permute-start.26 = (bf16[4,48,1536]{2,1,0:T(8,128)(2,1)S(1)}, bf16[4,48,1536]{2,1,0:T(8,128)(2,1)}, u32[]{:S(2)}, u32[]{:S(2)}) collective-permute-start(bf16[4,48,1536]{2,1,0:T(8,128)(2,1)S(1)} %collective-permute-done.25.refs_2_), channel_id=1, source_target_pairs={{0,8},{1,9},{2,10},{3,11},{4,12},{5,13},{6,14},{7,15},{8,0},{9,1},... | collective-permute-start | bytes 1769480 | tf_op jit(solution)/shard_map/ppermute | solution.py:26
  172.5 23.7 %collective-permute-start.28 = (bf16[4,48,1536]{2,1,0:T(8,128)(2,1)}, bf16[4,48,1536]{2,1,0:T(8,128)(2,1)S(1)}, u32[]{:S(2)}, u32[]{:S(2)}) collective-permute-start(bf16[4,48,1536]{2,1,0:T(8,128)(2,1)} %collective-permute-done.24.refs_1_), channel_id=1, source_target_pairs={{0,1},{1,0},{2,3},{3,2},{4,5},{5,4},{6,7},{7,6},{8,9},{9,8},{10,11... | collective-permute-start | bytes 1769480 | tf_op jit(solution)/shard_map/ppermute | solution.py:26
  172.5 24.4 %collective-permute-start.29 = (bf16[4,48,1536]{2,1,0:T(8,128)(2,1)S(1)}, bf16[4,48,1536]{2,1,0:T(8,128)(2,1)S(1)}, u32[]{:S(2)}, u32[]{:S(2)}) collective-permute-start(bf16[4,48,1536]{2,1,0:T(8,128)(2,1)S(1)} %collective-permute-done.25.refs_2_), channel_id=1, source_target_pairs={{0,1},{1,0},{2,3},{3,2},{4,5},{5,4},{6,7},{7,6},{8,9},{9,8},{10,11... | collective-permute-start | bytes 1769480 | tf_op jit(solution)/shard_map/ppermute | solution.py:26
  198.3 49.5 %collective-permute-start.49 = (bf16[4,48,1536]{2,1,0:T(8,128)(2,1)S(1)}, bf16[4,48,1536]{2,1,0:T(8,128)(2,1)}, u32[]{:S(2)}, u32[]{:S(2)}) collective-permute-start(bf16[4,48,1536]{2,1,0:T(8,128)(2,1)S(1)} %pad_maximum_fusion.5.refs_0_), channel_id=1, source_target_pairs={{0,1},{1,0},{2,3},{3,2},{4,5},{5,4},{6,7},{7,6},{8,9},{9,8},{10,11... | collective-permute-start | bytes 1769480 | tf_op jit(solution)/shard_map/ppermute | solution.py:26
  198.4 49.5 %collective-permute-start.51 = (bf16[4,48,1536]{2,1,0:T(8,128)(2,1)}, bf16[4,48,1536]{2,1,0:T(8,128)(2,1)}, u32[]{:S(2)}, u32[]{:S(2)}) collective-permute-start(bf16[4,48,1536]{2,1,0:T(8,128)(2,1)} %collective-permute-done.47.refs_2_), channel_id=1, source_target_pairs={{0,1},{1,0},{2,3},{3,2},{4,5},{5,4},{6,7},{7,6},{8,9},{9,8},{10,11... | collective-permute-start | bytes 1769480 | tf_op jit(solution)/shard_map/ppermute | solution.py:26
  198.9 49.0 %collective-permute-start.50 = (bf16[4,48,1536]{2,1,0:T(8,128)(2,1)S(1)}, bf16[4,48,1536]{2,1,0:T(8,128)(2,1)}, u32[]{:S(2)}, u32[]{:S(2)}) collective-permute-start(bf16[4,48,1536]{2,1,0:T(8,128)(2,1)S(1)} %collective-permute-done.46.refs_1_), channel_id=1, source_target_pairs={{0,1},{1,0},{2,3},{3,2},{4,5},{5,4},{6,7},{7,6},{8,9},{9,8},{10,11... | collective-permute-start | bytes 1769480 | tf_op jit(solution)/shard_map/ppermute | solution.py:26
  212.2 30.6 %collective-permute-start.41 = (bf16[4,192,384]{2,1,0:T(8,128)(2,1)}, bf16[4,192,384]{2,1,0:T(8,128)(2,1)}, u32[]{:S(2)}, u32[]{:S(2)}) collective-permute-start(bf16[4,192,384]{2,1,0:T(8,128)(2,1)} %collective-permute-done.37.refs_3_), channel_id=1, source_target_pairs={{0,1},{1,0},{2,3},{3,2},{4,5},{5,4},{6,7},{7,6},{8,9},{9,8},{10,11... | collective-permute-start | bytes 1769480 | tf_op jit(solution)/shard_map/ppermute | solution.py:26
  212.3 35.6 %collective-permute-start.52 = (bf16[4,48,1536]{2,1,0:T(8,128)(2,1)}, bf16[4,48,1536]{2,1,0:T(8,128)(2,1)}, u32[]{:S(2)}, u32[]{:S(2)}) collective-permute-start(bf16[4,48,1536]{2,1,0:T(8,128)(2,1)} %collective-permute-done.48.refs_3_), channel_id=1, source_target_pairs={{0,1},{1,0},{2,3},{3,2},{4,5},{5,4},{6,7},{7,6},{8,9},{9,8},{10,11... | collective-permute-start | bytes 1769480 | tf_op jit(solution)/shard_map/ppermute | solution.py:26
  311.9 119.4 %all-gather.15.cloned.1.call-start = ((), (), s32[]{:S(2)}) async-start(), calls=%async_computation.11 | async-start | bytes 3538944 | tf_op jit(solution)/shard_map/all_gather | solution.py:381
  313.5 19.7 %collective-permute-start.55 = (bf16[48,1536]{1,0:T(8,128)(2,1)S(1)}, bf16[48,1536]{1,0:T(8,128)(2,1)S(1)}, u32[]{:S(2)}, u32[]{:S(2)}) collective-permute-start(bf16[48,1536]{1,0:T(8,128)(2,1)S(1)} %maximum_select_fusion.15), channel_id=1, source_target_pairs={{0,4},{1,5},{2,6},{3,7},{4,0},{5,1},{6,2},{7,3},{8,12},{9,13},{10,... | collective-permute-start | bytes 442376 | tf_op jit(solution)/shard_map/ppermute | solution.py:26
  313.8 19.4 %collective-permute-start.56 = (bf16[48,1536]{1,0:T(8,128)(2,1)S(1)}, bf16[48,1536]{1,0:T(8,128)(2,1)S(1)}, u32[]{:S(2)}, u32[]{:S(2)}) collective-permute-start(bf16[48,1536]{1,0:T(8,128)(2,1)S(1)} %maximum_select_fusion.15), channel_id=1, source_target_pairs={{0,6},{1,7},{2,4},{3,5},{4,2},{5,3},{6,0},{7,1},{8,14},{9,15},{10,... | collective-permute-start | bytes 442376 | tf_op jit(solution)/shard_map/ppermute | solution.py:26
  318.6 42.0 %collective-permute-start.66 = (bf16[192,384]{1,0:T(8,128)(2,1)}, bf16[192,384]{1,0:T(8,128)(2,1)S(1)}, u32[]{:S(2)}, u32[]{:S(2)}) collective-permute-start(bf16[192,384]{1,0:T(8,128)(2,1)} %maximum_select_fusion.17), channel_id=1, source_target_pairs={{0,4},{1,5},{2,6},{3,7},{4,0},{5,1},{6,2},{7,3},{8,12},{9,13},{10,... | collective-permute-start | bytes 442376 | tf_op jit(solution)/shard_map/ppermute | solution.py:26
  322.2 329.7 %reduce-scatter.5.cloned.1.call-start = ((), (), s32[]{:S(2)}) async-start(), calls=%async_computation.4 | async-start | bytes 3538944 | tf_op jit(solution)/shard_map/reduce_scatter | solution.py:484
  326.5 34.1 %collective-permute-start.67 = (bf16[192,384]{1,0:T(8,128)(2,1)}, bf16[192,384]{1,0:T(8,128)(2,1)S(1)}, u32[]{:S(2)}, u32[]{:S(2)}) collective-permute-start(bf16[192,384]{1,0:T(8,128)(2,1)} %maximum_select_fusion.17), channel_id=1, source_target_pairs={{0,6},{1,7},{2,4},{3,5},{4,2},{5,3},{6,0},{7,1},{8,14},{9,15},{10,... | collective-permute-start | bytes 442376 | tf_op jit(solution)/shard_map/ppermute | solution.py:26
  333.3 31.2 %collective-permute-start.57 = (bf16[4,48,1536]{2,1,0:T(8,128)(2,1)S(1)}, bf16[4,48,1536]{2,1,0:T(8,128)(2,1)S(1)}, u32[]{:S(2)}, u32[]{:S(2)}) collective-permute-start(bf16[4,48,1536]{2,1,0:T(8,128)(2,1)S(1)} %pad_maximum_fusion.6.refs_0_), channel_id=1, source_target_pairs={{0,8},{1,9},{2,10},{3,11},{4,12},{5,13},{6,14},{7,15},{8,0},{9,1},... | collective-permute-start | bytes 1769480 | tf_op jit(solution)/shard_map/ppermute | solution.py:26
  334.2 30.9 %collective-permute-start.58 = (bf16[4,48,1536]{2,1,0:T(8,128)(2,1)S(1)}, bf16[4,48,1536]{2,1,0:T(8,128)(2,1)S(1)}, u32[]{:S(2)}, u32[]{:S(2)}) collective-permute-start(bf16[4,48,1536]{2,1,0:T(8,128)(2,1)S(1)} %pad_maximum_fusion.6.refs_0_), channel_id=1, source_target_pairs={{0,16},{1,17},{2,18},{3,19},{4,20},{5,21},{6,22},{7,23},{8,24},{9,... | collective-permute-start | bytes 1769480 | tf_op jit(solution)/shard_map/ppermute | solution.py:26
  337.5 27.6 %collective-permute-start.60 = (bf16[4,48,1536]{2,1,0:T(8,128)(2,1)S(1)}, bf16[4,48,1536]{2,1,0:T(8,128)(2,1)S(1)}, u32[]{:S(2)}, u32[]{:S(2)}) collective-permute-start(bf16[4,48,1536]{2,1,0:T(8,128)(2,1)S(1)} %pad_maximum_fusion.6.refs_0_), channel_id=1, source_target_pairs={{0,1},{1,0},{2,3},{3,2},{4,5},{5,4},{6,7},{7,6},{8,9},{9,8},{10,11... | collective-permute-start | bytes 1769480 | tf_op jit(solution)/shard_map/ppermute | solution.py:26
  364.5 22.6 %collective-permute-start.59 = (bf16[4,48,1536]{2,1,0:T(8,128)(2,1)S(1)}, bf16[4,48,1536]{2,1,0:T(8,128)(2,1)}, u32[]{:S(2)}, u32[]{:S(2)}) collective-permute-start(bf16[4,48,1536]{2,1,0:T(8,128)(2,1)S(1)} %collective-permute-done.57.refs_1_), channel_id=1, source_target_pairs={{0,16},{1,17},{2,18},{3,19},{4,20},{5,21},{6,22},{7,23},{8,24},{9,... | collective-permute-start | bytes 1769480 | tf_op jit(solution)/shard_map/ppermute | solution.py:26
  365.1 22.1 %collective-permute-start.61 = (bf16[4,48,1536]{2,1,0:T(8,128)(2,1)S(1)}, bf16[4,48,1536]{2,1,0:T(8,128)(2,1)S(1)}, u32[]{:S(2)}, u32[]{:S(2)}) collective-permute-start(bf16[4,48,1536]{2,1,0:T(8,128)(2,1)S(1)} %collective-permute-done.57.refs_1_), channel_id=1, source_target_pairs={{0,1},{1,0},{2,3},{3,2},{4,5},{5,4},{6,7},{7,6},{8,9},{9,8},{10,11... | collective-permute-start | bytes 1769480 | tf_op jit(solution)/shard_map/ppermute | solution.py:26
  365.1 22.6 %collective-permute-start.62 = (bf16[4,48,1536]{2,1,0:T(8,128)(2,1)S(1)}, bf16[4,48,1536]{2,1,0:T(8,128)(2,1)S(1)}, u32[]{:S(2)}, u32[]{:S(2)}) collective-permute-start(bf16[4,48,1536]{2,1,0:T(8,128)(2,1)S(1)} %collective-permute-done.58.refs_2_), channel_id=1, source_target_pairs={{0,1},{1,0},{2,3},{3,2},{4,5},{5,4},{6,7},{7,6},{8,9},{9,8},{10,11... | collective-permute-start | bytes 1769480 | tf_op jit(solution)/shard_map/ppermute | solution.py:26
  565.6 89.1 %reduce-scatter.7.cloned.1.call-start = ((), (), s32[]{:S(2)}) async-start(), calls=%async_computation.5 | async-start | bytes 3538944 | tf_op jit(solution)/shard_map/reduce_scatter | solution.py:487
  566.2 382.0 %reduce-scatter.9.cloned.1.call-start = ((), (), s32[]{:S(2)}) async-start(), calls=%async_computation.6 | async-start | bytes 3538944 | tf_op jit(solution)/shard_map/reduce_scatter | solution.py:484
  571.5 19.2 %collective-permute-start.134 = (bf16[3072,384]{1,0:T(8,128)(2,1)}, bf16[3072,384]{1,0:T(8,128)(2,1)}, u32[]{:S(2)}, u32[]{:S(2)}) collective-permute-start(bf16[3072,384]{1,0:T(8,128)(2,1)} %convolution_convert_fusion), channel_id=1, source_target_pairs={{0,1},{1,0},{2,3},{3,2},{4,5},{5,4},{6,7},{7,6},{8,9},{9,8},{10,11... | collective-permute-start | bytes 7077896 | tf_op jit(solution)/shard_map/ppermute | solution.py:26
  574.3 22.0 %collective-permute-start.120 = (bf16[768,1536]{1,0:T(8,128)(2,1)S(1)}, bf16[768,1536]{1,0:T(8,128)(2,1)}, u32[]{:S(2)}, u32[]{:S(2)}) collective-permute-start(bf16[768,1536]{1,0:T(8,128)(2,1)S(1)} %convolution_convert_fusion.2), channel_id=1, source_target_pairs={{0,1},{1,0},{2,3},{3,2},{4,5},{5,4},{6,7},{7,6},{8,9},{9,8},{10,11... | collective-permute-start | bytes 7077896 | tf_op jit(solution)/shard_map/ppermute | solution.py:26
  595.7 27.4 %collective-permute-start.135 = (bf16[2,4,192,384]{3,2,1,0:T(8,128)(2,1)}, bf16[2,4,192,384]{3,2,1,0:T(8,128)(2,1)}, u32[]{:S(2)}, u32[]{:S(2)}) collective-permute-start(bf16[2,4,192,384]{3,2,1,0:T(8,128)(2,1)} %dynamic-slice_bitcast_fusion), channel_id=1, source_target_pairs={{0,16},{1,17},{2,18},{3,19},{4,20},{5,21},{6,22},{7,23},{8,24},{9,... | collective-permute-start | bytes 3538952 | tf_op jit(solution)/shard_map/ppermute | solution.py:26
  600.2 28.3 %collective-permute-start.121 = (bf16[2,4,48,1536]{3,2,1,0:T(8,128)(2,1)}, bf16[2,4,48,1536]{3,2,1,0:T(8,128)(2,1)}, u32[]{:S(2)}, u32[]{:S(2)}) collective-permute-start(bf16[2,4,48,1536]{3,2,1,0:T(8,128)(2,1)} %dynamic-slice_bitcast_fusion.2), channel_id=1, source_target_pairs={{0,8},{1,9},{2,10},{3,11},{4,12},{5,13},{6,14},{7,15},{8,0},{9,1},... | collective-permute-start | bytes 3538952 | tf_op jit(solution)/shard_map/ppermute | solution.py:26
  616.1 176.4 %collective-permute-start.112 = (f32[24,384]{1,0:T(8,128)}, f32[24,384]{1,0:T(8,128)}, u32[]{:S(2)}, u32[]{:S(2)}) collective-permute-start(f32[24,384]{1,0:T(8,128)} %get-tuple-element.764), channel_id=1, source_target_pairs={{0,1},{1,0},{2,3},{3,2},{4,5},{5,4},{6,7},{7,6},{8,9},{9,8},{10,11... | collective-permute-start | bytes 110600 | tf_op jit(solution)/shard_map/ppermute | solution.py:26
  632.0 140.5 %collective-permute-start.122 = (bf16[4,48,1536]{2,1,0:T(8,128)(2,1)}, bf16[4,48,1536]{2,1,0:T(8,128)(2,1)}, u32[]{:S(2)}, u32[]{:S(2)}) collective-permute-start(bf16[4,48,1536]{2,1,0:T(8,128)(2,1)} %dynamic-slice_bitcast_fusion.8), channel_id=1, source_target_pairs={{0,16},{1,17},{2,18},{3,19},{4,20},{5,21},{6,22},{7,23},{8,24},{9,... | collective-permute-start | bytes 1769480 | tf_op jit(solution)/shard_map/ppermute | solution.py:26
  641.7 133.3 %collective-permute-start.137 = (bf16[192,384]{1,0:T(8,128)(2,1)}, bf16[192,384]{1,0:T(8,128)(2,1)}, u32[]{:S(2)}, u32[]{:S(2)}) collective-permute-start(bf16[192,384]{1,0:T(8,128)(2,1)} %get-tuple-element.706), channel_id=1, source_target_pairs={{0,2},{1,3},{2,0},{3,1},{4,6},{5,7},{6,4},{7,5},{8,10},{9,11},{10,... | collective-permute-start | bytes 442376 | tf_op jit(solution)/shard_map/ppermute | solution.py:26
  649.5 129.2 %collective-permute-start.138 = (bf16[192,384]{1,0:T(8,128)(2,1)}, bf16[192,384]{1,0:T(8,128)(2,1)}, u32[]{:S(2)}, u32[]{:S(2)}) collective-permute-start(bf16[192,384]{1,0:T(8,128)(2,1)} %get-tuple-element.708), channel_id=1, source_target_pairs={{0,4},{1,5},{2,6},{3,7},{4,0},{5,1},{6,2},{7,3},{8,12},{9,13},{10,... | collective-permute-start | bytes 442376 | tf_op jit(solution)/shard_map/ppermute | solution.py:26
  649.5 129.9 %collective-permute-start.139 = (bf16[192,384]{1,0:T(8,128)(2,1)}, bf16[192,384]{1,0:T(8,128)(2,1)}, u32[]{:S(2)}, u32[]{:S(2)}) collective-permute-start(bf16[192,384]{1,0:T(8,128)(2,1)} %get-tuple-element.707), channel_id=1, source_target_pairs={{0,6},{1,7},{2,4},{3,5},{4,2},{5,3},{6,0},{7,1},{8,14},{9,15},{10,... | collective-permute-start | bytes 442376 | tf_op jit(solution)/shard_map/ppermute | solution.py:26
  772.2 175.9 %reduce-scatter.11.cloned.1.call-start = ((), (), s32[]{:S(2)}) async-start(), calls=%async_computation.7 | async-start | bytes 3538944 | tf_op jit(solution)/shard_map/reduce_scatter | solution.py:487
  798.4 49.0 %collective-permute-start.127 = (bf16[3072,384]{1,0:T(8,128)(2,1)}, bf16[3072,384]{1,0:T(8,128)(2,1)}, u32[]{:S(2)}, u32[]{:S(2)}) collective-permute-start(bf16[3072,384]{1,0:T(8,128)(2,1)} %convolution_convert_fusion.1), channel_id=1, source_target_pairs={{0,1},{1,0},{2,3},{3,2},{4,5},{5,4},{6,7},{7,6},{8,9},{9,8},{10,11... | collective-permute-start | bytes 7077896 | tf_op jit(solution)/shard_map/ppermute | solution.py:26
  800.5 39.5 %collective-permute-start.92 = (bf16[768,1152]{1,0:T(8,128)(2,1)S(1)}, bf16[768,1152]{1,0:T(8,128)(2,1)}, u32[]{:S(2)}, u32[]{:S(2)}) collective-permute-start(bf16[768,1152]{1,0:T(8,128)(2,1)S(1)} %convolution_convert_fusion.4), channel_id=1, source_target_pairs={{0,1},{1,0},{2,3},{3,2},{4,5},{5,4},{6,7},{7,6},{8,9},{9,8},{10,11... | collective-permute-start | bytes 5308424 | tf_op jit(solution)/shard_map/ppermute | solution.py:26
  835.3 33.9 %collective-permute-start.113 = (bf16[768,1536]{1,0:T(8,128)(2,1)}, bf16[768,1536]{1,0:T(8,128)(2,1)}, u32[]{:S(2)}, u32[]{:S(2)}) collective-permute-start(bf16[768,1536]{1,0:T(8,128)(2,1)} %convolution_convert_fusion.3), channel_id=1, source_target_pairs={{0,1},{1,0},{2,3},{3,2},{4,5},{5,4},{6,7},{7,6},{8,9},{9,8},{10,11... | collective-permute-start | bytes 7077896 | tf_op jit(solution)/shard_map/ppermute | solution.py:26
  843.6 22.3 %collective-permute-start.93 = (bf16[2,4,48,1152]{3,2,1,0:T(8,128)(2,1)}, bf16[2,4,48,1152]{3,2,1,0:T(8,128)(2,1)}, u32[]{:S(2)}, u32[]{:S(2)}) collective-permute-start(bf16[2,4,48,1152]{3,2,1,0:T(8,128)(2,1)} %dynamic-slice_bitcast_fusion.4), channel_id=1, source_target_pairs={{0,16},{1,17},{2,18},{3,19},{4,20},{5,21},{6,22},{7,23},{8,24},{9,... | collective-permute-start | bytes 2654216 | tf_op jit(solution)/shard_map/ppermute | solution.py:26
  852.1 49.3 %collective-permute-start.128 = (bf16[2,4,192,384]{3,2,1,0:T(8,128)(2,1)S(1)}, bf16[2,4,192,384]{3,2,1,0:T(8,128)(2,1)S(1)}, u32[]{:S(2)}, u32[]{:S(2)}) collective-permute-start(bf16[2,4,192,384]{3,2,1,0:T(8,128)(2,1)S(1)} %dynamic-slice_bitcast_fusion.1), channel_id=1, source_target_pairs={{0,8},{1,9},{2,10},{3,11},{4,12},{5,13},{6,14},{7,15},{8,0},{9,1},... | collective-permute-start | bytes 3538952 | tf_op jit(solution)/shard_map/ppermute | solution.py:26
  867.4 22.3 %collective-permute-start.94 = (bf16[4,48,1152]{2,1,0:T(8,128)(2,1)S(1)}, bf16[4,48,1152]{2,1,0:T(8,128)(2,1)S(1)}, u32[]{:S(2)}, u32[]{:S(2)}) collective-permute-start(bf16[4,48,1152]{2,1,0:T(8,128)(2,1)S(1)} %dynamic-slice_bitcast_fusion.10), channel_id=1, source_target_pairs={{0,8},{1,9},{2,10},{3,11},{4,12},{5,13},{6,14},{7,15},{8,0},{9,1},... | collective-permute-start | bytes 1327112 | tf_op jit(solution)/shard_map/ppermute | solution.py:26
  872.0 30.5 %collective-permute-start.114 = (bf16[2,4,48,1536]{3,2,1,0:T(8,128)(2,1)S(1)}, bf16[2,4,48,1536]{3,2,1,0:T(8,128)(2,1)S(1)}, u32[]{:S(2)}, u32[]{:S(2)}) collective-permute-start(bf16[2,4,48,1536]{3,2,1,0:T(8,128)(2,1)S(1)} %dynamic-slice_bitcast_fusion.3), channel_id=1, source_target_pairs={{0,16},{1,17},{2,18},{3,19},{4,20},{5,21},{6,22},{7,23},{8,24},{9,... | collective-permute-start | bytes 3538952 | tf_op jit(solution)/shard_map/ppermute | solution.py:26
  903.1 19.1 %collective-permute-start.115 = (bf16[4,48,1536]{2,1,0:T(8,128)(2,1)S(1)}, bf16[4,48,1536]{2,1,0:T(8,128)(2,1)S(1)}, u32[]{:S(2)}, u32[]{:S(2)}) collective-permute-start(bf16[4,48,1536]{2,1,0:T(8,128)(2,1)S(1)} %dynamic-slice_bitcast_fusion.9), channel_id=1, source_target_pairs={{0,8},{1,9},{2,10},{3,11},{4,12},{5,13},{6,14},{7,15},{8,0},{9,1},... | collective-permute-start | bytes 1769480 | tf_op jit(solution)/shard_map/ppermute | solution.py:26
  923.4 22.3 %collective-permute-start.117 = (bf16[48,1536]{1,0:T(8,128)(2,1)S(1)}, bf16[48,1536]{1,0:T(8,128)(2,1)S(1)}, u32[]{:S(2)}, u32[]{:S(2)}) collective-permute-start(bf16[48,1536]{1,0:T(8,128)(2,1)S(1)} %get-tuple-element.711), channel_id=1, source_target_pairs={{0,4},{1,5},{2,6},{3,7},{4,0},{5,1},{6,2},{7,3},{8,12},{9,13},{10,... | collective-permute-start | bytes 442376 | tf_op jit(solution)/shard_map/ppermute | solution.py:26
  925.3 20.4 %collective-permute-start.118 = (bf16[48,1536]{1,0:T(8,128)(2,1)S(1)}, bf16[48,1536]{1,0:T(8,128)(2,1)S(1)}, u32[]{:S(2)}, u32[]{:S(2)}) collective-permute-start(bf16[48,1536]{1,0:T(8,128)(2,1)S(1)} %get-tuple-element.710), channel_id=1, source_target_pairs={{0,6},{1,7},{2,4},{3,5},{4,2},{5,3},{6,0},{7,1},{8,14},{9,15},{10,... | collective-permute-start | bytes 442376 | tf_op jit(solution)/shard_map/ppermute | solution.py:26
  968.5 22.8 %collective-permute-start.86 = (bf16[2,4,48,1152]{3,2,1,0:T(8,128)(2,1)}, bf16[2,4,48,1152]{3,2,1,0:T(8,128)(2,1)}, u32[]{:S(2)}, u32[]{:S(2)}) collective-permute-start(bf16[2,4,48,1152]{3,2,1,0:T(8,128)(2,1)} %dynamic-slice_bitcast_fusion.5), channel_id=1, source_target_pairs={{0,8},{1,9},{2,10},{3,11},{4,12},{5,13},{6,14},{7,15},{8,0},{9,1},... | collective-permute-start | bytes 2654216 | tf_op jit(solution)/shard_map/ppermute | solution.py:26
  970.7 23.9 %collective-permute-start.75 = (f32[8,8,128]{2,1,0:T(8,128)S(1)}, f32[8,8,128]{2,1,0:T(8,128)S(1)}, u32[]{:S(2)}, u32[]{:S(2)}) collective-permute-start(f32[8,8,128]{2,1,0:T(8,128)S(1)} %get-tuple-element.758), channel_id=1, source_target_pairs={{0,8},{1,9},{2,10},{3,11},{4,12},{5,13},{6,14},{7,15},{8,0},{9,1},... | collective-permute-start | bytes 98312 | tf_op jit(solution)/shard_map/ppermute | solution.py:26
  971.0 23.5 %collective-permute-start.76 = (f32[8,8,128]{2,1,0:T(8,128)S(1)}, f32[8,8,128]{2,1,0:T(8,128)S(1)}, u32[]{:S(2)}, u32[]{:S(2)}) collective-permute-start(f32[8,8,128]{2,1,0:T(8,128)S(1)} %get-tuple-element.760), channel_id=1, source_target_pairs={{0,16},{1,17},{2,18},{3,19},{4,20},{5,21},{6,22},{7,23},{8,24},{9,... | collective-permute-start | bytes 98312 | tf_op jit(solution)/shard_map/ppermute | solution.py:26
  971.6 22.9 %collective-permute-start.77 = (f32[8,8,128]{2,1,0:T(8,128)S(1)}, f32[8,8,128]{2,1,0:T(8,128)S(1)}, u32[]{:S(2)}, u32[]{:S(2)}) collective-permute-start(f32[8,8,128]{2,1,0:T(8,128)S(1)} %get-tuple-element.759), channel_id=1, source_target_pairs={{0,24},{1,25},{2,26},{3,27},{4,28},{5,29},{6,30},{7,31},{8,16},{9,... | collective-permute-start | bytes 98312 | tf_op jit(solution)/shard_map/ppermute | solution.py:26
  (276 other events, 3607.1 us)
Sparse Core Ops, SparseCore 0:
  88.8 54.1 all-gather.8
  159.5 36.9 all-gather.10
  312.1 57.4 all-gather.12
  371.7 36.2 all-gather.14
  565.7 45.3 reduce-scatter.4
  613.3 41.3 reduce-scatter.6
  772.3 46.1 reduce-scatter.8
  846.7 38.7 reduce-scatter.10

commit v2 on v1

v2 whole, which is shorter than its diff:
```python
import functools
import math

import jax
import jax.numpy as jnp
from jax import lax
from jax.experimental import pallas as pl
from jax.experimental.pallas import tpu as pltpu
from jax.sharding import PartitionSpec as P

HEAD = 64
LAYERS = 2
DOCS = 8


norm_eps = 1e-05
masked_value = -1e30
gelu_coeff = 0.7978845608028654
cubic_coeff = 0.044715

def swap(value, dp_bits, ctx_bits):
    dp_size, ctx_size = lax.axis_size("dp"), lax.axis_size("ctx")
    pairs = [
        (i, ((i // ctx_size) ^ dp_bits) * ctx_size + ((i % ctx_size) ^ ctx_bits))
        for i in range(dp_size * ctx_size)
    ]
    return lax.ppermute(value, ("dp", "ctx"), pairs)


def place_kernel(dp_size, chips, *refs):
    pieces, whole, held, in_sem, out_sem = refs[: 2 * dp_size], *refs[2 * dp_size :]
    half = held.shape[-1]
    dp_rank, ctx_rank = lax.axis_index("dp"), lax.axis_index("ctx")
    chip, core = ctx_rank // 2, ctx_rank % 2
    arrivals = []
    for n, piece in enumerate(pieces):
        for k in range(chips):
            copy = pltpu.make_async_copy(piece.at[k], held.at[n, k], in_sem.at[n, k])
            copy.start()
            arrivals.append((n, k, copy))
    leaving = []
    for n, k, copy in arrivals:
        copy.wait()
        side, move = n // dp_size, n % dp_size
        row = (dp_rank ^ move) * chips + (chip ^ k)
        column = pl.multiple_of((core ^ side) * half, half)
        out = pltpu.make_async_copy(
            held.at[n, k], whole.at[row, :, pl.ds(column, half)], out_sem.at[n, k]
        )
        out.start()
        leaving.append(out)
    for out in leaving:
        out.wait()


def gather_rows(shard, order):
    dp_size, chips = lax.axis_size("dp"), lax.axis_size("ctx") // 2
    rows, columns = shard.shape
    half = columns // 2
    core = lax.axis_index("ctx") % 2
    kept = lax.dynamic_slice_in_dim(shard, core * half, half, 1)
    given = lax.dynamic_slice_in_dim(shard, (1 - core) * half, half, 1)
    got = swap(given, 0, 1)
    own = jnp.where(core == 0, jnp.concatenate([kept, got]), jnp.concatenate([got, kept]))
    line = jnp.stack([own] + [swap(own, 0, 2 * k) for k in range(1, chips)])
    pieces = {0: line}
    for bit in order:
        for place in list(pieces):
            pieces[place ^ bit] = swap(pieces[place], bit, 0)
    near = [pieces[place] for place in range(dp_size)]
    far = [swap(piece, 0, 1) for piece in near]
    whole = pl.pallas_call(
        functools.partial(place_kernel, dp_size, chips),
        out_shape=jax.ShapeDtypeStruct((dp_size * chips, 2 * rows, columns), shard.dtype),
        in_specs=[pl.BlockSpec(memory_space=pl.ANY)] * (2 * dp_size),
        out_specs=pl.BlockSpec(memory_space=pl.ANY),
        scratch_shapes=[
            pltpu.VMEM((2 * dp_size, chips, 2 * rows, half), shard.dtype),
            pltpu.SemaphoreType.DMA((2 * dp_size, chips)),
            pltpu.SemaphoreType.DMA((2 * dp_size, chips)),
        ],
        cost_estimate=pl.CostEstimate(
            flops=0, transcendentals=0, bytes_accessed=4 * dp_size * chips * rows * columns * 2
        ),
    )(*near, *far)
    return whole.reshape(dp_size * chips * 2 * rows, columns)


def pick(value, place, axis):
    return lax.dynamic_index_in_dim(value, place, axis, keepdims=False)


def reduce_rows(left, right, order, left_dim=0, right_dim=0):
    dp_size, chips = lax.axis_size("dp"), lax.axis_size("ctx") // 2
    dp_rank, ctx_rank = lax.axis_index("dp"), lax.axis_index("ctx")
    chip, core = ctx_rank // 2, ctx_rank % 2
    rows = left.shape[1 - left_dim] // (dp_size * chips * 2)
    columns = right.shape[1 - right_dim]
    half = columns // 2
    own_side = lax.dynamic_slice_in_dim(right, core * half, half, 1 - right_dim)
    far_side = lax.dynamic_slice_in_dim(right, (1 - core) * half, half, 1 - right_dim)
    got = swap(contract(left, far_side, left_dim, right_dim).astype(jnp.bfloat16), 0, 1)
    part = (contract(left, own_side, left_dim, right_dim) + got.astype(jnp.float32)).astype(
        jnp.bfloat16
    )
    bits = [1 << n for n in reversed(range(dp_size.bit_length() - 1))]
    part = part.reshape([2] * len(bits) + [chips, 2 * rows, half])
    for bit in order:
        axis = bits.index(bit)
        bits.remove(bit)
        side = (dp_rank // bit) % 2
        got = swap(pick(part, 1 - side, axis), bit, 0)
        part = (pick(part, side, axis).astype(jnp.float32) + got.astype(jnp.float32)).astype(
            jnp.bfloat16
        )
    total = pick(part, chip, 0).astype(jnp.float32)
    for k in range(1, chips):
        total = total + swap(pick(part, chip ^ k, 0), 0, 2 * k).astype(jnp.float32)
    total = total.reshape(2, rows, half)
    got = swap(pick(total, 1 - core, 0), 0, 1)
    kept = pick(total, core, 0)
    return jnp.where(
        core == 0,
        jnp.concatenate([kept, got], axis=1),
        jnp.concatenate([got, kept], axis=1),
    )


def gather_small(packed):
    dp_size, ctx_size = lax.axis_size("dp"), lax.axis_size("ctx")
    mine = lax.axis_index("dp") * ctx_size + lax.axis_index("ctx")
    held = packed.reshape(1, 8, -1)
    held = jnp.concatenate([held] + [swap(held, 0, k) for k in range(1, ctx_size)])
    bit = 1
    while bit < dp_size:
        held = jnp.concatenate([held, swap(held, bit, 0)])
        bit *= 2
    devices = dp_size * ctx_size
    held = held.reshape(devices, -1)
    source = mine ^ jnp.arange(devices, dtype=jnp.int32)
    chosen = (source[:, None] == jnp.arange(devices, dtype=jnp.int32)[None, :]).astype(held.dtype)
    return jnp.dot(chosen, held, preferred_element_type=jnp.float32).astype(held.dtype)


def reduce_small(terms):
    dp_size, ctx_size = lax.axis_size("dp"), lax.axis_size("ctx")
    dp_rank, ctx_rank = lax.axis_index("dp"), lax.axis_index("ctx")
    width = terms.shape[1]
    part = terms.reshape(dp_size, ctx_size, 8, width // 8)
    total = pick(part, dp_rank, 0)
    for k in range(1, dp_size):
        total = total + swap(pick(part, dp_rank ^ k, 0), k, 0)
    row = pick(total, ctx_rank, 0)
    for k in range(1, ctx_size):
        row = row + swap(pick(total, ctx_rank ^ k, 0), 0, k)
    return row.reshape(width)


def layer_norm(residual, norm_gain, norm_bias):
    row_mean = jnp.mean(residual, axis=-1, keepdims=True)
    centered = residual - row_mean
    variance = jnp.mean(centered * centered, axis=-1, keepdims=True)
    inv_std = lax.rsqrt(variance + norm_eps)
    normed = centered * inv_std
    return (normed * norm_gain + norm_bias, normed, inv_std)


def norm_back(grad_norm, normed, inv_std, norm_gain):
    scaled = grad_norm * norm_gain
    return inv_std * (
        scaled
        - jnp.mean(scaled, axis=-1, keepdims=True)
        - normed * jnp.mean(scaled * normed, axis=-1, keepdims=True)
    )


def gelu_value(values_in):
    inner_arg = gelu_coeff * (values_in + cubic_coeff * values_in * values_in * values_in)
    return 0.5 * values_in * (1.0 + jnp.tanh(inner_arg))


def gelu_slope(values_in):
    tanh_val = jnp.tanh(gelu_coeff * (values_in + cubic_coeff * values_in * values_in * values_in))
    return 0.5 * (1.0 + tanh_val) + 0.5 * values_in * (1.0 - tanh_val * tanh_val) * gelu_coeff * (
        1.0 + 3.0 * cubic_coeff * values_in * values_in
    )


def fetch(pairs):
    copies = [pltpu.make_async_copy(*pair) for pair in pairs]
    for copy in copies:
        copy.start()
    for copy in copies:
        copy.wait()


def contract(left, right, left_dim, right_dim):
    return lax.dot_general(
        left, right, (((left_dim,), (right_dim,)), ((), ())), preferred_element_type=jnp.float32
    )


def allowed_keys(key_chunk, starts, length, own):
    places = lax.broadcasted_iota(jnp.int32, (length, length), 0)
    allowed = places + key_chunk * length >= starts
    if own:
        allowed &= places <= lax.broadcasted_iota(jnp.int32, (length, length), 1)
    return allowed


def mix_kernel(parts, shares, *refs):
    first_ref, starts_ref = refs[:2]
    mine, theirs = refs[2 : 2 + parts], refs[2 + parts]
    out_ref, log_ref, queries, both, total, sems = refs[3 + parts :]
    width, length = out_ref.shape[1:]
    ctx_rank = lax.axis_index("ctx")
    part, share = ctx_rank // shares, ctx_rank % shares
    pairs = []
    for k in range(parts):
        chunk = (part ^ k) * shares
        pairs.append((mine[k].at[pl.ds(0, width)], queries.at[k], sems.at[k, 0]))
        pairs.append(
            (mine[k].at[pl.ds(width, 2 * width)], both.at[chunk + share], sems.at[k, 1])
        )
        for j in range(1, shares):
            pairs.append((theirs.at[j - 1, k], both.at[chunk + (share ^ j)], sems.at[k, 1 + j]))
    fetch(pairs)
    heads = width // HEAD

    def one_chunk(k, carry):
        chunk = (part ^ k) * shares + share
        starts = starts_ref[chunk]
        total[...] = jnp.zeros_like(total)

        def block(key_chunk, state, own):
            allowed = allowed_keys(key_chunk, starts, length, own)
            following = []
            for head in range(heads):
                top, weight = state[head]
                rows = slice(head * HEAD, (head + 1) * HEAD)
                value_rows = slice(width + head * HEAD, width + (head + 1) * HEAD)
                score = contract(both[key_chunk, rows], queries[k, rows], 0, 0)
                score = jnp.where(allowed, score, masked_value)
                new_top = jnp.maximum(top, jnp.max(score, axis=0, keepdims=True))
                prob = jnp.exp(score - new_top)
                shrink = jnp.exp(top - new_top)
                weight = weight * shrink + jnp.sum(prob, axis=0, keepdims=True)
                total[rows] = total[rows] * shrink + contract(
                    both[key_chunk, value_rows], prob.astype(jnp.bfloat16), 1, 0
                )
                following.append((new_top, weight))
            return tuple(following)

        empty = (
            jnp.full((1, length), masked_value, jnp.float32),
            jnp.zeros((1, length), jnp.float32),
        )
        state = lax.fori_loop(
            first_ref[chunk], chunk, lambda at, s: block(at, s, False), (empty,) * heads
        )
        state = block(chunk, state, True)
        for head in range(heads):
            top, weight = state[head]
            rows = slice(head * HEAD, (head + 1) * HEAD)
            out_ref[k, rows] = (total[rows] / weight).astype(out_ref.dtype)
            log_ref[k, head : head + 1] = top + jnp.log(weight)
        return carry

    lax.fori_loop(0, parts, one_chunk, 0)


def mix_back_kernel(parts, shares, *refs):
    first_ref, starts_ref, mixed, log_ref = refs[:4]
    mine, grads, theirs = refs[4 : 4 + parts], refs[4 + parts : 4 + 2 * parts], refs[4 + 2 * parts]
    out_ref, own_ref, far_ref, queries, both, slopes, totals, sems = refs[5 + 2 * parts :]
    width, length = out_ref.shape[1:]
    ctx_rank = lax.axis_index("ctx")
    part, share = ctx_rank // shares, ctx_rank % shares
    pairs = []
    for k in range(parts):
        chunk = (part ^ k) * shares
        pairs.append((mine[k].at[pl.ds(0, width)], queries.at[k], sems.at[k, 0]))
        pairs.append((grads[k], slopes.at[k], sems.at[k, 1]))
        pairs.append(
            (mine[k].at[pl.ds(width, 2 * width)], both.at[chunk + share], sems.at[k, 2])
        )
        for j in range(1, shares):
            pairs.append((theirs.at[j - 1, k], both.at[chunk + (share ^ j)], sems.at[k, 2 + j]))
    fetch(pairs)
    totals[...] = jnp.zeros_like(totals)
    heads = width // HEAD

    def one_chunk(k, carry):
        chunk = (part ^ k) * shares + share
        starts = starts_ref[chunk]
        deltas, logs = [], []
        for head in range(heads):
            rows = slice(head * HEAD, (head + 1) * HEAD)
            deltas.append(
                jnp.sum(
                    slopes[k, rows].astype(jnp.float32) * mixed[k, rows].astype(jnp.float32),
                    axis=0,
                    keepdims=True,
                )
            )
            logs.append(log_ref[k, head : head + 1])

        def block(key_chunk, state, own):
            allowed = allowed_keys(key_chunk, starts, length, own)
            following = []
            for head in range(heads):
                rows = slice(head * HEAD, (head + 1) * HEAD)
                value_rows = slice(width + head * HEAD, width + (head + 1) * HEAD)
                keys, values = both[key_chunk, rows], both[key_chunk, value_rows]
                asked, slope = queries[k, rows], slopes[k, rows]
                score = contract(keys, asked, 0, 0)
                prob = jnp.exp(jnp.where(allowed, score - logs[head], masked_value))
                grad_prob = contract(values, slope, 0, 0)
                grad_score = (prob * (grad_prob - deltas[head])).astype(jnp.bfloat16)
                totals[key_chunk, value_rows] += contract(slope, prob.astype(jnp.bfloat16), 1, 1)
                totals[key_chunk, rows] += contract(asked, grad_score, 1, 1)
                following.append(state[head] + contract(keys, grad_score, 1, 0))
            return tuple(following)

        zero = jnp.zeros((HEAD, length), jnp.float32)
        state = lax.fori_loop(
            first_ref[chunk], chunk, lambda at, s: block(at, s, False), (zero,) * heads
        )
        state = block(chunk, state, True)
        for head in range(heads):
            rows = slice(head * HEAD, (head + 1) * HEAD)
            out_ref[k, rows] = (state[head] * HEAD ** (-0.5)).astype(out_ref.dtype)
        return carry

    lax.fori_loop(0, parts, one_chunk, 0)
    for k in range(parts):
        chunk = (part ^ k) * shares
        own_ref[k] = totals[chunk + share]
        for j in range(1, shares):
            far_ref[j - 1, k] = totals[chunk + (share ^ j)].astype(far_ref.dtype)


def spread(grouped, parts, shares):
    part = lax.axis_index("ctx") // shares
    return [
        pick(grouped, part ^ k, 0) if k == 0 else swap(pick(grouped, part ^ k, 0), 0, shares * k)
        for k in range(parts)
    ]


def collect(pieces, parts, shares):
    part = lax.axis_index("ctx") // shares
    held = jnp.stack([p if k == 0 else swap(p, 0, shares * k) for k, p in enumerate(pieces)])
    return jnp.concatenate([pick(held, part ^ j, 0) for j in range(parts)])


def attend(grouped, starts, first, parts, shares):
    width, length = grouped.shape[1] // 3, grouped.shape[2]
    mine = spread(grouped, parts, shares)
    joint = jnp.stack([piece[width:] for piece in mine])
    theirs = jnp.stack([swap(joint, 0, j) for j in range(1, shares)])
    mixed, logs = pl.pallas_call(
        functools.partial(mix_kernel, parts, shares),
        out_shape=(
            jax.ShapeDtypeStruct((parts, width, length), jnp.bfloat16),
            jax.ShapeDtypeStruct((parts, 8, length), jnp.float32),
        ),
        in_specs=[
            pl.BlockSpec(memory_space=pltpu.SMEM),
            pl.BlockSpec(memory_space=pltpu.VMEM),
        ]
        + [pl.BlockSpec(memory_space=pl.ANY)] * (parts + 1),
        out_specs=(pl.BlockSpec(memory_space=pltpu.VMEM),) * 2,
        scratch_shapes=[
            pltpu.VMEM((parts, width, length), jnp.bfloat16),
            pltpu.VMEM((parts * shares, 2 * width, length), jnp.bfloat16),
            pltpu.VMEM((width, length), jnp.float32),
            pltpu.SemaphoreType.DMA((parts, 1 + shares)),
        ],
        cost_estimate=pl.CostEstimate(
            flops=2 * parts * parts * shares * length * length * width * 2,
            transcendentals=0,
            bytes_accessed=4 * parts * width * length * 2,
        ),
    )(first, starts, *mine, theirs)
    return mixed, logs, mine, theirs


def attend_back(grouped_grads, kept, starts, first, parts, shares):
    mixed, logs, mine, theirs = kept
    width, length = mixed.shape[1:]
    grads = spread(grouped_grads, parts, shares)
    grad_queries, own, far = pl.pallas_call(
        functools.partial(mix_back_kernel, parts, shares),
        out_shape=(
            jax.ShapeDtypeStruct((parts, width, length), jnp.bfloat16),
            jax.ShapeDtypeStruct((parts, 2 * width, length), jnp.float32),
            jax.ShapeDtypeStruct((shares - 1, parts, 2 * width, length), jnp.bfloat16),
        ),
        in_specs=[
            pl.BlockSpec(memory_space=pltpu.SMEM),
            pl.BlockSpec(memory_space=pltpu.VMEM),
            pl.BlockSpec(memory_space=pltpu.VMEM),
            pl.BlockSpec(memory_space=pltpu.VMEM),
        ]
        + [pl.BlockSpec(memory_space=pl.ANY)] * (2 * parts + 1),
        out_specs=(pl.BlockSpec(memory_space=pltpu.VMEM),) * 3,
        scratch_shapes=[
            pltpu.VMEM((parts, width, length), jnp.bfloat16),
            pltpu.VMEM((parts * shares, 2 * width, length), jnp.bfloat16),
            pltpu.VMEM((parts, width, length), jnp.bfloat16),
            pltpu.VMEM((parts * shares, 2 * width, length), jnp.float32),
            pltpu.SemaphoreType.DMA((parts, 2 + shares)),
        ],
        cost_estimate=pl.CostEstimate(
            flops=5 * parts * parts * shares * length * length * width * 2,
            transcendentals=0,
            bytes_accessed=8 * parts * width * length * 2,
        ),
    )(first, starts, mixed, logs, *mine, *grads, theirs)
    for j in range(1, shares):
        own = own + swap(far[j - 1], 0, j).astype(jnp.float32)
    joint = jnp.concatenate([grad_queries, own.astype(jnp.bfloat16)], axis=1)
    return collect([joint[k] for k in range(parts)], parts, shares)


def forward_layer(residual, layer_params, plan):
    (
        norm1_gain,
        norm1_bias,
        qkv_weight,
        qkv_bias,
        qkv_scale,
        out_weight,
        out_bias,
        norm2_gain,
        norm2_bias,
        fc_weight,
        fc_bias,
        proj_weight,
        proj_bias,
    ) = layer_params
    starts, first, parts, shares = plan
    normed_in, normed1, inv_std1 = layer_norm(residual, norm1_gain, norm1_bias)
    attn_in = normed_in.astype(jnp.bfloat16)
    projected = (contract(qkv_weight, attn_in, 0, 1) + qkv_bias[:, None]) * qkv_scale[:, None]
    grouped = projected.astype(jnp.bfloat16).reshape(parts, -1, residual.shape[0])
    kept = attend(grouped, starts, first, parts, shares)
    mixed_columns = collect([kept[0][k] for k in range(parts)], parts, shares)
    middle = residual + contract(mixed_columns, out_weight, 0, 0) + out_bias
    normed_mid, normed2, inv_std2 = layer_norm(middle, norm2_gain, norm2_bias)
    ffn_in = normed_mid.astype(jnp.bfloat16)
    pre_act = jnp.dot(ffn_in, fc_weight, preferred_element_type=jnp.float32) + fc_bias
    hidden = gelu_value(pre_act).astype(jnp.bfloat16)
    result = middle + jnp.dot(hidden, proj_weight, preferred_element_type=jnp.float32) + proj_bias
    return (
        result,
        (
            normed1,
            inv_std1,
            attn_in,
            kept,
            mixed_columns,
            normed2,
            inv_std2,
            ffn_in,
            pre_act,
            hidden,
        ),
    )


def backward_layer(grad_residual, saved_rows, layer_params, plan, orders):
    (
        normed1,
        inv_std1,
        attn_in,
        kept,
        mixed_columns,
        normed2,
        inv_std2,
        ffn_in,
        pre_act,
        hidden,
    ) = saved_rows
    (
        norm1_gain,
        norm1_bias,
        qkv_weight,
        qkv_bias,
        qkv_scale,
        out_weight,
        out_bias,
        norm2_gain,
        norm2_bias,
        fc_weight,
        fc_bias,
        proj_weight,
        proj_bias,
    ) = layer_params
    starts, first, parts, shares = plan
    grad_narrow = grad_residual.astype(jnp.bfloat16)
    grad_proj_w = reduce_rows(hidden, grad_narrow, orders[2])
    grad_proj_b = jnp.sum(grad_residual, axis=0)
    grad_hidden = contract(grad_narrow, proj_weight, 1, 1)
    grad_pre = grad_hidden * gelu_slope(pre_act)
    pre_narrow = grad_pre.astype(jnp.bfloat16)
    grad_fc_w = reduce_rows(ffn_in, pre_narrow, orders[1])
    grad_fc_b = jnp.sum(grad_pre, axis=0)
    grad_norm2 = contract(pre_narrow, fc_weight, 1, 1)
    grad_gain2 = jnp.sum(grad_norm2 * normed2, axis=0)
    grad_bias2 = jnp.sum(grad_norm2, axis=0)
    grad_middle = grad_residual + norm_back(grad_norm2, normed2, inv_std2, norm2_gain)
    middle_narrow = grad_middle.astype(jnp.bfloat16)
    grad_out_w = reduce_rows(mixed_columns, middle_narrow, orders[1], left_dim=1)
    grad_out_b = jnp.sum(grad_middle, axis=0)
    grad_mixed = contract(out_weight, middle_narrow, 1, 1).astype(jnp.bfloat16)
    grad_mixed = grad_mixed.reshape(parts, -1, grad_mixed.shape[1])
    grad_qkv = attend_back(grad_mixed, kept, starts, first, parts, shares)
    grad_qkv_w = reduce_rows(attn_in, grad_qkv, orders[0], right_dim=1)
    grad_qkv_b = jnp.sum(grad_qkv.astype(jnp.float32), axis=1).reshape(parts, 3, -1)
    grad_norm1 = contract(grad_qkv, qkv_weight, 0, 1)
    grad_gain1 = jnp.sum(grad_norm1 * normed1, axis=0)
    grad_bias1 = jnp.sum(grad_norm1, axis=0)
    grad_before = grad_middle + norm_back(grad_norm1, normed1, inv_std1, norm1_gain)
    return (
        grad_before,
        (
            grad_gain1,
            grad_bias1,
            by_kind(grad_qkv_w, parts),
            grad_qkv_b[:, 0].reshape(-1),
            grad_qkv_b[:, 2].reshape(-1),
            grad_out_w,
            grad_out_b,
            grad_gain2,
            grad_bias2,
            grad_fc_w,
            grad_fc_b,
            grad_proj_w,
            grad_proj_b,
        ),
    )


def by_part(columns, parts):
    rows = columns.shape[0]
    return jnp.swapaxes(columns.reshape(rows, 3, parts, -1), 1, 2).reshape(rows, -1)


def by_kind(columns, parts):
    rows = columns.shape[0]
    return jnp.swapaxes(columns.reshape(rows, parts, 3, -1), 1, 2).reshape(rows, -1)


def shards(
    block_input,
    doc_ids,
    out_grad,
    ln1_gain,
    ln1_bias,
    w_qkv,
    b_query,
    b_value,
    w_out,
    b_out,
    ln2_gain,
    ln2_bias,
    w_fc,
    b_fc,
    w_proj,
    b_proj,
):
    seq_count, local_len, model_width = block_input.shape
    row_count = seq_count * local_len
    dp_size, ctx_size = lax.axis_size("dp"), lax.axis_size("ctx")
    devices = dp_size * ctx_size
    parts = math.gcd(model_width // HEAD, ctx_size)
    shares = ctx_size // parts
    rising = [1 << n for n in range(dp_size.bit_length() - 1)]
    falling = rising[::-1]
    narrow_list = (ln1_gain, ln1_bias, b_query, b_value, b_out, ln2_gain, ln2_bias, b_proj)
    narrow_count = LAYERS * len(narrow_list)
    slot = narrow_list[0].shape[1]
    fc_slot = b_fc.shape[1]
    used = narrow_count * slot + LAYERS * fc_slot
    packed_size = -(-(used + row_count) // 1024) * 1024
    packed = jnp.concatenate(
        [
            jnp.stack(narrow_list, 1).reshape(-1),
            b_fc.reshape(-1),
            doc_ids.reshape(-1).astype(jnp.bfloat16),
            jnp.zeros((packed_size - used - row_count,), jnp.bfloat16),
        ]
    )
    small = gather_small(packed)
    narrow_all = (
        jnp.transpose(
            small[:, : narrow_count * slot].reshape(devices, narrow_count, slot), (1, 0, 2)
        )
        .reshape(LAYERS, len(narrow_list), devices * slot)
        .astype(jnp.float32)
    )
    fc_all = (
        jnp.transpose(
            small[:, narrow_count * slot : used].reshape(devices, LAYERS, fc_slot), (1, 0, 2)
        )
        .reshape(LAYERS, devices * fc_slot)
        .astype(jnp.float32)
    )
    ids = pick(
        small[:, used : used + row_count].reshape(dp_size, ctx_size, row_count),
        lax.axis_index("dp"),
        0,
    )
    ids = lax.optimization_barrier(ids.astype(jnp.int32))
    starts = jnp.zeros((ctx_size, row_count), jnp.int32)
    for number in range(DOCS):
        before = jnp.sum((ids < number).astype(jnp.int32))
        starts = jnp.where(ids == number, before, starts)
    first = starts[:, 0] // row_count
    plan = (starts.reshape(ctx_size, 1, row_count), first, parts, shares)
    qkv_scale = jnp.tile(
        jnp.concatenate(
            [
                jnp.full((model_width // parts,), HEAD ** (-0.5), jnp.float32),
                jnp.ones((2 * model_width // parts,), jnp.float32),
            ]
        ),
        parts,
    )

    residual = block_input.reshape(row_count, model_width).astype(jnp.float32)
    kept_params = []
    saved_list = []
    for layer_idx in range(LAYERS):
        ways = (rising, falling) if layer_idx % 2 == 0 else (falling, rising)
        joined = gather_rows(
            jnp.concatenate([by_part(w_qkv[layer_idx], parts), w_out[layer_idx]], axis=1), ways[0]
        )
        fc_weight = gather_rows(w_fc[layer_idx], ways[1])
        proj_weight = gather_rows(w_proj[layer_idx], ways[0])
        narrow = narrow_all[layer_idx]
        qkv_bias = by_part(
            jnp.concatenate([narrow[2], jnp.zeros_like(narrow[2]), narrow[3]])[None], parts
        )[0]
        layer_params = (
            narrow[0],
            narrow[1],
            joined[:, : 3 * model_width],
            qkv_bias,
            qkv_scale,
            joined[:, 3 * model_width :],
            narrow[4],
            narrow[5],
            narrow[6],
            fc_weight,
            fc_all[layer_idx],
            proj_weight,
            narrow[7],
        )
        residual, saved_rows = forward_layer(residual, layer_params, plan)
        kept_params.append(layer_params)
        saved_list.append(saved_rows)
    output_rows = residual.astype(jnp.bfloat16).reshape(seq_count, local_len, model_width)
    grad_residual = out_grad.reshape(row_count, model_width).astype(jnp.float32)
    reduced = [None] * LAYERS
    for layer_idx in reversed(range(LAYERS)):
        orders = (rising, falling, rising) if layer_idx % 2 == 0 else (falling, rising, falling)
        grad_residual, reduced[layer_idx] = backward_layer(
            grad_residual, saved_list[layer_idx], kept_params[layer_idx], plan, orders
        )
    grad_rows = grad_residual.astype(jnp.bfloat16).reshape(seq_count, local_len, model_width)
    term_size = -(-used // 1024) * 1024
    narrow_members = (0, 1, 3, 4, 6, 7, 8, 12)
    narrow_terms = jnp.stack([grads[member] for grads in reduced for member in narrow_members])
    fc_terms = jnp.stack([grads[10] for grads in reduced])
    terms = jnp.concatenate(
        [
            jnp.transpose(narrow_terms.reshape(narrow_count, devices, slot), (1, 0, 2)).reshape(
                devices, -1
            ),
            jnp.transpose(fc_terms.reshape(LAYERS, devices, fc_slot), (1, 0, 2)).reshape(
                devices, -1
            ),
            jnp.zeros((devices, term_size - used), jnp.float32),
        ],
        axis=1,
    )
    sums = reduce_small(terms)
    narrow_sums = sums[: narrow_count * slot].reshape(LAYERS, len(narrow_list), slot)
    fc_sums = sums[narrow_count * slot : used].reshape(LAYERS, fc_slot)
    stacked = []
    for member in range(13):
        if member in narrow_members:
            stacked.append(narrow_sums[:, narrow_members.index(member)])
        elif member == 10:
            stacked.append(fc_sums)
        else:
            stacked.append(jnp.stack([grads[member] for grads in reduced]))
    return (output_rows, grad_rows, *stacked)


def solution(mesh):
    return jax.shard_map(
        shards,
        mesh=mesh,
        in_specs=(
            P("dp", "ctx", None),
            P("dp", "ctx"),
            P("dp", "ctx", None),
            P(None, ("dp", "ctx")),
            P(None, ("dp", "ctx")),
            P(None, ("dp", "ctx"), None),
            P(None, ("dp", "ctx")),
            P(None, ("dp", "ctx")),
            P(None, ("dp", "ctx"), None),
            P(None, ("dp", "ctx")),
            P(None, ("dp", "ctx")),
            P(None, ("dp", "ctx")),
            P(None, ("dp", "ctx"), None),
            P(None, ("dp", "ctx")),
            P(None, ("dp", "ctx"), None),
            P(None, ("dp", "ctx")),
        ),
        out_specs=(
            P("dp", "ctx", None),
            P("dp", "ctx", None),
            P(None, ("dp", "ctx")),
            P(None, ("dp", "ctx")),
            P(None, ("dp", "ctx"), None),
            P(None, ("dp", "ctx")),
            P(None, ("dp", "ctx")),
            P(None, ("dp", "ctx"), None),
            P(None, ("dp", "ctx")),
            P(None, ("dp", "ctx")),
            P(None, ("dp", "ctx")),
            P(None, ("dp", "ctx"), None),
            P(None, ("dp", "ctx")),
            P(None, ("dp", "ctx"), None),
            P(None, ("dp", "ctx")),
        ),
        check_vma=False,
    )
```

time: 1040 us -> 788 us (0.76)
  matrix products: 274 us -> 84.8 us
  Pallas kernels: 29.8 us -> 96 us
  waiting for transfers between devices: 319 us -> 273 us
  local copies, waits for them, and re-layouts: 129 us -> 91.9 us
  other arithmetic: 79.2 us -> 54.5 us
  blocking collectives: 17.7 us -> 0 us
  between operations: 18.1 us -> 3.83 us
    dot_general x74 -> x30, matrix products: 265 us -> 79.8 us  [the longest x28 76.8 us: contract(): lax.dot_general(left, right, (((left_dim,), (right_dim,)), ((), ())), pre...]
    pallas_call x0 -> x4, Pallas kernels: none -> 65.9 us  [the longest x2 34.6 us: attend_back(): pl.pallas_call(functools.partial(mix_back_kernel, parts, shares), out_sha...]
    ppermute x141 -> x169, waiting for transfers between devices: 316 us -> 273 us  [swap(): return lax.ppermute(value, ('dp', 'ctx'), pairs)]
    dynamic_slice x40 -> x0, local copies, waits for them, and re-layouts: 30.7 us -> none  [the longest x16 19 us: block_terms(): lax.dynamic_slice_in_dim(value_all, offset, key_block, 1)]
    reduce_sum x8 -> x3, other arithmetic: 31.5 us -> 2.7 us  [the longest x2 1.96 us: backward_layer(): jnp.sum(grad_qkv.astype(jnp.float32), axis=1).reshape(parts, 3, -1)]
    all_gather x4 -> x0, local copies, waits for them, and re-layouts: 19.1 us -> none  [the longest x2 9.66 us: attend_fwd(): key_piece = lax.all_gather(as_seqs(keys), 'ctx', axis=1, tiled=True)]
    all_gather x1 -> x0, blocking collectives: 17.7 us -> none  [shards(): all_ids = lax.all_gather(doc_ids, 'ctx', axis=1, tiled=True)]
    another operation x17, local copies, waits for them, and re-layouts: 8.81 us -> 22.5 us  [shards(): jnp.stack([grads[member] for grads in reduced for member in narrow_members])]
  transfers between devices with their start and end apart: 149 -> 169, of which waited for: 47 -> 52; matrix products, arithmetic and copies ran while one was open for 28% -> 26% of each run, Pallas kernels for 2% -> 12%
where the time goes in v2:
time: 788 us; the launch traced here: 777 us
  waiting for transfers between devices  273 us (35%)
  starting transfers between devices  173 us (22%)
  Pallas kernels  96 us (12%)
  local copies, waits for them, and re-layouts  91.9 us (12%)
  matrix products  84.8 us (11%)
  other arithmetic  54.5 us (7%)
    ppermute x169, waiting for transfers between devices, swap(): return lax.ppermute(value, ('dp', 'ctx'), pairs)  273 us
    ppermute x169, starting transfers between devices, swap(): return lax.ppermute(value, ('dp', 'ctx'), pairs)  173 us
    dot_general x28, matrix products, contract(): lax.dot_general(left, right, (((left_dim,), (right_dim,)), ((), ())), pre...  76.8 us
    pallas_call x2, Pallas kernels, attend_back(): pl.pallas_call(functools.partial(mix_back_kernel, parts, shares), out_sha...  34.6 us
    pallas_call x2, Pallas kernels, attend(): pl.pallas_call(functools.partial(mix_kernel, parts, shares), out_shape=(j...  31.3 us
    pallas_call x6, Pallas kernels, gather_rows(): pl.pallas_call(functools.partial(place_kernel, dp_size, chips), out_shape...  30.1 us
    unnamed x347, local copies, waits for them, and re-layouts  23.7 us
    another operation x17, local copies, waits for them, and re-layouts, shards(): jnp.stack([grads[member] for grads in reduced for member in narrow_members])  22.5 us
  transfers between devices with their start and end apart: 169, of which 52 were waited for; matrix products, arithmetic and copies ran while one was open for 26% of the time, Pallas kernels for 12%

profile of v2, /device:TPU:0, one launch (start us, length us, event | category | flops | bytes accessed | tf_op | source)
XLA Modules:
  0.0 777.0 jit_solution(17398049982633132471)
XLA Ops:
  19.8 3.6 collective-permute-start.5
  25.2 3.0 collective-permute-done.6
  39.5 3.8 collective-permute-start.10
  43.3 4.1 collective-permute-done.12
  47.4 3.3 collective-permute-done.11
  56.6 10.0 %collective-permute-done.13.refs_1_ = bf16[4,48,1536]{2,1,0:T(8,128)(2,1)S(1)} collective-permute-done((bf16[4,48,1536]{2,1,0:T(8,128)(2,1)S(1)}, bf16[4,48,1536]{2,1,0:T(8,128)(2,1)S(1)}, u32[]{:S(2)}, u32[]{:S(2)}) %collective-permute-start.13) | collective-permute-done | bytes 589856 | tf_op jit(solution)/shard_map/ppermute | solution.py:27
  72.7 7.1 collective-permute-done.40
  79.8 4.3 collective-permute-start.28
  84.1 8.3 %collective-permute-done.29 = bf16[48,1536]{1,0:T(8,128)(2,1)S(1)} collective-permute-done((bf16[48,1536]{1,0:T(8,128)(2,1)S(1)}, bf16[48,1536]{1,0:T(8,128)(2,1)S(1)}, u32[]{:S(2)}, u32[]{:S(2)}) %collective-permute-start.29) | collective-permute-done | bytes 147488 | tf_op jit(solution)/shard_map/ppermute | solution.py:27
  94.2 7.5 collective-permute-done.51
  101.9 5.6 collective-permute-done.50
  114.4 5.1 shard_map.271
  124.2 3.7 fusion.3
  132.4 5.2 select_select_fusion
  144.9 6.0 collective-permute-done.53.refs_1_
  153.1 5.0 collective-permute-done.21.refs_4_.refs_6_
  161.5 9.3 %collective-permute-done.44.refs_3_ = bf16[4,192,384]{2,1,0:T(8,128)(2,1)} collective-permute-done((bf16[4,192,384]{2,1,0:T(8,128)(2,1)S(1)}, bf16[4,192,384]{2,1,0:T(8,128)(2,1)}, u32[]{:S(2)}, u32[]{:S(2)}) %collective-permute-start.44) | collective-permute-done | bytes 589856 | tf_op jit(solution)/shard_map/ppermute | solution.py:27
  177.6 9.4 %collective-permute-done.55.refs_3_ = bf16[4,48,1536]{2,1,0:T(8,128)(2,1)S(1)} collective-permute-done((bf16[4,48,1536]{2,1,0:T(8,128)(2,1)S(1)}, bf16[4,48,1536]{2,1,0:T(8,128)(2,1)S(1)}, u32[]{:S(2)}, u32[]{:S(2)}) %collective-permute-start.55) | collective-permute-done | bytes 589856 | tf_op jit(solution)/shard_map/ppermute | solution.py:27
  189.2 15.6 %shard_map.272 = (bf16[4,192,256]{2,1,0:T(8,128)(2,1)}, f32[4,8,256]{2,1,0:T(8,128)}) custom-call(s32[8]{0:T(128)} %and_select_fusion.refs_0_, s32[8,1,256]{2,1,0:T(1,128)} %reshape.1054.refs_1_, bf16[576,256]{1,0:T(8,128)(2,1)} %get-tuple-element.118.refs_2_.refs_4_, bf16[576,256]{1,0:T(8,128)(2,1)} %copy-done.73, bf16[576,256]{1,0:T(8,128)(2,1)} %copy-done.74, ...), custom_call_target="tpu_custom_call" | custom-call | flops 1610612736 | bytes 1572864 | tf_op jit(solution)/shard_map/pallas_call | solution.py:362
  211.5 5.2 shard_map.274
  216.7 5.0 shard_map.273
  223.9 5.0 shard_map.275
  231.2 4.1 collective-permute-start.82
  250.4 6.3 collective-permute-done.62.refs_5_.refs_7_
  256.7 7.9 %collective-permute-done.60.refs_3_.refs_5_ = bf16[576,256]{1,0:T(8,128)(2,1)S(1)} collective-permute-done((bf16[576,256]{1,0:T(8,128)(2,1)S(1)}, bf16[576,256]{1,0:T(8,128)(2,1)S(1)}, u32[]{:S(2)}, u32[]{:S(2)}) %collective-permute-start.60) | collective-permute-done | bytes 294944 | tf_op jit(solution)/shard_map/ppermute | solution.py:27
  265.0 8.1 %collective-permute-done.61.refs_4_.refs_6_ = bf16[576,256]{1,0:T(8,128)(2,1)S(1)} collective-permute-done((bf16[576,256]{1,0:T(8,128)(2,1)S(1)}, bf16[576,256]{1,0:T(8,128)(2,1)S(1)}, u32[]{:S(2)}, u32[]{:S(2)}) %collective-permute-start.61) | collective-permute-done | bytes 294944 | tf_op jit(solution)/shard_map/ppermute | solution.py:27
  275.0 5.9 collective-permute-done.71.refs_1_
  280.9 7.3 collective-permute-done.72.refs_2_
  288.6 4.1 collective-permute-done.84.refs_3_
  293.2 9.6 %collective-permute-done.73.refs_3_ = bf16[4,48,1536]{2,1,0:T(8,128)(2,1)S(1)} collective-permute-done((bf16[4,48,1536]{2,1,0:T(8,128)(2,1)}, bf16[4,48,1536]{2,1,0:T(8,128)(2,1)S(1)}, u32[]{:S(2)}, u32[]{:S(2)}) %collective-permute-start.73) | collective-permute-done | bytes 589856 | tf_op jit(solution)/shard_map/ppermute | solution.py:27
  303.7 15.7 %shard_map.276 = (bf16[4,192,256]{2,1,0:T(8,128)(2,1)}, f32[4,8,256]{2,1,0:T(8,128)}) custom-call(s32[8]{0:T(128)} %and_select_fusion.refs_0_, s32[8,1,256]{2,1,0:T(1,128)} %reshape.1054.refs_1_, bf16[576,256]{1,0:T(8,128)(2,1)} %get-tuple-element.114.refs_2_.refs_4_, bf16[576,256]{1,0:T(8,128)(2,1)} %copy-done.76, bf16[576,256]{1,0:T(8,128)(2,1)} %copy-done.77, ...), custom_call_target="tpu_custom_call" | custom-call | flops 1610612736 | bytes 1572864 | tf_op jit(solution)/shard_map/pallas_call | solution.py:362
  325.7 4.9 shard_map.278
  330.7 4.9 shard_map.277
  340.4 3.5 fusion.202
  361.9 17.2 %shard_map.279 = (bf16[4,192,256]{2,1,0:T(8,128)(2,1)}, f32[4,384,256]{2,1,0:T(8,128)}, bf16[1,4,384,256]{3,2,1,0:T(8,128)(2,1)}) custom-call(s32[8]{0:T(128)} %and_select_fusion.refs_0_, s32[8,1,256]{2,1,0:T(1,128)} %reshape.1054.refs_1_, bf16[4,192,256]{2,1,0:T(8,128)(2,1)} %get-tuple-element.26.refs_2_, f32[4,8,256]{2,1,0:T(8,128)} %get-tuple-element.27.refs_3_, ...), custom_call_target="tpu_custom_call" | custom-call | flops 4026531840 | bytes 3145728 | tf_op jit(solution)/shard_map/pallas_call | solution.py:393
  379.1 5.4 collective-permute-start.92
  386.4 4.8 convolution_convert_fusion
  391.2 4.1 collective-permute-done.135
  395.8 4.8 collective-permute-done.136
  410.6 7.1 collective-permute-done.138
  429.6 3.1 collective-permute-done.94
  435.2 4.4 multiply_reduce_fusion.1
  441.6 3.5 fusion.201
  451.5 2.9 convolution_convert_fusion.1
  465.4 17.4 %shard_map.280 = (bf16[4,192,256]{2,1,0:T(8,128)(2,1)}, f32[4,384,256]{2,1,0:T(8,128)}, bf16[1,4,384,256]{3,2,1,0:T(8,128)(2,1)}) custom-call(s32[8]{0:T(128)} %and_select_fusion.refs_0_, s32[8,1,256]{2,1,0:T(1,128)} %reshape.1054.refs_1_, bf16[4,192,256]{2,1,0:T(8,128)(2,1)} %get-tuple-element.25.refs_2_, f32[4,8,256]{2,1,0:T(8,128)} %get-tuple-element.31.refs_3_, ...), custom_call_target="tpu_custom_call" | custom-call | flops 4026531840 | bytes 3145728 | tf_op jit(solution)/shard_map/pallas_call | solution.py:393
  490.5 3.3 convolution_convert_fusion.4
  493.8 3.9 collective-permute-done.128
  511.7 9.6 %collective-permute-done.131 = bf16[48,384]{1,0:T(8,128)(2,1)S(1)} collective-permute-done((bf16[48,384]{1,0:T(8,128)(2,1)S(1)}, bf16[48,384]{1,0:T(8,128)(2,1)S(1)}, u32[]{:S(2)}, u32[]{:S(2)}) %collective-permute-start.131) | collective-permute-done | bytes 36896 | tf_op jit(solution)/shard_map/ppermute | solution.py:27
  540.4 5.2 fusion.57
  573.1 2.9 add_convert_fusion.2
  576.1 4.5 add_convert_fusion
  600.9 19.0 %collective-permute-done.149 = bf16[2,4,48,1536]{3,2,1,0:T(8,128)(2,1)} collective-permute-done((bf16[2,4,48,1536]{3,2,1,0:T(8,128)(2,1)}, bf16[2,4,48,1536]{3,2,1,0:T(8,128)(2,1)}, u32[]{:S(2)}, u32[]{:S(2)}) %collective-permute-start.149) | collective-permute-done | bytes 1179680 | tf_op jit(solution)/shard_map/ppermute | solution.py:27
  621.8 5.1 collective-permute-done.163
  636.1 3.6 add_convert_fusion.1
  641.0 4.9 collective-permute-done.121
  647.6 11.0 %collective-permute-done.150 = bf16[4,48,1536]{2,1,0:T(8,128)(2,1)S(1)} collective-permute-done((bf16[4,48,1536]{2,1,0:T(8,128)(2,1)S(1)}, bf16[4,48,1536]{2,1,0:T(8,128)(2,1)S(1)}, u32[]{:S(2)}, u32[]{:S(2)}) %collective-permute-start.150) | collective-permute-done | bytes 589856 | tf_op jit(solution)/shard_map/ppermute | solution.py:27
  668.9 8.8 %collective-permute-done.152 = bf16[48,1536]{1,0:T(8,128)(2,1)S(1)} collective-permute-done((bf16[48,1536]{1,0:T(8,128)(2,1)S(1)}, bf16[48,1536]{1,0:T(8,128)(2,1)S(1)}, u32[]{:S(2)}, u32[]{:S(2)}) %collective-permute-start.152) | collective-permute-done | bytes 147488 | tf_op jit(solution)/shard_map/ppermute | solution.py:27
  681.1 5.3 collective-permute-done.166
  711.9 16.7 %collective-permute-done.114 = bf16[2,4,48,1152]{3,2,1,0:T(8,128)(2,1)} collective-permute-done((bf16[2,4,48,1152]{3,2,1,0:T(8,128)(2,1)}, bf16[2,4,48,1152]{3,2,1,0:T(8,128)(2,1)}, u32[]{:S(2)}, u32[]{:S(2)}) %collective-permute-start.114) | collective-permute-done | bytes 884768 | tf_op jit(solution)/shard_map/ppermute | solution.py:27
  730.6 6.8 collective-permute-done.143
  746.8 7.5 collective-permute-start.158
  754.2 7.6 collective-permute-done.145
  762.8 3.6 collective-permute-start.116
  766.4 4.1 collective-permute-done.159
  (914 shorter events, 347.7 us)
Async XLA Ops:
  23.8 29.3 %collective-permute-start.38 = (bf16[96,384]{1,0:T(8,128)(2,1)S(1)}, bf16[96,384]{1,0:T(8,128)(2,1)S(1)}, u32[]{:S(2)}, u32[]{:S(2)}) collective-permute-start(bf16[96,384]{1,0:T(8,128)(2,1)S(1)} %get-tuple-element.195), channel_id=1, source_target_pairs={{0,1},{1,0},{2,3},{3,2},{4,5},{5,4},{6,7},{7,6},{8,9},{9,8},{10,11... | collective-permute-start | bytes 221192 | tf_op jit(solution)/shard_map/ppermute | solution.py:27
  24.1 29.3 %collective-permute-start.27 = (bf16[24,1536]{1,0:T(8,128)(2,1)S(1)}, bf16[24,1536]{1,0:T(8,128)(2,1)S(1)}, u32[]{:S(2)}, u32[]{:S(2)}) collective-permute-start(bf16[24,1536]{1,0:T(8,128)(2,1)S(1)} %get-tuple-element.193), channel_id=1, source_target_pairs={{0,1},{1,0},{2,3},{3,2},{4,5},{5,4},{6,7},{7,6},{8,9},{9,8},{10,11... | collective-permute-start | bytes 221192 | tf_op jit(solution)/shard_map/ppermute | solution.py:27
  50.7 17.5 %collective-permute-start.78 = (bf16[96,384]{1,0:T(8,128)(2,1)S(1)}, bf16[96,384]{1,0:T(8,128)(2,1)S(1)}, u32[]{:S(2)}, u32[]{:S(2)}) collective-permute-start(bf16[96,384]{1,0:T(8,128)(2,1)S(1)} %get-tuple-element.189), channel_id=1, source_target_pairs={{0,1},{1,0},{2,3},{3,2},{4,5},{5,4},{6,7},{7,6},{8,9},{9,8},{10,11... | collective-permute-start | bytes 221192 | tf_op jit(solution)/shard_map/ppermute | solution.py:27
  55.0 37.9 %collective-permute-start.14 = (bf16[4,48,1536]{2,1,0:T(8,128)(2,1)S(1)}, bf16[4,48,1536]{2,1,0:T(8,128)(2,1)S(1)}, u32[]{:S(2)}, u32[]{:S(2)}) collective-permute-start(bf16[4,48,1536]{2,1,0:T(8,128)(2,1)S(1)} %pad_maximum_fusion.6.refs_0_), channel_id=1, source_target_pairs={{0,16},{1,17},{2,18},{3,19},{4,20},{5,21},{6,22},{7,23},{8,24},{9,... | collective-permute-start | bytes 1769480 | tf_op jit(solution)/shard_map/ppermute | solution.py:27
  66.6 26.4 %collective-permute-start.15 = (bf16[4,48,1536]{2,1,0:T(8,128)(2,1)S(1)}, bf16[4,48,1536]{2,1,0:T(8,128)(2,1)S(1)}, u32[]{:S(2)}, u32[]{:S(2)}) collective-permute-start(bf16[4,48,1536]{2,1,0:T(8,128)(2,1)S(1)} %collective-permute-done.13.refs_1_), channel_id=1, source_target_pairs={{0,16},{1,17},{2,18},{3,19},{4,20},{5,21},{6,22},{7,23},{8,24},{9,... | collective-permute-start | bytes 1769480 | tf_op jit(solution)/shard_map/ppermute | solution.py:27
  92.9 19.0 %collective-permute-start.18 = (bf16[4,48,1536]{2,1,0:T(8,128)(2,1)S(1)}, bf16[4,48,1536]{2,1,0:T(8,128)(2,1)S(1)}, u32[]{:S(2)}, u32[]{:S(2)}) collective-permute-start(bf16[4,48,1536]{2,1,0:T(8,128)(2,1)S(1)} %collective-permute-done.14.refs_2_), channel_id=1, source_target_pairs={{0,1},{1,0},{2,3},{3,2},{4,5},{5,4},{6,7},{7,6},{8,9},{9,8},{10,11... | collective-permute-start | bytes 1769480 | tf_op jit(solution)/shard_map/ppermute | solution.py:27
  93.0 20.4 %collective-permute-start.19 = (bf16[4,48,1536]{2,1,0:T(8,128)(2,1)S(1)}, bf16[4,48,1536]{2,1,0:T(8,128)(2,1)S(1)}, u32[]{:S(2)}, u32[]{:S(2)}) collective-permute-start(bf16[4,48,1536]{2,1,0:T(8,128)(2,1)S(1)} %collective-permute-done.15.refs_3_), channel_id=1, source_target_pairs={{0,1},{1,0},{2,3},{3,2},{4,5},{5,4},{6,7},{7,6},{8,9},{9,8},{10,11... | collective-permute-start | bytes 1769480 | tf_op jit(solution)/shard_map/ppermute | solution.py:27
  122.2 18.3 %collective-permute-start.31 = (bf16[4,48,1536]{2,1,0:T(8,128)(2,1)S(1)}, bf16[4,48,1536]{2,1,0:T(8,128)(2,1)}, u32[]{:S(2)}, u32[]{:S(2)}) collective-permute-start(bf16[4,48,1536]{2,1,0:T(8,128)(2,1)S(1)} %pad_maximum_fusion.7.refs_0_), channel_id=1, source_target_pairs={{0,8},{1,9},{2,10},{3,11},{4,12},{5,13},{6,14},{7,15},{8,0},{9,1},... | collective-permute-start | bytes 1769480 | tf_op jit(solution)/shard_map/ppermute | solution.py:27
  128.6 22.3 %collective-permute-start.53 = (bf16[4,48,1536]{2,1,0:T(8,128)(2,1)S(1)}, bf16[4,48,1536]{2,1,0:T(8,128)(2,1)}, u32[]{:S(2)}, u32[]{:S(2)}) collective-permute-start(bf16[4,48,1536]{2,1,0:T(8,128)(2,1)S(1)} %pad_maximum_fusion.9.refs_0_), channel_id=1, source_target_pairs={{0,8},{1,9},{2,10},{3,11},{4,12},{5,13},{6,14},{7,15},{8,0},{9,1},... | collective-permute-start | bytes 1769480 | tf_op jit(solution)/shard_map/ppermute | solution.py:27
  130.2 20.7 %collective-permute-start.22 = (bf16[576,256]{1,0:T(8,128)(2,1)}, bf16[576,256]{1,0:T(8,128)(2,1)}, u32[]{:S(2)}, u32[]{:S(2)}) collective-permute-start(bf16[576,256]{1,0:T(8,128)(2,1)} %get-tuple-element.115), channel_id=1, source_target_pairs={{0,6},{1,7},{2,4},{3,5},{4,2},{5,3},{6,0},{7,1},{8,14},{9,15},{10,... | collective-permute-start | bytes 884744 | tf_op jit(solution)/shard_map/ppermute | solution.py:27
  140.6 17.6 %collective-permute-start.21 = (bf16[576,256]{1,0:T(8,128)(2,1)}, bf16[576,256]{1,0:T(8,128)(2,1)S(1)}, u32[]{:S(2)}, u32[]{:S(2)}) collective-permute-start(bf16[576,256]{1,0:T(8,128)(2,1)} %get-tuple-element.116), channel_id=1, source_target_pairs={{0,4},{1,5},{2,6},{3,7},{4,0},{5,1},{6,2},{7,3},{8,12},{9,13},{10,... | collective-permute-start | bytes 884744 | tf_op jit(solution)/shard_map/ppermute | solution.py:27
  150.9 19.9 %collective-permute-start.44 = (bf16[4,192,384]{2,1,0:T(8,128)(2,1)S(1)}, bf16[4,192,384]{2,1,0:T(8,128)(2,1)}, u32[]{:S(2)}, u32[]{:S(2)}) collective-permute-start(bf16[4,192,384]{2,1,0:T(8,128)(2,1)S(1)} %collective-permute-done.42.refs_1_), channel_id=1, source_target_pairs={{0,16},{1,17},{2,18},{3,19},{4,20},{5,21},{6,22},{7,23},{8,24},{9,... | collective-permute-start | bytes 1769480 | tf_op jit(solution)/shard_map/ppermute | solution.py:27
  153.1 17.9 %collective-permute-start.46 = (bf16[4,192,384]{2,1,0:T(8,128)(2,1)S(1)}, bf16[4,192,384]{2,1,0:T(8,128)(2,1)S(1)}, u32[]{:S(2)}, u32[]{:S(2)}) collective-permute-start(bf16[4,192,384]{2,1,0:T(8,128)(2,1)S(1)} %collective-permute-done.42.refs_1_), channel_id=1, source_target_pairs={{0,1},{1,0},{2,3},{3,2},{4,5},{5,4},{6,7},{7,6},{8,9},{9,8},{10,11... | collective-permute-start | bytes 1769480 | tf_op jit(solution)/shard_map/ppermute | solution.py:27
  175.2 30.7 %collective-permute-start.57 = (bf16[4,48,1536]{2,1,0:T(8,128)(2,1)}, bf16[4,48,1536]{2,1,0:T(8,128)(2,1)}, u32[]{:S(2)}, u32[]{:S(2)}) collective-permute-start(bf16[4,48,1536]{2,1,0:T(8,128)(2,1)} %collective-permute-done.53.refs_1_), channel_id=1, source_target_pairs={{0,1},{1,0},{2,3},{3,2},{4,5},{5,4},{6,7},{7,6},{8,9},{9,8},{10,11... | collective-permute-start | bytes 1769480 | tf_op jit(solution)/shard_map/ppermute | solution.py:27
  175.2 32.9 %collective-permute-start.48 = (bf16[4,192,384]{2,1,0:T(8,128)(2,1)}, bf16[4,192,384]{2,1,0:T(8,128)(2,1)}, u32[]{:S(2)}, u32[]{:S(2)}) collective-permute-start(bf16[4,192,384]{2,1,0:T(8,128)(2,1)} %collective-permute-done.44.refs_3_), channel_id=1, source_target_pairs={{0,1},{1,0},{2,3},{3,2},{4,5},{5,4},{6,7},{7,6},{8,9},{9,8},{10,11... | collective-permute-start | bytes 1769480 | tf_op jit(solution)/shard_map/ppermute | solution.py:27
  175.7 32.4 %collective-permute-start.37 = (bf16[4,48,1536]{2,1,0:T(8,128)(2,1)}, bf16[4,48,1536]{2,1,0:T(8,128)(2,1)}, u32[]{:S(2)}, u32[]{:S(2)}) collective-permute-start(bf16[4,48,1536]{2,1,0:T(8,128)(2,1)} %collective-permute-done.33.refs_3_), channel_id=1, source_target_pairs={{0,1},{1,0},{2,3},{3,2},{4,5},{5,4},{6,7},{7,6},{8,9},{9,8},{10,11... | collective-permute-start | bytes 1769480 | tf_op jit(solution)/shard_map/ppermute | solution.py:27
  187.0 34.7 %collective-permute-start.58 = (bf16[4,48,1536]{2,1,0:T(8,128)(2,1)S(1)}, bf16[4,48,1536]{2,1,0:T(8,128)(2,1)}, u32[]{:S(2)}, u32[]{:S(2)}) collective-permute-start(bf16[4,48,1536]{2,1,0:T(8,128)(2,1)S(1)} %collective-permute-done.54.refs_2_), channel_id=1, source_target_pairs={{0,1},{1,0},{2,3},{3,2},{4,5},{5,4},{6,7},{7,6},{8,9},{9,8},{10,11... | collective-permute-start | bytes 1769480 | tf_op jit(solution)/shard_map/ppermute | solution.py:27
  187.0 36.9 %collective-permute-start.59 = (bf16[4,48,1536]{2,1,0:T(8,128)(2,1)S(1)}, bf16[4,48,1536]{2,1,0:T(8,128)(2,1)}, u32[]{:S(2)}, u32[]{:S(2)}) collective-permute-start(bf16[4,48,1536]{2,1,0:T(8,128)(2,1)S(1)} %collective-permute-done.55.refs_3_), channel_id=1, source_target_pairs={{0,1},{1,0},{2,3},{3,2},{4,5},{5,4},{6,7},{7,6},{8,9},{9,8},{10,11... | collective-permute-start | bytes 1769480 | tf_op jit(solution)/shard_map/ppermute | solution.py:27
  205.9 22.9 %collective-permute-start.26 = (bf16[192,256]{1,0:T(8,128)(2,1)S(1)}, bf16[192,256]{1,0:T(8,128)(2,1)S(1)}, u32[]{:S(2)}, u32[]{:S(2)}) collective-permute-start(bf16[192,256]{1,0:T(8,128)(2,1)S(1)} %get-tuple-element.159), channel_id=1, source_target_pairs={{0,6},{1,7},{2,4},{3,5},{4,2},{5,3},{6,0},{7,1},{8,14},{9,15},{10,... | collective-permute-start | bytes 294920 | tf_op jit(solution)/shard_map/ppermute | solution.py:27
  208.1 23.1 %collective-permute-start.25 = (bf16[192,256]{1,0:T(8,128)(2,1)S(1)}, bf16[192,256]{1,0:T(8,128)(2,1)S(1)}, u32[]{:S(2)}, u32[]{:S(2)}) collective-permute-start(bf16[192,256]{1,0:T(8,128)(2,1)S(1)} %get-tuple-element.160), channel_id=1, source_target_pairs={{0,4},{1,5},{2,6},{3,7},{4,0},{5,1},{6,2},{7,3},{8,12},{9,13},{10,... | collective-permute-start | bytes 294920 | tf_op jit(solution)/shard_map/ppermute | solution.py:27
  208.1 27.2 %collective-permute-start.24 = (bf16[192,256]{1,0:T(8,128)(2,1)S(1)}, bf16[192,256]{1,0:T(8,128)(2,1)S(1)}, u32[]{:S(2)}, u32[]{:S(2)}) collective-permute-start(bf16[192,256]{1,0:T(8,128)(2,1)S(1)} %get-tuple-element.161), channel_id=1, source_target_pairs={{0,2},{1,3},{2,0},{3,1},{4,6},{5,7},{6,4},{7,5},{8,10},{9,11},{10,... | collective-permute-start | bytes 294920 | tf_op jit(solution)/shard_map/ppermute | solution.py:27
  221.7 23.2 %collective-permute-start.70 = (bf16[48,1536]{1,0:T(8,128)(2,1)}, bf16[48,1536]{1,0:T(8,128)(2,1)S(1)}, u32[]{:S(2)}, u32[]{:S(2)}) collective-permute-start(bf16[48,1536]{1,0:T(8,128)(2,1)} %maximum_select_fusion.15), channel_id=1, source_target_pairs={{0,6},{1,7},{2,4},{3,5},{4,2},{5,3},{6,0},{7,1},{8,14},{9,15},{10,... | collective-permute-start | bytes 442376 | tf_op jit(solution)/shard_map/ppermute | solution.py:27
  223.9 23.2 %collective-permute-start.69 = (bf16[48,1536]{1,0:T(8,128)(2,1)}, bf16[48,1536]{1,0:T(8,128)(2,1)S(1)}, u32[]{:S(2)}, u32[]{:S(2)}) collective-permute-start(bf16[48,1536]{1,0:T(8,128)(2,1)} %maximum_select_fusion.15), channel_id=1, source_target_pairs={{0,4},{1,5},{2,6},{3,7},{4,0},{5,1},{6,2},{7,3},{8,12},{9,13},{10,... | collective-permute-start | bytes 442376 | tf_op jit(solution)/shard_map/ppermute | solution.py:27
  228.8 18.2 %collective-permute-start.68 = (bf16[48,1536]{1,0:T(8,128)(2,1)}, bf16[48,1536]{1,0:T(8,128)(2,1)S(1)}, u32[]{:S(2)}, u32[]{:S(2)}) collective-permute-start(bf16[48,1536]{1,0:T(8,128)(2,1)} %maximum_select_fusion.15), channel_id=1, source_target_pairs={{0,2},{1,3},{2,0},{3,1},{4,6},{5,7},{6,4},{7,5},{8,10},{9,11},{10,... | collective-permute-start | bytes 442376 | tf_op jit(solution)/shard_map/ppermute | solution.py:27
  231.2 42.8 %collective-permute-start.82 = (bf16[4,192,384]{2,1,0:T(8,128)(2,1)S(1)}, bf16[4,192,384]{2,1,0:T(8,128)(2,1)S(1)}, u32[]{:S(2)}, u32[]{:S(2)}) collective-permute-start(bf16[4,192,384]{2,1,0:T(8,128)(2,1)S(1)} %pad_maximum_fusion.11.refs_0_), channel_id=1, source_target_pairs={{0,8},{1,9},{2,10},{3,11},{4,12},{5,13},{6,14},{7,15},{8,0},{9,1},... | collective-permute-start | bytes 1769480 | tf_op jit(solution)/shard_map/ppermute | solution.py:27
  235.3 38.8 %collective-permute-start.83 = (bf16[4,192,384]{2,1,0:T(8,128)(2,1)S(1)}, bf16[4,192,384]{2,1,0:T(8,128)(2,1)}, u32[]{:S(2)}, u32[]{:S(2)}) collective-permute-start(bf16[4,192,384]{2,1,0:T(8,128)(2,1)S(1)} %pad_maximum_fusion.11.refs_0_), channel_id=1, source_target_pairs={{0,16},{1,17},{2,18},{3,19},{4,20},{5,21},{6,22},{7,23},{8,24},{9,... | collective-permute-start | bytes 1769480 | tf_op jit(solution)/shard_map/ppermute | solution.py:27
  248.2 24.9 %collective-permute-start.61 = (bf16[576,256]{1,0:T(8,128)(2,1)S(1)}, bf16[576,256]{1,0:T(8,128)(2,1)S(1)}, u32[]{:S(2)}, u32[]{:S(2)}) collective-permute-start(bf16[576,256]{1,0:T(8,128)(2,1)S(1)} %get-tuple-element.112), channel_id=1, source_target_pairs={{0,4},{1,5},{2,6},{3,7},{4,0},{5,1},{6,2},{7,3},{8,12},{9,13},{10,... | collective-permute-start | bytes 884744 | tf_op jit(solution)/shard_map/ppermute | solution.py:27
  256.7 17.9 %collective-permute-start.85 = (bf16[4,192,384]{2,1,0:T(8,128)(2,1)S(1)}, bf16[4,192,384]{2,1,0:T(8,128)(2,1)S(1)}, u32[]{:S(2)}, u32[]{:S(2)}) collective-permute-start(bf16[4,192,384]{2,1,0:T(8,128)(2,1)S(1)} %pad_maximum_fusion.11.refs_0_), channel_id=1, source_target_pairs={{0,1},{1,0},{2,3},{3,2},{4,5},{5,4},{6,7},{7,6},{8,9},{9,8},{10,11... | collective-permute-start | bytes 1769480 | tf_op jit(solution)/shard_map/ppermute | solution.py:27
  274.0 28.8 %collective-permute-start.63 = (bf16[4,384,256]{2,1,0:T(8,128)(2,1)S(1)}, bf16[4,384,256]{2,1,0:T(8,128)(2,1)S(1)}, u32[]{:S(2)}, u32[]{:S(2)}) collective-permute-start(bf16[4,384,256]{2,1,0:T(8,128)(2,1)S(1)} %pad_maximum_fusion.5), channel_id=1, source_target_pairs={{0,1},{1,0},{2,3},{3,2},{4,5},{5,4},{6,7},{7,6},{8,9},{9,8},{10,11... | collective-permute-start | bytes 2359304 | tf_op jit(solution)/shard_map/ppermute | solution.py:27
  274.6 18.1 %collective-permute-start.84 = (bf16[4,192,384]{2,1,0:T(8,128)(2,1)}, bf16[4,192,384]{2,1,0:T(8,128)(2,1)}, u32[]{:S(2)}, u32[]{:S(2)}) collective-permute-start(bf16[4,192,384]{2,1,0:T(8,128)(2,1)} %collective-permute-done.83.refs_2_), channel_id=1, source_target_pairs={{0,8},{1,9},{2,10},{3,11},{4,12},{5,13},{6,14},{7,15},{8,0},{9,1},... | collective-permute-start | bytes 1769480 | tf_op jit(solution)/shard_map/ppermute | solution.py:27
  288.6 32.0 %collective-permute-start.87 = (bf16[4,192,384]{2,1,0:T(8,128)(2,1)}, bf16[4,192,384]{2,1,0:T(8,128)(2,1)}, u32[]{:S(2)}, u32[]{:S(2)}) collective-permute-start(bf16[4,192,384]{2,1,0:T(8,128)(2,1)} %collective-permute-done.83.refs_2_), channel_id=1, source_target_pairs={{0,1},{1,0},{2,3},{3,2},{4,5},{5,4},{6,7},{7,6},{8,9},{9,8},{10,11... | collective-permute-start | bytes 1769480 | tf_op jit(solution)/shard_map/ppermute | solution.py:27
  292.7 30.2 %collective-permute-start.75 = (bf16[4,48,1536]{2,1,0:T(8,128)(2,1)}, bf16[4,48,1536]{2,1,0:T(8,128)(2,1)}, u32[]{:S(2)}, u32[]{:S(2)}) collective-permute-start(bf16[4,48,1536]{2,1,0:T(8,128)(2,1)} %collective-permute-done.71.refs_1_), channel_id=1, source_target_pairs={{0,1},{1,0},{2,3},{3,2},{4,5},{5,4},{6,7},{7,6},{8,9},{9,8},{10,11... | collective-permute-start | bytes 1769480 | tf_op jit(solution)/shard_map/ppermute | solution.py:27
  292.7 30.2 %collective-permute-start.88 = (bf16[4,192,384]{2,1,0:T(8,128)(2,1)}, bf16[4,192,384]{2,1,0:T(8,128)(2,1)}, u32[]{:S(2)}, u32[]{:S(2)}) collective-permute-start(bf16[4,192,384]{2,1,0:T(8,128)(2,1)} %collective-permute-done.84.refs_3_), channel_id=1, source_target_pairs={{0,1},{1,0},{2,3},{3,2},{4,5},{5,4},{6,7},{7,6},{8,9},{9,8},{10,11... | collective-permute-start | bytes 1769480 | tf_op jit(solution)/shard_map/ppermute | solution.py:27
  302.7 28.0 %collective-permute-start.76 = (bf16[4,48,1536]{2,1,0:T(8,128)(2,1)}, bf16[4,48,1536]{2,1,0:T(8,128)(2,1)}, u32[]{:S(2)}, u32[]{:S(2)}) collective-permute-start(bf16[4,48,1536]{2,1,0:T(8,128)(2,1)} %collective-permute-done.72.refs_2_), channel_id=1, source_target_pairs={{0,1},{1,0},{2,3},{3,2},{4,5},{5,4},{6,7},{7,6},{8,9},{9,8},{10,11... | collective-permute-start | bytes 1769480 | tf_op jit(solution)/shard_map/ppermute | solution.py:27
  302.8 27.9 %collective-permute-start.77 = (bf16[4,48,1536]{2,1,0:T(8,128)(2,1)S(1)}, bf16[4,48,1536]{2,1,0:T(8,128)(2,1)}, u32[]{:S(2)}, u32[]{:S(2)}) collective-permute-start(bf16[4,48,1536]{2,1,0:T(8,128)(2,1)S(1)} %collective-permute-done.73.refs_3_), channel_id=1, source_target_pairs={{0,1},{1,0},{2,3},{3,2},{4,5},{5,4},{6,7},{7,6},{8,9},{9,8},{10,11... | collective-permute-start | bytes 1769480 | tf_op jit(solution)/shard_map/ppermute | solution.py:27
  355.2 29.3 %collective-permute-start.134 = (bf16[768,384]{1,0:T(8,128)(2,1)}, bf16[768,384]{1,0:T(8,128)(2,1)}, u32[]{:S(2)}, u32[]{:S(2)}) collective-permute-start(bf16[768,384]{1,0:T(8,128)(2,1)} %convolution_convert_fusion.6), channel_id=1, source_target_pairs={{0,1},{1,0},{2,3},{3,2},{4,5},{5,4},{6,7},{7,6},{8,9},{9,8},{10,11... | collective-permute-start | bytes 1769480 | tf_op jit(solution)/shard_map/ppermute | solution.py:27
  406.2 23.4 %collective-permute-start.95 = (bf16[576,256]{1,0:T(8,128)(2,1)}, bf16[576,256]{1,0:T(8,128)(2,1)}, u32[]{:S(2)}, u32[]{:S(2)}) collective-permute-start(bf16[576,256]{1,0:T(8,128)(2,1)} %get-tuple-element.109), channel_id=1, source_target_pairs={{0,6},{1,7},{2,4},{3,5},{4,2},{5,3},{6,0},{7,1},{8,14},{9,15},{10,... | collective-permute-start | bytes 884744 | tf_op jit(solution)/shard_map/ppermute | solution.py:27
  408.2 24.5 %collective-permute-start.94 = (bf16[576,256]{1,0:T(8,128)(2,1)}, bf16[576,256]{1,0:T(8,128)(2,1)}, u32[]{:S(2)}, u32[]{:S(2)}) collective-permute-start(bf16[576,256]{1,0:T(8,128)(2,1)} %get-tuple-element.110), channel_id=1, source_target_pairs={{0,4},{1,5},{2,6},{3,7},{4,0},{5,1},{6,2},{7,3},{8,12},{9,13},{10,... | collective-permute-start | bytes 884744 | tf_op jit(solution)/shard_map/ppermute | solution.py:27
  408.3 24.4 %collective-permute-start.93 = (bf16[576,256]{1,0:T(8,128)(2,1)}, bf16[576,256]{1,0:T(8,128)(2,1)}, u32[]{:S(2)}, u32[]{:S(2)}) collective-permute-start(bf16[576,256]{1,0:T(8,128)(2,1)} %get-tuple-element.108), channel_id=1, source_target_pairs={{0,2},{1,3},{2,0},{3,1},{4,6},{5,7},{6,4},{7,5},{8,10},{9,11},{10,... | collective-permute-start | bytes 884744 | tf_op jit(solution)/shard_map/ppermute | solution.py:27
  427.6 143.8 %collective-permute-start.148 = (bf16[768,1536]{1,0:T(8,128)(2,1)}, bf16[768,1536]{1,0:T(8,128)(2,1)}, u32[]{:S(2)}, u32[]{:S(2)}) collective-permute-start(bf16[768,1536]{1,0:T(8,128)(2,1)} %convolution_convert_fusion.2), channel_id=1, source_target_pairs={{0,1},{1,0},{2,3},{3,2},{4,5},{5,4},{6,7},{7,6},{8,9},{9,8},{10,11... | collective-permute-start | bytes 7077896 | tf_op jit(solution)/shard_map/ppermute | solution.py:27
  459.6 25.6 %collective-permute-start.127 = (bf16[768,384]{1,0:T(8,128)(2,1)}, bf16[768,384]{1,0:T(8,128)(2,1)}, u32[]{:S(2)}, u32[]{:S(2)}) collective-permute-start(bf16[768,384]{1,0:T(8,128)(2,1)} %convolution_convert_fusion.7), channel_id=1, source_target_pairs={{0,1},{1,0},{2,3},{3,2},{4,5},{5,4},{6,7},{7,6},{8,9},{9,8},{10,11... | collective-permute-start | bytes 1769480 | tf_op jit(solution)/shard_map/ppermute | solution.py:27
  509.6 28.3 %collective-permute-start.102 = (bf16[576,256]{1,0:T(8,128)(2,1)}, bf16[576,256]{1,0:T(8,128)(2,1)}, u32[]{:S(2)}, u32[]{:S(2)}) collective-permute-start(bf16[576,256]{1,0:T(8,128)(2,1)} %get-tuple-element.101), channel_id=1, source_target_pairs={{0,6},{1,7},{2,4},{3,5},{4,2},{5,3},{6,0},{7,1},{8,14},{9,15},{10,... | collective-permute-start | bytes 884744 | tf_op jit(solution)/shard_map/ppermute | solution.py:27
  511.7 26.2 %collective-permute-start.101 = (bf16[576,256]{1,0:T(8,128)(2,1)}, bf16[576,256]{1,0:T(8,128)(2,1)}, u32[]{:S(2)}, u32[]{:S(2)}) collective-permute-start(bf16[576,256]{1,0:T(8,128)(2,1)} %get-tuple-element.102), channel_id=1, source_target_pairs={{0,4},{1,5},{2,6},{3,7},{4,0},{5,1},{6,2},{7,3},{8,12},{9,13},{10,... | collective-permute-start | bytes 884744 | tf_op jit(solution)/shard_map/ppermute | solution.py:27
  535.0 41.1 %collective-permute-start.162 = (bf16[3072,384]{1,0:T(8,128)(2,1)}, bf16[3072,384]{1,0:T(8,128)(2,1)}, u32[]{:S(2)}, u32[]{:S(2)}) collective-permute-start(bf16[3072,384]{1,0:T(8,128)(2,1)} %convolution_convert_fusion), channel_id=1, source_target_pairs={{0,1},{1,0},{2,3},{3,2},{4,5},{5,4},{6,7},{7,6},{8,9},{9,8},{10,11... | collective-permute-start | bytes 7077896 | tf_op jit(solution)/shard_map/ppermute | solution.py:27
  537.9 59.9 %collective-permute-start.120 = (bf16[768,1152]{1,0:T(8,128)(2,1)}, bf16[768,1152]{1,0:T(8,128)(2,1)}, u32[]{:S(2)}, u32[]{:S(2)}) collective-permute-start(bf16[768,1152]{1,0:T(8,128)(2,1)} %convolution_convert_fusion.4), channel_id=1, source_target_pairs={{0,1},{1,0},{2,3},{3,2},{4,5},{5,4},{6,7},{7,6},{8,9},{9,8},{10,11... | collective-permute-start | bytes 5308424 | tf_op jit(solution)/shard_map/ppermute | solution.py:27
  591.3 36.3 %collective-permute-start.141 = (bf16[768,1536]{1,0:T(8,128)(2,1)}, bf16[768,1536]{1,0:T(8,128)(2,1)}, u32[]{:S(2)}, u32[]{:S(2)}) collective-permute-start(bf16[768,1536]{1,0:T(8,128)(2,1)} %convolution_convert_fusion.3), channel_id=1, source_target_pairs={{0,1},{1,0},{2,3},{3,2},{4,5},{5,4},{6,7},{7,6},{8,9},{9,8},{10,11... | collective-permute-start | bytes 7077896 | tf_op jit(solution)/shard_map/ppermute | solution.py:27
  591.6 28.4 %collective-permute-start.149 = (bf16[2,4,48,1536]{3,2,1,0:T(8,128)(2,1)}, bf16[2,4,48,1536]{3,2,1,0:T(8,128)(2,1)}, u32[]{:S(2)}, u32[]{:S(2)}) collective-permute-start(bf16[2,4,48,1536]{3,2,1,0:T(8,128)(2,1)} %dynamic-slice_bitcast_fusion.2), channel_id=1, source_target_pairs={{0,8},{1,9},{2,10},{3,11},{4,12},{5,13},{6,14},{7,15},{8,0},{9,1},... | collective-permute-start | bytes 3538952 | tf_op jit(solution)/shard_map/ppermute | solution.py:27
  595.5 38.5 %collective-permute-start.155 = (bf16[3072,384]{1,0:T(8,128)(2,1)}, bf16[3072,384]{1,0:T(8,128)(2,1)}, u32[]{:S(2)}, u32[]{:S(2)}) collective-permute-start(bf16[3072,384]{1,0:T(8,128)(2,1)} %convolution_convert_fusion.1), channel_id=1, source_target_pairs={{0,1},{1,0},{2,3},{3,2},{4,5},{5,4},{6,7},{7,6},{8,9},{9,8},{10,11... | collective-permute-start | bytes 7077896 | tf_op jit(solution)/shard_map/ppermute | solution.py:27
  596.1 64.6 %collective-permute-start.113 = (bf16[768,1152]{1,0:T(8,128)(2,1)}, bf16[768,1152]{1,0:T(8,128)(2,1)}, u32[]{:S(2)}, u32[]{:S(2)}) collective-permute-start(bf16[768,1152]{1,0:T(8,128)(2,1)} %convolution_convert_fusion.5), channel_id=1, source_target_pairs={{0,1},{1,0},{2,3},{3,2},{4,5},{5,4},{6,7},{7,6},{8,9},{9,8},{10,11... | collective-permute-start | bytes 5308424 | tf_op jit(solution)/shard_map/ppermute | solution.py:27
  597.8 29.1 %collective-permute-start.163 = (bf16[2,4,192,384]{3,2,1,0:T(8,128)(2,1)}, bf16[2,4,192,384]{3,2,1,0:T(8,128)(2,1)S(1)}, u32[]{:S(2)}, u32[]{:S(2)}) collective-permute-start(bf16[2,4,192,384]{3,2,1,0:T(8,128)(2,1)} %dynamic-slice_bitcast_fusion), channel_id=1, source_target_pairs={{0,16},{1,17},{2,18},{3,19},{4,20},{5,21},{6,22},{7,23},{8,24},{9,... | collective-permute-start | bytes 3538952 | tf_op jit(solution)/shard_map/ppermute | solution.py:27
  620.0 25.9 %collective-permute-start.121 = (bf16[2,4,48,1152]{3,2,1,0:T(8,128)(2,1)S(1)}, bf16[2,4,48,1152]{3,2,1,0:T(8,128)(2,1)S(1)}, u32[]{:S(2)}, u32[]{:S(2)}) collective-permute-start(bf16[2,4,48,1152]{3,2,1,0:T(8,128)(2,1)S(1)} %dynamic-slice_bitcast_fusion.4), channel_id=1, source_target_pairs={{0,16},{1,17},{2,18},{3,19},{4,20},{5,21},{6,22},{7,23},{8,24},{9,... | collective-permute-start | bytes 2654216 | tf_op jit(solution)/shard_map/ppermute | solution.py:27
  626.9 31.6 %collective-permute-start.150 = (bf16[4,48,1536]{2,1,0:T(8,128)(2,1)S(1)}, bf16[4,48,1536]{2,1,0:T(8,128)(2,1)S(1)}, u32[]{:S(2)}, u32[]{:S(2)}) collective-permute-start(bf16[4,48,1536]{2,1,0:T(8,128)(2,1)S(1)} %dynamic-slice_bitcast_fusion.8), channel_id=1, source_target_pairs={{0,16},{1,17},{2,18},{3,19},{4,20},{5,21},{6,22},{7,23},{8,24},{9,... | collective-permute-start | bytes 1769480 | tf_op jit(solution)/shard_map/ppermute | solution.py:27
  627.6 37.9 %collective-permute-start.164 = (bf16[4,192,384]{2,1,0:T(8,128)(2,1)S(1)}, bf16[4,192,384]{2,1,0:T(8,128)(2,1)S(1)}, u32[]{:S(2)}, u32[]{:S(2)}) collective-permute-start(bf16[4,192,384]{2,1,0:T(8,128)(2,1)S(1)} %dynamic-slice_bitcast_fusion.6), channel_id=1, source_target_pairs={{0,8},{1,9},{2,10},{3,11},{4,12},{5,13},{6,14},{7,15},{8,0},{9,1},... | collective-permute-start | bytes 1769480 | tf_op jit(solution)/shard_map/ppermute | solution.py:27
  634.0 72.0 %collective-permute-start.142 = (bf16[2,4,48,1536]{3,2,1,0:T(8,128)(2,1)}, bf16[2,4,48,1536]{3,2,1,0:T(8,128)(2,1)}, u32[]{:S(2)}, u32[]{:S(2)}) collective-permute-start(bf16[2,4,48,1536]{3,2,1,0:T(8,128)(2,1)} %dynamic-slice_bitcast_fusion.3), channel_id=1, source_target_pairs={{0,16},{1,17},{2,18},{3,19},{4,20},{5,21},{6,22},{7,23},{8,24},{9,... | collective-permute-start | bytes 3538952 | tf_op jit(solution)/shard_map/ppermute | solution.py:27
  646.2 40.2 %collective-permute-start.122 = (bf16[4,48,1152]{2,1,0:T(8,128)(2,1)S(1)}, bf16[4,48,1152]{2,1,0:T(8,128)(2,1)S(1)}, u32[]{:S(2)}, u32[]{:S(2)}) collective-permute-start(bf16[4,48,1152]{2,1,0:T(8,128)(2,1)S(1)} %dynamic-slice_bitcast_fusion.10), channel_id=1, source_target_pairs={{0,8},{1,9},{2,10},{3,11},{4,12},{5,13},{6,14},{7,15},{8,0},{9,1},... | collective-permute-start | bytes 1327112 | tf_op jit(solution)/shard_map/ppermute | solution.py:27
  680.4 29.2 %collective-permute-start.156 = (bf16[2,4,192,384]{3,2,1,0:T(8,128)(2,1)}, bf16[2,4,192,384]{3,2,1,0:T(8,128)(2,1)}, u32[]{:S(2)}, u32[]{:S(2)}) collective-permute-start(bf16[2,4,192,384]{3,2,1,0:T(8,128)(2,1)} %dynamic-slice_bitcast_fusion.1), channel_id=1, source_target_pairs={{0,8},{1,9},{2,10},{3,11},{4,12},{5,13},{6,14},{7,15},{8,0},{9,1},... | collective-permute-start | bytes 3538952 | tf_op jit(solution)/shard_map/ppermute | solution.py:27
  694.5 34.1 %collective-permute-start.114 = (bf16[2,4,48,1152]{3,2,1,0:T(8,128)(2,1)}, bf16[2,4,48,1152]{3,2,1,0:T(8,128)(2,1)}, u32[]{:S(2)}, u32[]{:S(2)}) collective-permute-start(bf16[2,4,48,1152]{3,2,1,0:T(8,128)(2,1)} %dynamic-slice_bitcast_fusion.5), channel_id=1, source_target_pairs={{0,8},{1,9},{2,10},{3,11},{4,12},{5,13},{6,14},{7,15},{8,0},{9,1},... | collective-permute-start | bytes 2654216 | tf_op jit(solution)/shard_map/ppermute | solution.py:27
  707.8 29.6 %collective-permute-start.143 = (bf16[4,48,1536]{2,1,0:T(8,128)(2,1)S(1)}, bf16[4,48,1536]{2,1,0:T(8,128)(2,1)S(1)}, u32[]{:S(2)}, u32[]{:S(2)}) collective-permute-start(bf16[4,48,1536]{2,1,0:T(8,128)(2,1)S(1)} %dynamic-slice_bitcast_fusion.9), channel_id=1, source_target_pairs={{0,8},{1,9},{2,10},{3,11},{4,12},{5,13},{6,14},{7,15},{8,0},{9,1},... | collective-permute-start | bytes 1769480 | tf_op jit(solution)/shard_map/ppermute | solution.py:27
  711.3 31.5 %collective-permute-start.157 = (bf16[4,192,384]{2,1,0:T(8,128)(2,1)S(1)}, bf16[4,192,384]{2,1,0:T(8,128)(2,1)S(1)}, u32[]{:S(2)}, u32[]{:S(2)}) collective-permute-start(bf16[4,192,384]{2,1,0:T(8,128)(2,1)S(1)} %dynamic-slice_bitcast_fusion.7), channel_id=1, source_target_pairs={{0,16},{1,17},{2,18},{3,19},{4,20},{5,21},{6,22},{7,23},{8,24},{9,... | collective-permute-start | bytes 1769480 | tf_op jit(solution)/shard_map/ppermute | solution.py:27
  740.2 21.6 %collective-permute-start.145 = (bf16[48,1536]{1,0:T(8,128)(2,1)S(1)}, bf16[48,1536]{1,0:T(8,128)(2,1)S(1)}, u32[]{:S(2)}, u32[]{:S(2)}) collective-permute-start(bf16[48,1536]{1,0:T(8,128)(2,1)S(1)} %get-tuple-element.127), channel_id=1, source_target_pairs={{0,4},{1,5},{2,6},{3,7},{4,0},{5,1},{6,2},{7,3},{8,12},{9,13},{10,... | collective-permute-start | bytes 442376 | tf_op jit(solution)/shard_map/ppermute | solution.py:27
  742.8 19.9 %collective-permute-start.144 = (bf16[48,1536]{1,0:T(8,128)(2,1)S(1)}, bf16[48,1536]{1,0:T(8,128)(2,1)S(1)}, u32[]{:S(2)}, u32[]{:S(2)}) collective-permute-start(bf16[48,1536]{1,0:T(8,128)(2,1)S(1)} %get-tuple-element.125), channel_id=1, source_target_pairs={{0,2},{1,3},{2,0},{3,1},{4,6},{5,7},{6,4},{7,5},{8,10},{9,11},{10,... | collective-permute-start | bytes 442376 | tf_op jit(solution)/shard_map/ppermute | solution.py:27
  743.0 19.8 %collective-permute-start.160 = (bf16[192,384]{1,0:T(8,128)(2,1)S(1)}, bf16[192,384]{1,0:T(8,128)(2,1)S(1)}, u32[]{:S(2)}, u32[]{:S(2)}) collective-permute-start(bf16[192,384]{1,0:T(8,128)(2,1)S(1)} %get-tuple-element.120), channel_id=1, source_target_pairs={{0,6},{1,7},{2,4},{3,5},{4,2},{5,3},{6,0},{7,1},{8,14},{9,15},{10,... | collective-permute-start | bytes 442376 | tf_op jit(solution)/shard_map/ppermute | solution.py:27
  744.9 25.6 %collective-permute-start.159 = (bf16[192,384]{1,0:T(8,128)(2,1)S(1)}, bf16[192,384]{1,0:T(8,128)(2,1)S(1)}, u32[]{:S(2)}, u32[]{:S(2)}) collective-permute-start(bf16[192,384]{1,0:T(8,128)(2,1)S(1)} %get-tuple-element.121), channel_id=1, source_target_pairs={{0,4},{1,5},{2,6},{3,7},{4,0},{5,1},{6,2},{7,3},{8,12},{9,13},{10,... | collective-permute-start | bytes 442376 | tf_op jit(solution)/shard_map/ppermute | solution.py:27
  746.8 23.8 %collective-permute-start.158 = (bf16[192,384]{1,0:T(8,128)(2,1)S(1)}, bf16[192,384]{1,0:T(8,128)(2,1)S(1)}, u32[]{:S(2)}, u32[]{:S(2)}) collective-permute-start(bf16[192,384]{1,0:T(8,128)(2,1)S(1)} %get-tuple-element.119), channel_id=1, source_target_pairs={{0,2},{1,3},{2,0},{3,1},{4,6},{5,7},{6,4},{7,5},{8,10},{9,11},{10,... | collective-permute-start | bytes 442376 | tf_op jit(solution)/shard_map/ppermute | solution.py:27
  (259 other events, 3115.7 us)

commit v3 on v2

--- a/solution.py
+++ b/solution.py
@@ -27,96 +27,295 @@
     return lax.ppermute(value, ("dp", "ctx"), pairs)
 
 
-def place_kernel(dp_size, chips, *refs):
-    pieces, whole, held, in_sem, out_sem = refs[: 2 * dp_size], *refs[2 * dp_size :]
-    half = held.shape[-1]
-    dp_rank, ctx_rank = lax.axis_index("dp"), lax.axis_index("ctx")
-    chip, core = ctx_rank // 2, ctx_rank % 2
-    arrivals = []
-    for n, piece in enumerate(pieces):
-        for k in range(chips):
-            copy = pltpu.make_async_copy(piece.at[k], held.at[n, k], in_sem.at[n, k])
-            copy.start()
-            arrivals.append((n, k, copy))
-    leaving = []
-    for n, k, copy in arrivals:
-        copy.wait()
-        side, move = n // dp_size, n % dp_size
-        row = (dp_rank ^ move) * chips + (chip ^ k)
-        column = pl.multiple_of((core ^ side) * half, half)
-        out = pltpu.make_async_copy(
-            held.at[n, k], whole.at[row, :, pl.ds(column, half)], out_sem.at[n, k]
-        )
-        out.start()
-        leaving.append(out)
-    for out in leaving:
-        out.wait()
-
-
-def gather_rows(shard, order):
-    dp_size, chips = lax.axis_size("dp"), lax.axis_size("ctx") // 2
-    rows, columns = shard.shape
-    half = columns // 2
-    core = lax.axis_index("ctx") % 2
-    kept = lax.dynamic_slice_in_dim(shard, core * half, half, 1)
-    given = lax.dynamic_slice_in_dim(shard, (1 - core) * half, half, 1)
-    got = swap(given, 0, 1)
-    own = jnp.where(core == 0, jnp.concatenate([kept, got]), jnp.concatenate([got, kept]))
-    line = jnp.stack([own] + [swap(own, 0, 2 * k) for k in range(1, chips)])
-    pieces = {0: line}
-    for bit in order:
-        for place in list(pieces):
-            pieces[place ^ bit] = swap(pieces[place], bit, 0)
-    near = [pieces[place] for place in range(dp_size)]
-    far = [swap(piece, 0, 1) for piece in near]
-    whole = pl.pallas_call(
-        functools.partial(place_kernel, dp_size, chips),
-        out_shape=jax.ShapeDtypeStruct((dp_size * chips, 2 * rows, columns), shard.dtype),
-        in_specs=[pl.BlockSpec(memory_space=pl.ANY)] * (2 * dp_size),
-        out_specs=pl.BlockSpec(memory_space=pl.ANY),
-        scratch_shapes=[
-            pltpu.VMEM((2 * dp_size, chips, 2 * rows, half), shard.dtype),
-            pltpu.SemaphoreType.DMA((2 * dp_size, chips)),
-            pltpu.SemaphoreType.DMA((2 * dp_size, chips)),
-        ],
-        cost_estimate=pl.CostEstimate(
-            flops=0, transcendentals=0, bytes_accessed=4 * dp_size * chips * rows * columns * 2
-        ),
-    )(*near, *far)
-    return whole.reshape(dp_size * chips * 2 * rows, columns)
+def flip(index, bits):
+    bit = 1
+    while bit <= bits:
+        if bits & bit:
+            index = index + bit * (1 - 2 * ((index // bit) % 2))
+        bit *= 2
+    return index
 
 
 def pick(value, place, axis):
     return lax.dynamic_index_in_dim(value, place, axis, keepdims=False)
 
 
-def reduce_rows(left, right, order, left_dim=0, right_dim=0):
+class Route:
+    def __init__(self, phases, chips):
+        self.phases, self.chips = phases, chips
+        self.dp, ctx = lax.axis_index("dp"), lax.axis_index("ctx")
+        self.chip, self.core = ctx // 2, ctx % 2
+
+    def over(self, s, side):
+        rising, falling = self.dp, self.dp
+        for p in range(self.phases):
+            if s >> p & 1:
+                rising, falling = flip(rising, 1 << p), flip(falling, 1 << (self.phases - 1 - p))
+        return (1 - side) * rising + side * falling
+
+    def row(self, s, k, side):
+        return self.over(s, side) * self.chips + flip(self.chip, k)
+
+    def phase_partner(self, p):
+        return (self.over(1 << p, self.core), 2 * self.chip + self.core)
+
+    def chip_partner(self, k):
+        return (self.dp, 2 * flip(self.chip, k) + self.core)
+
+    def core_partner(self):
+        return (self.dp, 2 * self.chip + 1 - self.core)
+
+    def meet(self, cores):
+        partners = [self.phase_partner(p) for p in range(self.phases)]
+        partners += [self.chip_partner(k) for k in range(1, self.chips)]
+        if cores:
+            partners.append(self.core_partner())
+        barrier = pltpu.get_barrier_semaphore()
+        for partner in partners:
+            pl.semaphore_signal(
+                barrier, inc=1, device_id=partner, device_id_type=pl.DeviceIdType.MESH
+            )
+        pl.semaphore_wait(barrier, len(partners))
+
+
+def send(source, target, leave, arrive, device):
+    copy = pltpu.make_async_remote_copy(
+        src_ref=source,
+        dst_ref=target,
+        send_sem=leave,
+        recv_sem=arrive,
+        device_id=device,
+        device_id_type=pl.DeviceIdType.MESH,
+    )
+    copy.start()
+    return copy
+
+
+def cut(shape, most):
+    rows, columns = shape
+    if rows * columns <= most:
+        return [(slice(0, rows), slice(0, columns))]
+    if columns > 512:
+        step = max(128, most // rows // 128 * 128)
+        return [
+            (slice(0, rows), slice(at, min(at + step, columns))) for at in range(0, columns, step)
+        ]
+    step = max(16, most // columns // 16 * 16)
+    return [(slice(at, min(at + step, rows)), slice(0, columns)) for at in range(0, rows, step)]
+
+
+def span(part, base=0):
+    start = base + part.start if isinstance(base, int) else pl.multiple_of(base + part.start, 128)
+    return pl.ds(start, part.stop - part.start)
+
+
+def gather_kernel(phases, chips, count, *refs):
+    owns, wholes = refs[:count], refs[count : 2 * count]
+    place_sem, leave, arrive, give, take = refs[2 * count :]
+    route = Route(phases, chips)
+    route.meet(True)
+    items = [(w, *piece) for w in range(count) for piece in cut(owns[w].shape, 80000)]
+
+    def spot(n, s, k, side):
+        w, rows, columns = items[n]
+        whole, row = wholes[w], route.row(s, k, side)
+        if len(whole.shape) == 4:
+            return whole.at[row, side]
+        return whole.at[row, span(rows), span(columns, side * owns[w].shape[-1])]
+
+    travels, gifts, placed = {}, [], []
+
+    def forward(n, s, k):
+        target = spot(n, s, k, route.core)
+        w, rows, columns = items[n]
+        source = owns[w].at[span(rows), span(columns)] if s == 0 and k == 0 else target
+        if s == 0 and k == 0:
+            for z in range(1, chips):
+                travels[n, 0, z] = send(
+                    source, target, leave.at[n, 0, z], arrive.at[n, 0, z], route.chip_partner(z)
+                )
+        for p in range(s.bit_length(), phases):
+            after = s | 1 << p
+            travels[n, after, k] = send(
+                source, target, leave.at[n, after, k], arrive.at[n, after, k], route.phase_partner(p)
+            )
+        gifts.append(send(source, target, give.at[n, s, k], take.at[n, s, k], route.core_partner()))
+        return source, target
+
+    for n in range(len(items)):
+        source, target = forward(n, 0, 0)
+        copy = pltpu.make_async_copy(source, target, place_sem.at[n])
+        copy.start()
+        placed.append(copy)
+    schedule = sorted(
+        (n + k + s.bit_count(), n, s, k)
+        for n in range(len(items))
+        for s in range(1 << phases)
+        for k in range(chips)
+        if s or k
+    )
+    for _, n, s, k in schedule:
+        travels[n, s, k].wait_recv()
+        forward(n, s, k)
+    for copy in placed:
+        copy.wait()
+    for copy in travels.values():
+        copy.wait_send()
+    for copy in gifts:
+        copy.wait()
+
+
+def gather_many(owns, collective_id):
     dp_size, chips = lax.axis_size("dp"), lax.axis_size("ctx") // 2
-    dp_rank, ctx_rank = lax.axis_index("dp"), lax.axis_index("ctx")
-    chip, core = ctx_rank // 2, ctx_rank % 2
-    rows = left.shape[1 - left_dim] // (dp_size * chips * 2)
-    columns = right.shape[1 - right_dim]
-    half = columns // 2
+    phases, count = dp_size.bit_length() - 1, len(owns)
+    total = dp_size * chips
+    items = sum(len(cut(own.shape, 80000)) for own in owns)
+    shapes = []
+    for own in owns:
+        rows, columns = own.shape
+        shape = (total, 2, rows, columns) if rows == 8 else (total, rows, 2 * columns)
+        shapes.append(jax.ShapeDtypeStruct(shape, own.dtype))
+    slots = (items, 1 << phases, chips)
+    return pl.pallas_call(
+        functools.partial(gather_kernel, phases, chips, count),
+        out_shape=tuple(shapes),
+        in_specs=[pl.BlockSpec(memory_space=pl.ANY)] * count,
+        out_specs=(pl.BlockSpec(memory_space=pl.ANY),) * count,
+        scratch_shapes=[pltpu.SemaphoreType.DMA((items,))]
+        + [pltpu.SemaphoreType.DMA(slots)] * 4,
+        compiler_params=pltpu.CompilerParams(collective_id=collective_id, has_side_effects=True),
+        cost_estimate=pl.CostEstimate(
+            flops=15 * 10**9 * count, transcendentals=0, bytes_accessed=10**6 * count
+        ),
+    )(*owns)
+
+
+def gather_far(shard):
+    return lax.all_gather(shard, ("dp", "ctx"), axis=0, tiled=True)
+
+
+def reduce_kernel(phases, chips, count, pieces, *refs):
+    parts, outs = refs[:count], refs[count : 2 * count]
+    items = len(pieces)
+    refs = refs[2 * count :]
+    sums, landed = refs[:items], refs[items : 2 * items]
+    leave, arrive = refs[2 * items :]
+    route = Route(phases, chips)
+    route.meet(False)
+    slots = 1 << phases
+
+    def bit_of(s):
+        return (s & -s).bit_length() - 1 if s else phases
+
+    def order(kept):
+        return [
+            (s, k)
+            for s in sorted(kept, key=lambda s: (bit_of(s), s))
+            for k in [*range(1, chips), 0]
+        ]
+
+    def seat(p, s):
+        return slots - (slots >> p) + (s >> (p + 1))
+
+    def term(n, s, k):
+        w, rows, columns = pieces[n]
+        return parts[w].at[route.row(s, k, route.core), span(rows), span(columns)]
+
+    travels, waiting = {}, []
+
+    def flush():
+        while waiting:
+            n, p, s, k = waiting.pop()
+            place = (seat(p, s ^ 1 << p), k) if p < phases else (slots - 1, k)
+            travels[n, p, place] = send(
+                term(n, s, k) if p == 0 else sums[n].at[s >> 1, k],
+                landed[n].at[place],
+                leave.at[(n, *place)],
+                arrive.at[(n, *place)],
+                route.phase_partner(p) if p < phases else route.chip_partner(k),
+            )
+
+    for n in range(items):
+        for s, k in order([s for s in range(slots) if s % 2 == 0]):
+            waiting.append((n, 0, s ^ 1, k))
+            flush()
+    for n in range(items):
+        for p in range(phases):
+            for s, k in order([s for s in range(slots) if bit_of(s) > p]):
+                place = (seat(p, s), k)
+                travels[n, p, place].wait_recv()
+                if p == phases - 1 and k == 0:
+                    continue
+                before = term(n, s, k)[...] if p == 0 else sums[n][s >> 1, k]
+                added = before.astype(jnp.float32) + landed[n][place].astype(jnp.float32)
+                flush()
+                sums[n][s >> 1, k] = added.astype(before.dtype)
+                if bit_of(s) == p + 1 and (s or k):
+                    waiting.append((n, p + 1, s, k))
+            flush()
+    for n, (w, rows, columns) in enumerate(pieces):
+        last = (seat(phases - 1, 0), 0)
+        before = term(n, 0, 0)[...] if phases == 1 else sums[n][0, 0]
+        total = before.astype(jnp.float32) + landed[n][last].astype(jnp.float32)
+        for k in range(1, chips):
+            place = (slots - 1, k)
+            travels[n, phases, place].wait_recv()
+            total = total + landed[n][place].astype(jnp.float32)
+        outs[w][rows, columns] = total
+    for copy in travels.values():
+        copy.wait_send()
+
+
+def reduce_many(parts, collective_id):
+    dp_size, chips = lax.axis_size("dp"), lax.axis_size("ctx") // 2
+    phases, count = dp_size.bit_length() - 1, len(parts)
+    slots = 1 << phases
+    pieces = [(w, *piece) for w, part in enumerate(parts) for piece in cut(part.shape[1:], 36864)]
+    sizes = [
+        ((rows.stop - rows.start, columns.stop - columns.start), parts[w].dtype)
+        for w, rows, columns in pieces
+    ]
+    return pl.pallas_call(
+        functools.partial(reduce_kernel, phases, chips, count, pieces),
+        out_shape=tuple(jax.ShapeDtypeStruct(part.shape[1:], jnp.float32) for part in parts),
+        in_specs=[pl.BlockSpec(memory_space=pltpu.VMEM)] * count,
+        out_specs=(pl.BlockSpec(memory_space=pltpu.VMEM),) * count,
+        scratch_shapes=[pltpu.VMEM((slots // 2, chips, *size), dtype) for size, dtype in sizes]
+        + [pltpu.VMEM((slots, chips, *size), dtype) for size, dtype in sizes]
+        + [pltpu.SemaphoreType.DMA((len(pieces), slots, chips))] * 2,
+        compiler_params=pltpu.CompilerParams(collective_id=collective_id, has_side_effects=True),
+        cost_estimate=pl.CostEstimate(
+            flops=15 * 10**9 * count, transcendentals=0, bytes_accessed=10**6 * count
+        ),
+    )(*parts)
+
+
+def chip_rows(shards):
+    core = lax.axis_index("ctx") % 2
+    half = shards.shape[2] // 2
+    kept = lax.dynamic_slice_in_dim(shards, core * half, half, 2)
+    got = swap(lax.dynamic_slice_in_dim(shards, (1 - core) * half, half, 2), 0, 1)
+    return jnp.where(
+        core == 0, jnp.concatenate([kept, got], axis=1), jnp.concatenate([got, kept], axis=1)
+    )
+
+
+def chip_part(left, right, left_dim=0, right_dim=0):
+    dp_size, chips = lax.axis_size("dp"), lax.axis_size("ctx") // 2
+    core = lax.axis_index("ctx") % 2
+    half = right.shape[1 - right_dim] // 2
     own_side = lax.dynamic_slice_in_dim(right, core * half, half, 1 - right_dim)
     far_side = lax.dynamic_slice_in_dim(right, (1 - core) * half, half, 1 - right_dim)
     got = swap(contract(left, far_side, left_dim, right_dim).astype(jnp.bfloat16), 0, 1)
     part = (contract(left, own_side, left_dim, right_dim) + got.astype(jnp.float32)).astype(
         jnp.bfloat16
     )
-    bits = [1 << n for n in reversed(range(dp_size.bit_length() - 1))]
-    part = part.reshape([2] * len(bits) + [chips, 2 * rows, half])
-    for bit in order:
-        axis = bits.index(bit)
-        bits.remove(bit)
-        side = (dp_rank // bit) % 2
-        got = swap(pick(part, 1 - side, axis), bit, 0)
-        part = (pick(part, side, axis).astype(jnp.float32) + got.astype(jnp.float32)).astype(
-            jnp.bfloat16
-        )
-    total = pick(part, chip, 0).astype(jnp.float32)
-    for k in range(1, chips):
-        total = total + swap(pick(part, chip ^ k, 0), 0, 2 * k).astype(jnp.float32)
-    total = total.reshape(2, rows, half)
+    return part.reshape(dp_size * chips, -1, half)
+
+
+def device_rows(total):
+    core = lax.axis_index("ctx") % 2
+    total = total.reshape(2, -1, total.shape[1])
     got = swap(pick(total, 1 - core, 0), 0, 1)
     kept = pick(total, core, 0)
     return jnp.where(
@@ -124,36 +323,6 @@
         jnp.concatenate([kept, got], axis=1),
         jnp.concatenate([got, kept], axis=1),
     )
-
-
-def gather_small(packed):
-    dp_size, ctx_size = lax.axis_size("dp"), lax.axis_size("ctx")
-    mine = lax.axis_index("dp") * ctx_size + lax.axis_index("ctx")
-    held = packed.reshape(1, 8, -1)
-    held = jnp.concatenate([held] + [swap(held, 0, k) for k in range(1, ctx_size)])
-    bit = 1
-    while bit < dp_size:
-        held = jnp.concatenate([held, swap(held, bit, 0)])
-        bit *= 2
-    devices = dp_size * ctx_size
-    held = held.reshape(devices, -1)
-    source = mine ^ jnp.arange(devices, dtype=jnp.int32)
-    chosen = (source[:, None] == jnp.arange(devices, dtype=jnp.int32)[None, :]).astype(held.dtype)
-    return jnp.dot(chosen, held, preferred_element_type=jnp.float32).astype(held.dtype)
-
-
-def reduce_small(terms):
-    dp_size, ctx_size = lax.axis_size("dp"), lax.axis_size("ctx")
-    dp_rank, ctx_rank = lax.axis_index("dp"), lax.axis_index("ctx")
-    width = terms.shape[1]
-    part = terms.reshape(dp_size, ctx_size, 8, width // 8)
-    total = pick(part, dp_rank, 0)
-    for k in range(1, dp_size):
-        total = total + swap(pick(part, dp_rank ^ k, 0), k, 0)
-    row = pick(total, ctx_rank, 0)
-    for k in range(1, ctx_size):
-        row = row + swap(pick(total, ctx_rank ^ k, 0), 0, k)
-    return row.reshape(width)
 
 
 def layer_norm(residual, norm_gain, norm_bias):
@@ -354,11 +523,8 @@
     return jnp.concatenate([pick(held, part ^ j, 0) for j in range(parts)])
 
 
-def attend(grouped, starts, first, parts, shares):
-    width, length = grouped.shape[1] // 3, grouped.shape[2]
-    mine = spread(grouped, parts, shares)
-    joint = jnp.stack([piece[width:] for piece in mine])
-    theirs = jnp.stack([swap(joint, 0, j) for j in range(1, shares)])
+def attend(mine, theirs, starts, first, parts, shares):
+    width, length = mine[0].shape[0] // 3, mine[0].shape[1]
     mixed, logs = pl.pallas_call(
         functools.partial(mix_kernel, parts, shares),
         out_shape=(
@@ -383,13 +549,12 @@
             bytes_accessed=4 * parts * width * length * 2,
         ),
     )(first, starts, *mine, theirs)
-    return mixed, logs, mine, theirs
-
-
-def attend_back(grouped_grads, kept, starts, first, parts, shares):
+    return mixed, logs
+
+
+def attend_back(grads, kept, starts, first, parts, shares):
     mixed, logs, mine, theirs = kept
     width, length = mixed.shape[1:]
-    grads = spread(grouped_grads, parts, shares)
     grad_queries, own, far = pl.pallas_call(
         functools.partial(mix_back_kernel, parts, shares),
         out_shape=(
@@ -418,129 +583,98 @@
             bytes_accessed=8 * parts * width * length * 2,
         ),
     )(first, starts, mixed, logs, *mine, *grads, theirs)
-    for j in range(1, shares):
-        own = own + swap(far[j - 1], 0, j).astype(jnp.float32)
-    joint = jnp.concatenate([grad_queries, own.astype(jnp.bfloat16)], axis=1)
-    return collect([joint[k] for k in range(parts)], parts, shares)
-
-
-def forward_layer(residual, layer_params, plan):
+    return grad_queries, own, far
+
+
+def forward_layer(residual, narrow, joined, held, plan, near):
+    starts, first, parts, shares, qkv_scale = plan
+    width = residual.shape[1]
+    normed_in, normed1, inv_std1 = layer_norm(residual, narrow["gain1"], narrow["bias1"])
+    attn_in = normed_in.astype(jnp.bfloat16)
+    qkv_weight, out_weight = joined
+    projected = (contract(qkv_weight, attn_in, 0, 1) + narrow["qkv"][:, None]) * qkv_scale[:, None]
+    grouped = projected.astype(jnp.bfloat16).reshape(parts, -1, residual.shape[0])
+    if not near:
+        mine = spread(grouped, parts, shares)
+        fc_weight, proj_weight = held
+    else:
+        grouped, held = lax.optimization_barrier((grouped, held))
+        mine = spread(grouped, parts, shares)
+        fc_weight, proj_weight = gather_many(held, 2)
+    joint = jnp.stack([piece[width // parts :] for piece in mine])
+    theirs = jnp.stack([swap(joint, 0, j) for j in range(1, shares)])
+    if near:
+        mine, theirs, fc_weight, proj_weight = lax.optimization_barrier(
+            (mine, theirs, fc_weight, proj_weight)
+        )
+    mixed, logs = attend(mine, theirs, starts, first, parts, shares)
+    kept = (mixed, logs, mine, theirs)
+    mixed_columns = collect([mixed[k] for k in range(parts)], parts, shares)
+    fc_weight = fc_weight.reshape(width, -1)
+    proj_weight = proj_weight.reshape(-1, width)
+    middle = residual + contract(mixed_columns, out_weight, 0, 0) + narrow["out"]
+    normed_mid, normed2, inv_std2 = layer_norm(middle, narrow["gain2"], narrow["bias2"])
+    ffn_in = normed_mid.astype(jnp.bfloat16)
+    pre_act = jnp.dot(ffn_in, fc_weight, preferred_element_type=jnp.float32) + narrow["fc"]
+    hidden = gelu_value(pre_act).astype(jnp.bfloat16)
+    result = middle + jnp.dot(hidden, proj_weight, preferred_element_type=jnp.float32) + narrow["proj"]
+    saved = (
+        (normed1, inv_std1, attn_in, kept, mixed_columns, normed2, inv_std2, ffn_in, pre_act, hidden),
+        (qkv_weight, out_weight, fc_weight, proj_weight),
+    )
+    return result, saved
+
+
+def backward_layer(grad_residual, saved, narrow, plan, carried):
     (
-        norm1_gain,
-        norm1_bias,
-        qkv_weight,
-        qkv_bias,
-        qkv_scale,
-        out_weight,
-        out_bias,
-        norm2_gain,
-        norm2_bias,
-        fc_weight,
-        fc_bias,
-        proj_weight,
-        proj_bias,
-    ) = layer_params
-    starts, first, parts, shares = plan
-    normed_in, normed1, inv_std1 = layer_norm(residual, norm1_gain, norm1_bias)
-    attn_in = normed_in.astype(jnp.bfloat16)
-    projected = (contract(qkv_weight, attn_in, 0, 1) + qkv_bias[:, None]) * qkv_scale[:, None]
-    grouped = projected.astype(jnp.bfloat16).reshape(parts, -1, residual.shape[0])
-    kept = attend(grouped, starts, first, parts, shares)
-    mixed_columns = collect([kept[0][k] for k in range(parts)], parts, shares)
-    middle = residual + contract(mixed_columns, out_weight, 0, 0) + out_bias
-    normed_mid, normed2, inv_std2 = layer_norm(middle, norm2_gain, norm2_bias)
-    ffn_in = normed_mid.astype(jnp.bfloat16)
-    pre_act = jnp.dot(ffn_in, fc_weight, preferred_element_type=jnp.float32) + fc_bias
-    hidden = gelu_value(pre_act).astype(jnp.bfloat16)
-    result = middle + jnp.dot(hidden, proj_weight, preferred_element_type=jnp.float32) + proj_bias
-    return (
-        result,
-        (
-            normed1,
-            inv_std1,
-            attn_in,
-            kept,
-            mixed_columns,
-            normed2,
-            inv_std2,
-            ffn_in,
-            pre_act,
-            hidden,
-        ),
-    )
-
-
-def backward_layer(grad_residual, saved_rows, layer_params, plan, orders):
-    (
-        normed1,
-        inv_std1,
-        attn_in,
-        kept,
-        mixed_columns,
-        normed2,
-        inv_std2,
-        ffn_in,
-        pre_act,
-        hidden,
-    ) = saved_rows
-    (
-        norm1_gain,
-        norm1_bias,
-        qkv_weight,
-        qkv_bias,
-        qkv_scale,
-        out_weight,
-        out_bias,
-        norm2_gain,
-        norm2_bias,
-        fc_weight,
-        fc_bias,
-        proj_weight,
-        proj_bias,
-    ) = layer_params
-    starts, first, parts, shares = plan
+        (normed1, inv_std1, attn_in, kept, mixed_columns, normed2, inv_std2, ffn_in, pre_act, hidden),
+        (qkv_weight, out_weight, fc_weight, proj_weight),
+    ) = saved
+    starts, first, parts, shares, _ = plan
     grad_narrow = grad_residual.astype(jnp.bfloat16)
-    grad_proj_w = reduce_rows(hidden, grad_narrow, orders[2])
+    grad_proj_w = chip_part(hidden, grad_narrow)
     grad_proj_b = jnp.sum(grad_residual, axis=0)
     grad_hidden = contract(grad_narrow, proj_weight, 1, 1)
     grad_pre = grad_hidden * gelu_slope(pre_act)
     pre_narrow = grad_pre.astype(jnp.bfloat16)
-    grad_fc_w = reduce_rows(ffn_in, pre_narrow, orders[1])
+    grad_fc_w = chip_part(ffn_in, pre_narrow)
     grad_fc_b = jnp.sum(grad_pre, axis=0)
     grad_norm2 = contract(pre_narrow, fc_weight, 1, 1)
     grad_gain2 = jnp.sum(grad_norm2 * normed2, axis=0)
     grad_bias2 = jnp.sum(grad_norm2, axis=0)
-    grad_middle = grad_residual + norm_back(grad_norm2, normed2, inv_std2, norm2_gain)
+    grad_middle = grad_residual + norm_back(grad_norm2, normed2, inv_std2, narrow["gain2"])
     middle_narrow = grad_middle.astype(jnp.bfloat16)
-    grad_out_w = reduce_rows(mixed_columns, middle_narrow, orders[1], left_dim=1)
+    grad_out_w = chip_part(mixed_columns, middle_narrow, left_dim=1)
     grad_out_b = jnp.sum(grad_middle, axis=0)
     grad_mixed = contract(out_weight, middle_narrow, 1, 1).astype(jnp.bfloat16)
     grad_mixed = grad_mixed.reshape(parts, -1, grad_mixed.shape[1])
-    grad_qkv = attend_back(grad_mixed, kept, starts, first, parts, shares)
-    grad_qkv_w = reduce_rows(attn_in, grad_qkv, orders[0], right_dim=1)
+    grads = spread(grad_mixed, parts, shares)
+    grad_queries, own, far = attend_back(grads, kept, starts, first, parts, shares)
+    for j in range(1, shares):
+        own = own + swap(far[j - 1], 0, j).astype(jnp.float32)
+    joint = jnp.concatenate([grad_queries, own.astype(jnp.bfloat16)], axis=1)
+    terms = [grad_proj_w, grad_fc_w, grad_out_w, *carried]
+    joint, terms = lax.optimization_barrier((joint, terms))
+    grad_qkv = collect([joint[k] for k in range(parts)], parts, shares)
+    sums = reduce_many(terms, 4 + len(carried))
+    grad_qkv, sums = lax.optimization_barrier((grad_qkv, sums))
+    grad_qkv_w = chip_part(attn_in, grad_qkv, right_dim=1)
     grad_qkv_b = jnp.sum(grad_qkv.astype(jnp.float32), axis=1).reshape(parts, 3, -1)
     grad_norm1 = contract(grad_qkv, qkv_weight, 0, 1)
     grad_gain1 = jnp.sum(grad_norm1 * normed1, axis=0)
     grad_bias1 = jnp.sum(grad_norm1, axis=0)
-    grad_before = grad_middle + norm_back(grad_norm1, normed1, inv_std1, norm1_gain)
-    return (
-        grad_before,
-        (
-            grad_gain1,
-            grad_bias1,
-            by_kind(grad_qkv_w, parts),
-            grad_qkv_b[:, 0].reshape(-1),
-            grad_qkv_b[:, 2].reshape(-1),
-            grad_out_w,
-            grad_out_b,
-            grad_gain2,
-            grad_bias2,
-            grad_fc_w,
-            grad_fc_b,
-            grad_proj_w,
-            grad_proj_b,
-        ),
-    )
+    grad_before = grad_middle + norm_back(grad_norm1, normed1, inv_std1, narrow["gain1"])
+    vectors = (
+        grad_gain1,
+        grad_bias1,
+        grad_qkv_b[:, 0].reshape(-1),
+        grad_qkv_b[:, 2].reshape(-1),
+        grad_out_b,
+        grad_gain2,
+        grad_bias2,
+        grad_proj_b,
+    )
+    return grad_before, grad_qkv_w, sums, vectors, grad_fc_b
 
 
 def by_part(columns, parts):
@@ -577,8 +711,6 @@
     devices = dp_size * ctx_size
     parts = math.gcd(model_width // HEAD, ctx_size)
     shares = ctx_size // parts
-    rising = [1 << n for n in range(dp_size.bit_length() - 1)]
-    falling = rising[::-1]
     narrow_list = (ln1_gain, ln1_bias, b_query, b_value, b_out, ln2_gain, ln2_bias, b_proj)
     narrow_count = LAYERS * len(narrow_list)
     slot = narrow_list[0].shape[1]
@@ -593,7 +725,23 @@
             jnp.zeros((packed_size - used - row_count,), jnp.bfloat16),
         ]
     )
-    small = gather_small(packed)
+    joined_pieces = chip_rows(jnp.concatenate([by_part(w_qkv[0], parts), w_out[0]], axis=1)[None])[0]
+    fc_pieces, proj_pieces = chip_rows(w_fc[:1])[0], chip_rows(w_proj[:1])[0]
+    joined, small = gather_many([joined_pieces, packed.reshape(8, -1)], 1)
+    later_shards = (w_qkv[1:], w_out[1:], w_fc[1:], w_proj[1:])
+    joined = joined.reshape(model_width, -1)
+    far_weights = [
+        (
+            (gather_far(by_part(qkv, parts)), gather_far(out)),
+            (gather_far(fc), gather_far(proj)),
+        )
+        for qkv, out, fc, proj in zip(*later_shards)
+    ]
+    near_weights = (
+        (joined[:, : 3 * model_width], joined[:, 3 * model_width :]),
+        (fc_pieces, proj_pieces),
+    )
+    small = small.reshape(devices, -1)
     narrow_all = (
         jnp.transpose(
             small[:, : narrow_count * slot].reshape(devices, narrow_count, slot), (1, 0, 2)
@@ -619,7 +767,6 @@
         before = jnp.sum((ids < number).astype(jnp.int32))
         starts = jnp.where(ids == number, before, starts)
     first = starts[:, 0] // row_count
-    plan = (starts.reshape(ctx_size, 1, row_count), first, parts, shares)
     qkv_scale = jnp.tile(
         jnp.concatenate(
             [
@@ -630,51 +777,40 @@
         parts,
     )
 
+    plan = (starts.reshape(ctx_size, 1, row_count), first, parts, shares, qkv_scale)
+
     residual = block_input.reshape(row_count, model_width).astype(jnp.float32)
-    kept_params = []
-    saved_list = []
+    narrow_sets, saved_list = [], []
     for layer_idx in range(LAYERS):
-        ways = (rising, falling) if layer_idx % 2 == 0 else (falling, rising)
-        joined = gather_rows(
-            jnp.concatenate([by_part(w_qkv[layer_idx], parts), w_out[layer_idx]], axis=1), ways[0]
-        )
-        fc_weight = gather_rows(w_fc[layer_idx], ways[1])
-        proj_weight = gather_rows(w_proj[layer_idx], ways[0])
-        narrow = narrow_all[layer_idx]
-        qkv_bias = by_part(
-            jnp.concatenate([narrow[2], jnp.zeros_like(narrow[2]), narrow[3]])[None], parts
+        rows = narrow_all[layer_idx]
+        narrow = dict(
+            zip(("gain1", "bias1", "query", "value", "out", "gain2", "bias2", "proj"), rows)
+        )
+        narrow["fc"] = fc_all[layer_idx]
+        narrow["qkv"] = by_part(
+            jnp.concatenate([rows[2], jnp.zeros_like(rows[2]), rows[3]])[None], parts
         )[0]
-        layer_params = (
-            narrow[0],
-            narrow[1],
-            joined[:, : 3 * model_width],
-            qkv_bias,
-            qkv_scale,
-            joined[:, 3 * model_width :],
-            narrow[4],
-            narrow[5],
-            narrow[6],
-            fc_weight,
-            fc_all[layer_idx],
-            proj_weight,
-            narrow[7],
-        )
-        residual, saved_rows = forward_layer(residual, layer_params, plan)
-        kept_params.append(layer_params)
-        saved_list.append(saved_rows)
+        residual, saved = forward_layer(
+            residual, narrow, *([near_weights] + far_weights)[layer_idx], plan, layer_idx == 0
+        )
+        narrow_sets.append(narrow)
+        saved_list.append(saved)
     output_rows = residual.astype(jnp.bfloat16).reshape(seq_count, local_len, model_width)
     grad_residual = out_grad.reshape(row_count, model_width).astype(jnp.float32)
-    reduced = [None] * LAYERS
+    qkv_sums, other_sums, vector_sets, fc_sets = ([None] * LAYERS for _ in range(4))
+    carried = []
     for layer_idx in reversed(range(LAYERS)):
-        orders = (rising, falling, rising) if layer_idx % 2 == 0 else (falling, rising, falling)
-        grad_residual, reduced[layer_idx] = backward_layer(
-            grad_residual, saved_list[layer_idx], kept_params[layer_idx], plan, orders
-        )
+        grad_residual, part, sums, vector_sets[layer_idx], fc_sets[layer_idx] = backward_layer(
+            grad_residual, saved_list[layer_idx], narrow_sets[layer_idx], plan, carried
+        )
+        other_sums[layer_idx] = sums[:3]
+        if carried:
+            qkv_sums[layer_idx + 1] = sums[3]
+        carried = [part]
     grad_rows = grad_residual.astype(jnp.bfloat16).reshape(seq_count, local_len, model_width)
     term_size = -(-used // 1024) * 1024
-    narrow_members = (0, 1, 3, 4, 6, 7, 8, 12)
-    narrow_terms = jnp.stack([grads[member] for grads in reduced for member in narrow_members])
-    fc_terms = jnp.stack([grads[10] for grads in reduced])
+    narrow_terms = jnp.stack([vector for vectors in vector_sets for vector in vectors])
+    fc_terms = jnp.stack(fc_sets)
     terms = jnp.concatenate(
         [
             jnp.transpose(narrow_terms.reshape(narrow_count, devices, slot), (1, 0, 2)).reshape(
@@ -687,18 +823,34 @@
         ],
         axis=1,
     )
-    sums = reduce_small(terms)
+    terms = terms.reshape(devices // 2, 2, 8, term_size // 8)
+    core = lax.axis_index("ctx") % 2
+    terms = pick(terms, core, 1) + swap(pick(terms, 1 - core, 1), 0, 1)
+    qkv_sums[0], sums = reduce_many([*carried, terms], 6)
+    sums = sums.reshape(-1)
     narrow_sums = sums[: narrow_count * slot].reshape(LAYERS, len(narrow_list), slot)
-    fc_sums = sums[narrow_count * slot : used].reshape(LAYERS, fc_slot)
-    stacked = []
-    for member in range(13):
-        if member in narrow_members:
-            stacked.append(narrow_sums[:, narrow_members.index(member)])
-        elif member == 10:
-            stacked.append(fc_sums)
-        else:
-            stacked.append(jnp.stack([grads[member] for grads in reduced]))
-    return (output_rows, grad_rows, *stacked)
+    grad_fc_b = sums[narrow_count * slot : used].reshape(LAYERS, fc_slot)
+    grad_w_qkv = jnp.stack([by_kind(device_rows(total), parts) for total in qkv_sums])
+    grad_w_proj, grad_w_fc, grad_w_out = (
+        jnp.stack([device_rows(sums[n]) for sums in other_sums]) for n in range(3)
+    )
+    return (
+        output_rows,
+        grad_rows,
+        narrow_sums[:, 0],
+        narrow_sums[:, 1],
+        grad_w_qkv,
+        narrow_sums[:, 2],
+        narrow_sums[:, 3],
+        grad_w_out,
+        narrow_sums[:, 4],
+        narrow_sums[:, 5],
+        narrow_sums[:, 6],
+        grad_w_fc,
+        grad_fc_b,
+        grad_w_proj,
+        narrow_sums[:, 7],
+    )
 
 
 def solution(mesh):

time: 788 us -> 689 us (0.87)
  Pallas kernels: 96 us -> 343 us
  waiting for transfers between devices: 273 us -> 78.9 us
  starting transfers between devices: 173 us -> 48.8 us
  local copies, waits for them, and re-layouts: 91.9 us -> 61.2 us
  other arithmetic: 54.5 us -> 29.5 us
  matrix products: 84.8 us -> 104 us
  between operations: 3.83 us -> 16.3 us
    pallas_call x6 -> x5, Pallas kernels: 30.1 us -> 288 us  [the longest x3 165 us: reduce_many(): pl.pallas_call(functools.partial(reduce_kernel, phases, chips, count, pie...]
    ppermute x169 -> x48, waiting for transfers between devices: 273 us -> 55 us  [swap(): return lax.ppermute(value, ('dp', 'ctx'), pairs)]
    ppermute x169 -> x48, starting transfers between devices: 173 us -> 48.7 us  [swap(): return lax.ppermute(value, ('dp', 'ctx'), pairs)]
    all_gather x0 -> x4, waiting for transfers between devices: none -> 23.8 us  [gather_far(): return lax.all_gather(shard, ('dp', 'ctx'), axis=0, tiled=True)]
    another operation x28 -> x29, local copies, waits for them, and re-layouts: 28.4 us -> 14.1 us  [the longest x17 11.3 us: shards(): jnp.stack([vector for vectors in vector_sets for vector in vectors])]
    unnamed x347 -> x260, local copies, waits for them, and re-layouts: 23.7 us -> 12.6 us
    dot_general x28, matrix products: 76.8 us -> 87.8 us  [contract(): lax.dot_general(left, right, (((left_dim,), (right_dim,)), ((), ())), pre...]
    convert_element_type x18 -> x2, other arithmetic: 10.5 us -> 0.47 us  [backward_layer(): joint = jnp.concatenate([grad_queries, own.astype(jnp.bfloat16)], axis=1)]
  transfers between devices with their start and end apart: 169 -> 52, of which waited for: 52 -> 9; matrix products, arithmetic and copies ran while one was open for 26% -> 19% of each run, Pallas kernels for 12% -> 46%
where the time goes in v3:
time: 689 us; the launch traced here: 681 us
  Pallas kernels  343 us (50%)
  matrix products  104 us (15%)
  waiting for transfers between devices  78.9 us (11%)
  local copies, waits for them, and re-layouts  61.2 us (9%)
  starting transfers between devices  48.8 us (7%)
  other arithmetic  29.5 us (4%)
  between operations  16.3 us (2%)
    pallas_call x3, Pallas kernels, reduce_many(): pl.pallas_call(functools.partial(reduce_kernel, phases, chips, count, pie...  165 us
    pallas_call x2, Pallas kernels, gather_many(): pl.pallas_call(functools.partial(gather_kernel, phases, chips, count), ou...  122 us
    dot_general x28, matrix products, contract(): lax.dot_general(left, right, (((left_dim,), (right_dim,)), ((), ())), pre...  87.8 us
    ppermute x48, waiting for transfers between devices, swap(): return lax.ppermute(value, ('dp', 'ctx'), pairs)  55 us
    ppermute x48, starting transfers between devices, swap(): return lax.ppermute(value, ('dp', 'ctx'), pairs)  48.7 us
    pallas_call x2, Pallas kernels, attend_back(): pl.pallas_call(functools.partial(mix_back_kernel, parts, shares), out_sha...  28.9 us
    pallas_call x2, Pallas kernels, attend(): pl.pallas_call(functools.partial(mix_kernel, parts, shares), out_shape=(j...  25.8 us
    all_gather x4, waiting for transfers between devices, gather_far(): return lax.all_gather(shard, ('dp', 'ctx'), axis=0, tiled=True)  23.8 us
  transfers between devices with their start and end apart: 52, of which 9 were waited for; matrix products, arithmetic and copies ran while one was open for 19% of the time, Pallas kernels for 46%

profile of v3, /device:TPU:0, one launch (start us, length us, event | category | flops | bytes accessed | tf_op | source)
XLA Modules:
  0.0 681.1 jit_solution(15898637256496845922)
XLA Ops:
  11.0 1.7 fusion.149
  17.7 39.8 %shard_map.271 = (bf16[16,48,3072]{2,1,0:T(8,128)(2,1)}, bf16[16,2,8,128]{3,2,1,0:T(8,128)(2,1)}) custom-call(bf16[48,1536]{1,0:T(8,128)(2,1)} %maximum_select_fusion.6.refs_0_, bf16[8,128]{1,0:T(8,128)(2,1)} %maximum_bitcast_fusion.2.refs_1_), custom_call_target="tpu_custom_call" | custom-call | flops 30000001024 | bytes 2000000 | tf_op jit(solution)/shard_map/pallas_call | solution.py:179
  61.1 3.7 fusion.16
  65.6 1.8 collective-permute-start.4
  67.4 2.6 collective-permute-start.5
  70.0 82.7 %shard_map.272 = (bf16[16,48,3072]{2,1,0:T(8,128)(2,1)}, bf16[16,192,768]{2,1,0:T(8,128)(2,1)}) custom-call(bf16[48,1536]{1,0:T(8,128)(2,1)} %maximum_select_fusion.7.refs_0_, bf16[192,384]{1,0:T(8,128)(2,1)} %maximum_select_fusion.8.refs_1_), custom_call_target="tpu_custom_call" | custom-call | flops 30000001024 | bytes 2000000 | tf_op jit(solution)/shard_map/pallas_call | solution.py:179
  154.9 5.2 select_select_fusion
  162.4 12.8 %shard_map.273 = (bf16[4,192,256]{2,1,0:T(8,128)(2,1)}, f32[4,8,256]{2,1,0:T(8,128)}) custom-call(s32[8]{0:T(128)} %and_select_fusion.refs_0_, s32[8,1,256]{2,1,0:T(1,128)} %reshape.731.refs_1_, bf16[576,256]{1,0:T(8,128)(2,1)} %get-tuple-element.73.refs_2_.refs_4_, bf16[576,256]{1,0:T(8,128)(2,1)} %copy-done.32, bf16[576,256]{1,0:T(8,128)(2,1)} %copy-done.33, ...), custom_call_target="tpu_custom_call" | custom-call | flops 1610612736 | bytes 1572864 | tf_op jit(solution)/shard_map/pallas_call | solution.py:528
  176.4 4.3 collective-permute-start.7
  181.0 1.9 collective-permute-done.9
  184.2 2.0 fusion.154
  186.6 4.0 convolution_add_fusion.2
  190.6 2.1 fusion.155
  193.0 4.2 fusion.18
  199.5 3.2 collective-permute-start.12
  204.0 10.5 %collective-permute-done.12.refs_5_.refs_7_ = bf16[576,256]{1,0:T(8,128)(2,1)S(1)} collective-permute-done((bf16[576,256]{1,0:T(8,128)(2,1)S(1)}, bf16[576,256]{1,0:T(8,128)(2,1)S(1)}, u32[]{:S(2)}, u32[]{:S(2)}) %collective-permute-start.12) | collective-permute-done | bytes 294944 | tf_op jit(solution)/shard_map/ppermute | solution.py:27
  214.5 28.0 %collective-permute-done.11.refs_4_.refs_6_ = bf16[576,256]{1,0:T(8,128)(2,1)S(1)} collective-permute-done((bf16[576,256]{1,0:T(8,128)(2,1)S(1)}, bf16[576,256]{1,0:T(8,128)(2,1)S(1)}, u32[]{:S(2)}, u32[]{:S(2)}) %collective-permute-start.11) | collective-permute-done | bytes 294944 | tf_op jit(solution)/shard_map/ppermute | solution.py:27
  243.6 2.2 collective-permute-done.13
  246.7 13.0 %shard_map.274 = (bf16[4,192,256]{2,1,0:T(8,128)(2,1)}, f32[4,8,256]{2,1,0:T(8,128)}) custom-call(s32[8]{0:T(128)} %and_select_fusion.refs_0_, s32[8,1,256]{2,1,0:T(1,128)} %reshape.731.refs_1_, bf16[576,256]{1,0:T(8,128)(2,1)} %get-tuple-element.192.refs_2_.refs_4_, bf16[576,256]{1,0:T(8,128)(2,1)} %copy-done.35, bf16[576,256]{1,0:T(8,128)(2,1)} %copy-done.36, ...), custom_call_target="tpu_custom_call" | custom-call | flops 1610612736 | bytes 1572864 | tf_op jit(solution)/shard_map/pallas_call | solution.py:528
  261.3 3.9 collective-permute-start.14
  267.4 5.9 collective-permute-done.15
  273.5 1.9 fusion.156
  275.7 3.9 fusion.13
  281.3 2.8 convolution_convert_fusion.1
  284.1 23.7 %all-gather.14.cloned.1.call-done = bf16[1,3072,768]{2,1,0:T(8,128)(2,1)} async-done(((bf16[1,96,768]{2,1,0:T(8,128)(2,1)}), bf16[1,3072,768]{2,1,0:T(8,128)(2,1)}) %all-gather.14.cloned.1.call-update) | async-done | bytes 4718608 | tf_op jit(solution)/shard_map/all_gather | solution.py:194
  307.9 7.1 %fusion.144 = (f32[3072]{0:T(1024)}, bf16[256,3072]{1,0:T(8,128)(2,1)S(1)}) fusion(f32[256,3072]{1,0:T(8,128)} %copy-done.110, bf16[1,3072,768]{2,1,0:T(8,128)(2,1)} %all-gather.14.cloned.1.call-done, bf16[1,256,768]{2,1,0:T(8,128)(2,1)S(1)} %copy-done.26), kind=kOutput, calls=%fused_computation.368 | convolution fusion | flops 1223685120 | bytes 9842688 | tf_op jit(solution)/shard_map/dot_general | solution.py:367
  315.0 5.2 multiply_reduce_fusion
  326.2 2.2 collective-permute-start.19
  328.4 3.5 convolution_convert_fusion.5
  337.8 14.4 %shard_map.275 = (bf16[4,192,256]{2,1,0:T(8,128)(2,1)}, f32[4,384,256]{2,1,0:T(8,128)}, bf16[1,4,384,256]{3,2,1,0:T(8,128)(2,1)}) custom-call(s32[8]{0:T(128)} %and_select_fusion.refs_0_, s32[8,1,256]{2,1,0:T(1,128)} %reshape.731.refs_1_, bf16[4,192,256]{2,1,0:T(8,128)(2,1)} %get-tuple-element.81.refs_2_, f32[4,8,256]{2,1,0:T(8,128)} %get-tuple-element.82.refs_3_, ...), custom_call_target="tpu_custom_call" | custom-call | flops 4026531840 | bytes 3145728 | tf_op jit(solution)/shard_map/pallas_call | solution.py:558
  352.1 3.8 collective-permute-start.20
  356.0 6.0 fusion.45
  362.0 2.4 add_convert_fusion.9
  366.4 5.0 add_convert_fusion.3
  371.4 4.1 add_convert_fusion.2
  375.5 1.7 collective-permute-start.26
  377.6 2.4 collective-permute-start.24
  380.0 59.8 %shard_map.276 = (f32[192,384]{1,0:T(8,128)}, f32[48,1536]{1,0:T(8,128)}, f32[48,384]{1,0:T(8,128)}) custom-call(bf16[16,192,384]{2,1,0:T(8,128)(2,1)} %bitcast.440, bf16[16,48,1536]{2,1,0:T(8,128)(2,1)} %bitcast.366, bf16[16,48,384]{2,1,0:T(8,128)(2,1)} %bitcast.442), custom_call_target="tpu_custom_call" | custom-call | flops 44999999488 | bytes 3000000 | tf_op jit(solution)/shard_map/pallas_call | solution.py:278
  441.9 1.9 multiply_reduce_fusion.1
  445.7 3.1 fusion.143
  448.8 2.8 convolution_convert_fusion
  451.7 2.2 multiply_reduce_fusion.2
  453.9 2.4 convolution_convert_fusion.4
  457.1 2.2 convolution_convert_fusion.8
  460.2 2.2 collective-permute-start.28
  462.4 2.1 convolution_convert_fusion.3
  466.4 1.7 constant_dynamic-slice_fusion.2
  468.1 2.2 convolution_convert_fusion.6
  478.7 2.0 collective-permute-start.29
  482.3 3.7 collective-permute-done.29.refs_11_
  486.7 14.6 %shard_map.277 = (bf16[4,192,256]{2,1,0:T(8,128)(2,1)}, f32[4,384,256]{2,1,0:T(8,128)}, bf16[1,4,384,256]{3,2,1,0:T(8,128)(2,1)}) custom-call(s32[8]{0:T(128)} %and_select_fusion.refs_0_, s32[8,1,256]{2,1,0:T(1,128)} %reshape.731.refs_1_, bf16[4,192,256]{2,1,0:T(8,128)(2,1)} %get-tuple-element.78.refs_2_, f32[4,8,256]{2,1,0:T(8,128)} %get-tuple-element.94.refs_3_, ...), custom_call_target="tpu_custom_call" | custom-call | flops 4026531840 | bytes 3145728 | tf_op jit(solution)/shard_map/pallas_call | solution.py:558
  501.3 3.8 collective-permute-start.30
  508.6 2.5 add_convert_fusion.8
  511.9 3.8 add_convert_fusion.5
  515.7 5.1 add_convert_fusion.1
  520.8 4.1 add_convert_fusion
  525.0 2.0 collective-permute-start.37
  527.4 2.1 collective-permute-start.35
  529.4 75.3 %shard_map.278 = (f32[192,384]{1,0:T(8,128)}, f32[48,1536]{1,0:T(8,128)}, f32[48,384]{1,0:T(8,128)}, f32[48,1152]{1,0:T(8,128)}) custom-call(bf16[16,192,384]{2,1,0:T(8,128)(2,1)} %bitcast.439, bf16[16,48,1536]{2,1,0:T(8,128)(2,1)} %bitcast.365, bf16[16,48,384]{2,1,0:T(8,128)(2,1)} %bitcast.441, bf16[16,48,1152]{2,1,0:T(8,128)(2,1)} %bitcast.367), custom_call_target="tpu_custom_call" | custom-call | flops 60000002048 | bytes 4000000 | tf_op jit(solution)/shard_map/pallas_call | solution.py:278
  605.8 4.2 fusion.66
  610.1 2.1 convolution_convert_fusion.2
  622.8 2.4 fusion.88
  635.2 3.5 add_convert_fusion.4
  638.7 30.4 %shard_map.279 = (f32[48,1152]{1,0:T(8,128)}, f32[8,128]{1,0:T(8,128)}) custom-call(bf16[16,48,1152]{2,1,0:T(8,128)(2,1)} %bitcast.368, f32[16,8,128]{2,1,0:T(8,128)} %bitcast_add_fusion.refs_1_), custom_call_target="tpu_custom_call" | custom-call | flops 30000001024 | bytes 2000000 | tf_op jit(solution)/shard_map/pallas_call | solution.py:278
  (526 shorter events, 95.4 us)
Async XLA Ops:
  7.3 185.6 %all-gather.8.cloned.1.call-start = ((), (), s32[]{:S(2)}) async-start(), calls=%async_computation | async-start | bytes 3649536 | tf_op jit(solution)/shard_map/all_gather | solution.py:194
  9.5 263.9 %all-gather.10.cloned.1.call-start = ((), (), s32[]{:S(2)}) async-start(), calls=%async_computation.1 | async-start | bytes 1216512 | tf_op jit(solution)/shard_map/all_gather | solution.py:194
  11.0 264.7 %all-gather.12.cloned.1.call-start = ((), (), s32[]{:S(2)}) async-start(), calls=%async_computation.2 | async-start | bytes 4866048 | tf_op jit(solution)/shard_map/all_gather | solution.py:194
  12.7 295.1 %all-gather.14.cloned.1.call-start = ((), (), s32[]{:S(2)}) async-start(), calls=%async_computation.3 | async-start | bytes 4866048 | tf_op jit(solution)/shard_map/all_gather | solution.py:194
  13.4 3.6 collective-permute-start
  14.0 45.5 %collective-permute-start.1 = (bf16[1,24,1536]{2,1,0:T(8,128)(2,1)S(1)}, bf16[1,24,1536]{2,1,0:T(8,128)(2,1)S(1)}, u32[]{:S(2)}, u32[]{:S(2)}) collective-permute-start(bf16[1,24,1536]{2,1,0:T(8,128)(2,1)S(1)} %get-tuple-element.243), channel_id=1, source_target_pairs={{0,1},{1,0},{2,3},{3,2},{4,5},{5,4},{6,7},{7,6},{8,9},{9,8},{10,11... | collective-permute-start | bytes 221192 | tf_op jit(solution)/shard_map/ppermute | solution.py:27
  14.8 45.6 %collective-permute-start.2 = (bf16[1,96,384]{2,1,0:T(8,128)(2,1)S(1)}, bf16[1,96,384]{2,1,0:T(8,128)(2,1)S(1)}, u32[]{:S(2)}, u32[]{:S(2)}) collective-permute-start(bf16[1,96,384]{2,1,0:T(8,128)(2,1)S(1)} %get-tuple-element.241), channel_id=1, source_target_pairs={{0,1},{1,0},{2,3},{3,2},{4,5},{5,4},{6,7},{7,6},{8,9},{9,8},{10,11... | collective-permute-start | bytes 221192 | tf_op jit(solution)/shard_map/ppermute | solution.py:27
  16.0 45.1 %copy-start.62 = (f32[256]{0:T(256)}, f32[256]{0:T(256)S(1)}, u32[]{:S(2)}) copy-start(f32[256]{0:T(256)S(1)} %broadcast_multiply_fusion.11) | copy-start | bytes 3076
  16.3 44.8 %copy-start.72 = (f32[256]{0:T(256)}, f32[256]{0:T(256)S(1)}, u32[]{:S(2)}) copy-start(f32[256]{0:T(256)S(1)} %add_rsqrt_fusion.3) | copy-start | bytes 3076
  59.5 127.0 %copy-start.58 = (f32[768]{0:T(1024)}, f32[768]{0:T(1024)S(1)}, u32[]{:S(2)}) copy-start(f32[768]{0:T(1024)S(1)} %get-tuple-element.142) | copy-start | bytes 9220
  59.5 216.2 %copy-start.60 = (f32[768]{0:T(1024)}, f32[768]{0:T(1024)S(1)}, u32[]{:S(2)}) copy-start(f32[768]{0:T(1024)S(1)} %get-tuple-element.135) | copy-start | bytes 9220
  65.6 88.9 %collective-permute-start.3 = (bf16[576,256]{1,0:T(8,128)(2,1)S(1)}, bf16[576,256]{1,0:T(8,128)(2,1)S(1)}, u32[]{:S(2)}, u32[]{:S(2)}) collective-permute-start(bf16[576,256]{1,0:T(8,128)(2,1)S(1)} %get-tuple-element.195), channel_id=1, source_target_pairs={{0,2},{1,3},{2,0},{3,1},{4,6},{5,7},{6,4},{7,5},{8,10},{9,11},{10,... | collective-permute-start | bytes 884744 | tf_op jit(solution)/shard_map/ppermute | solution.py:27
  65.6 88.9 %collective-permute-start.4 = (bf16[576,256]{1,0:T(8,128)(2,1)S(1)}, bf16[576,256]{1,0:T(8,128)(2,1)S(1)}, u32[]{:S(2)}, u32[]{:S(2)}) collective-permute-start(bf16[576,256]{1,0:T(8,128)(2,1)S(1)} %get-tuple-element.194), channel_id=1, source_target_pairs={{0,4},{1,5},{2,6},{3,7},{4,0},{5,1},{6,2},{7,3},{8,12},{9,13},{10,... | collective-permute-start | bytes 884744 | tf_op jit(solution)/shard_map/ppermute | solution.py:27
  67.4 86.1 %collective-permute-start.5 = (bf16[576,256]{1,0:T(8,128)(2,1)S(1)}, bf16[576,256]{1,0:T(8,128)(2,1)}, u32[]{:S(2)}, u32[]{:S(2)}) collective-permute-start(bf16[576,256]{1,0:T(8,128)(2,1)S(1)} %get-tuple-element.193), channel_id=1, source_target_pairs={{0,6},{1,7},{2,4},{3,5},{4,2},{5,3},{6,0},{7,1},{8,14},{9,15},{10,... | collective-permute-start | bytes 884744 | tf_op jit(solution)/shard_map/ppermute | solution.py:27
  154.7 6.8 collective-permute-start.6
  176.2 6.6 collective-permute-start.9
  176.3 7.8 %collective-permute-start.8 = (bf16[192,256]{1,0:T(8,128)(2,1)S(1)}, bf16[192,256]{1,0:T(8,128)(2,1)S(1)}, u32[]{:S(2)}, u32[]{:S(2)}) collective-permute-start(bf16[192,256]{1,0:T(8,128)(2,1)S(1)} %get-tuple-element.220), channel_id=1, source_target_pairs={{0,4},{1,5},{2,6},{3,7},{4,0},{5,1},{6,2},{7,3},{8,12},{9,13},{10,... | collective-permute-start | bytes 294920 | tf_op jit(solution)/shard_map/ppermute | solution.py:27
  176.4 7.7 %collective-permute-start.7 = (bf16[192,256]{1,0:T(8,128)(2,1)S(1)}, bf16[192,256]{1,0:T(8,128)(2,1)S(1)}, u32[]{:S(2)}, u32[]{:S(2)}) collective-permute-start(bf16[192,256]{1,0:T(8,128)(2,1)S(1)} %get-tuple-element.221), channel_id=1, source_target_pairs={{0,2},{1,3},{2,0},{3,1},{4,6},{5,7},{6,4},{7,5},{8,10},{9,11},{10,... | collective-permute-start | bytes 294920 | tf_op jit(solution)/shard_map/ppermute | solution.py:27
  199.5 14.9 %collective-permute-start.12 = (bf16[576,256]{1,0:T(8,128)(2,1)S(1)}, bf16[576,256]{1,0:T(8,128)(2,1)S(1)}, u32[]{:S(2)}, u32[]{:S(2)}) collective-permute-start(bf16[576,256]{1,0:T(8,128)(2,1)S(1)} %get-tuple-element.189), channel_id=1, source_target_pairs={{0,6},{1,7},{2,4},{3,5},{4,2},{5,3},{6,0},{7,1},{8,14},{9,15},{10,... | collective-permute-start | bytes 884744 | tf_op jit(solution)/shard_map/ppermute | solution.py:27
  202.7 40.6 %collective-permute-start.10 = (bf16[576,256]{1,0:T(8,128)(2,1)S(1)}, bf16[576,256]{1,0:T(8,128)(2,1)S(1)}, u32[]{:S(2)}, u32[]{:S(2)}) collective-permute-start(bf16[576,256]{1,0:T(8,128)(2,1)S(1)} %get-tuple-element.191), channel_id=1, source_target_pairs={{0,2},{1,3},{2,0},{3,1},{4,6},{5,7},{6,4},{7,5},{8,10},{9,11},{10,... | collective-permute-start | bytes 884744 | tf_op jit(solution)/shard_map/ppermute | solution.py:27
  202.7 39.8 %collective-permute-start.11 = (bf16[576,256]{1,0:T(8,128)(2,1)S(1)}, bf16[576,256]{1,0:T(8,128)(2,1)S(1)}, u32[]{:S(2)}, u32[]{:S(2)}) collective-permute-start(bf16[576,256]{1,0:T(8,128)(2,1)S(1)} %get-tuple-element.190), channel_id=1, source_target_pairs={{0,4},{1,5},{2,6},{3,7},{4,0},{5,1},{6,2},{7,3},{8,12},{9,13},{10,... | collective-permute-start | bytes 884744 | tf_op jit(solution)/shard_map/ppermute | solution.py:27
  214.5 31.3 %copy-start.34 = (bf16[576,256]{1,0:T(8,128)(2,1)}, bf16[576,256]{1,0:T(8,128)(2,1)S(1)}, u32[]{:S(2)}) copy-start(bf16[576,256]{1,0:T(8,128)(2,1)S(1)} %collective-permute-done.12.refs_5_.refs_7_) | copy-start | bytes 884740
  243.4 2.4 collective-permute-start.13
  260.8 6.6 collective-permute-start.16
  261.3 11.9 %collective-permute-start.15 = (bf16[192,256]{1,0:T(8,128)(2,1)S(1)}, bf16[192,256]{1,0:T(8,128)(2,1)S(1)}, u32[]{:S(2)}, u32[]{:S(2)}) collective-permute-start(bf16[192,256]{1,0:T(8,128)(2,1)S(1)} %get-tuple-element.212), channel_id=1, source_target_pairs={{0,4},{1,5},{2,6},{3,7},{4,0},{5,1},{6,2},{7,3},{8,12},{9,13},{10,... | collective-permute-start | bytes 294920 | tf_op jit(solution)/shard_map/ppermute | solution.py:27
  261.3 11.9 %collective-permute-start.14 = (bf16[192,256]{1,0:T(8,128)(2,1)S(1)}, bf16[192,256]{1,0:T(8,128)(2,1)S(1)}, u32[]{:S(2)}, u32[]{:S(2)}) collective-permute-start(bf16[192,256]{1,0:T(8,128)(2,1)S(1)} %get-tuple-element.213), channel_id=1, source_target_pairs={{0,2},{1,3},{2,0},{3,1},{4,6},{5,7},{6,4},{7,5},{8,10},{9,11},{10,... | collective-permute-start | bytes 294920 | tf_op jit(solution)/shard_map/ppermute | solution.py:27
  275.4 44.7 %copy-start.70 = (f32[256]{0:T(256)}, f32[256]{0:T(256)S(1)}, u32[]{:S(2)}) copy-start(f32[256]{0:T(256)S(1)} %broadcast_multiply_fusion.8) | copy-start | bytes 3076
  275.7 44.5 %copy-start.83 = (f32[256]{0:T(256)}, f32[256]{0:T(256)S(1)}, u32[]{:S(2)}) copy-start(f32[256]{0:T(256)S(1)} %add_rsqrt_fusion) | copy-start | bytes 3076
  322.1 42.7 %collective-permute-start.21 = (bf16[3072,384]{1,0:T(8,128)(2,1)}, bf16[3072,384]{1,0:T(8,128)(2,1)}, u32[]{:S(2)}, u32[]{:S(2)}) collective-permute-start(bf16[3072,384]{1,0:T(8,128)(2,1)} %convolution_convert_fusion.1), channel_id=1, source_target_pairs={{0,1},{1,0},{2,3},{3,2},{4,5},{5,4},{6,7},{7,6},{8,9},{9,8},{10,11... | collective-permute-start | bytes 7077896 | tf_op jit(solution)/shard_map/ppermute | solution.py:27
  323.9 12.0 %copy-start.77 = (f32[768]{0:T(1024)S(1)}, f32[768]{0:T(1024)}, u32[]{:S(2)}) copy-start(f32[768]{0:T(1024)} %get-tuple-element.197) | copy-start | bytes 9220
  323.9 12.7 %collective-permute-start.17 = (bf16[192,256]{1,0:T(8,128)(2,1)}, bf16[192,256]{1,0:T(8,128)(2,1)S(1)}, u32[]{:S(2)}, u32[]{:S(2)}) collective-permute-start(bf16[192,256]{1,0:T(8,128)(2,1)} %get-tuple-element.204), channel_id=1, source_target_pairs={{0,2},{1,3},{2,0},{3,1},{4,6},{5,7},{6,4},{7,5},{8,10},{9,11},{10,... | collective-permute-start | bytes 294920 | tf_op jit(solution)/shard_map/ppermute | solution.py:27
  325.4 11.7 %collective-permute-start.18 = (bf16[192,256]{1,0:T(8,128)(2,1)}, bf16[192,256]{1,0:T(8,128)(2,1)S(1)}, u32[]{:S(2)}, u32[]{:S(2)}) collective-permute-start(bf16[192,256]{1,0:T(8,128)(2,1)} %get-tuple-element.203), channel_id=1, source_target_pairs={{0,4},{1,5},{2,6},{3,7},{4,0},{5,1},{6,2},{7,3},{8,12},{9,13},{10,... | collective-permute-start | bytes 294920 | tf_op jit(solution)/shard_map/ppermute | solution.py:27
  326.2 10.9 %collective-permute-start.19 = (bf16[192,256]{1,0:T(8,128)(2,1)}, bf16[192,256]{1,0:T(8,128)(2,1)S(1)}, u32[]{:S(2)}, u32[]{:S(2)}) collective-permute-start(bf16[192,256]{1,0:T(8,128)(2,1)} %get-tuple-element.202), channel_id=1, source_target_pairs={{0,6},{1,7},{2,4},{3,5},{4,2},{5,3},{6,0},{7,1},{8,14},{9,15},{10,... | collective-permute-start | bytes 294920 | tf_op jit(solution)/shard_map/ppermute | solution.py:27
  331.9 39.4 %collective-permute-start.22 = (bf16[768,1536]{1,0:T(8,128)(2,1)}, bf16[768,1536]{1,0:T(8,128)(2,1)}, u32[]{:S(2)}, u32[]{:S(2)}) collective-permute-start(bf16[768,1536]{1,0:T(8,128)(2,1)} %convolution_convert_fusion.5), channel_id=1, source_target_pairs={{0,1},{1,0},{2,3},{3,2},{4,5},{5,4},{6,7},{7,6},{8,9},{9,8},{10,11... | collective-permute-start | bytes 7077896 | tf_op jit(solution)/shard_map/ppermute | solution.py:27
  336.6 25.4 %collective-permute-start.23 = (bf16[768,384]{1,0:T(8,128)(2,1)}, bf16[768,384]{1,0:T(8,128)(2,1)}, u32[]{:S(2)}, u32[]{:S(2)}) collective-permute-start(bf16[768,384]{1,0:T(8,128)(2,1)} %convolution_convert_fusion.7), channel_id=1, source_target_pairs={{0,1},{1,0},{2,3},{3,2},{4,5},{5,4},{6,7},{7,6},{8,9},{9,8},{10,11... | collective-permute-start | bytes 1769480 | tf_op jit(solution)/shard_map/ppermute | solution.py:27
  337.8 18.2 %copy-start.86 = (f32[768]{0:T(1024)S(1)}, f32[768]{0:T(1024)}, u32[]{:S(2)}) copy-start(f32[768]{0:T(1024)} %get-tuple-element.134) | copy-start | bytes 9220
  352.1 12.2 %collective-permute-start.20 = (bf16[4,384,256]{2,1,0:T(8,128)(2,1)}, bf16[4,384,256]{2,1,0:T(8,128)(2,1)S(1)}, u32[]{:S(2)}, u32[]{:S(2)}) collective-permute-start(bf16[4,384,256]{2,1,0:T(8,128)(2,1)} %bitcast.424), channel_id=1, source_target_pairs={{0,1},{1,0},{2,3},{3,2},{4,5},{5,4},{6,7},{7,6},{8,9},{9,8},{10,11... | collective-permute-start | bytes 2359304 | tf_op jit(solution)/shard_map/ppermute | solution.py:27
  375.5 64.2 %collective-permute-start.26 = (bf16[576,256]{1,0:T(8,128)(2,1)S(1)}, bf16[576,256]{1,0:T(8,128)(2,1)S(1)}, u32[]{:S(2)}, u32[]{:S(2)}) collective-permute-start(bf16[576,256]{1,0:T(8,128)(2,1)S(1)} %get-tuple-element.186), channel_id=1, source_target_pairs={{0,6},{1,7},{2,4},{3,5},{4,2},{5,3},{6,0},{7,1},{8,14},{9,15},{10,... | collective-permute-start | bytes 884744 | tf_op jit(solution)/shard_map/ppermute | solution.py:27
  377.2 62.5 %collective-permute-start.25 = (bf16[576,256]{1,0:T(8,128)(2,1)S(1)}, bf16[576,256]{1,0:T(8,128)(2,1)S(1)}, u32[]{:S(2)}, u32[]{:S(2)}) collective-permute-start(bf16[576,256]{1,0:T(8,128)(2,1)S(1)} %get-tuple-element.187), channel_id=1, source_target_pairs={{0,4},{1,5},{2,6},{3,7},{4,0},{5,1},{6,2},{7,3},{8,12},{9,13},{10,... | collective-permute-start | bytes 884744 | tf_op jit(solution)/shard_map/ppermute | solution.py:27
  377.6 62.2 %collective-permute-start.24 = (bf16[576,256]{1,0:T(8,128)(2,1)S(1)}, bf16[576,256]{1,0:T(8,128)(2,1)}, u32[]{:S(2)}, u32[]{:S(2)}) collective-permute-start(bf16[576,256]{1,0:T(8,128)(2,1)S(1)} %get-tuple-element.188), channel_id=1, source_target_pairs={{0,2},{1,3},{2,0},{3,1},{4,6},{5,7},{6,4},{7,5},{8,10},{9,11},{10,... | collective-permute-start | bytes 884744 | tf_op jit(solution)/shard_map/ppermute | solution.py:27
  460.0 20.7 %collective-permute-start.27 = (bf16[192,256]{1,0:T(8,128)(2,1)}, bf16[192,256]{1,0:T(8,128)(2,1)}, u32[]{:S(2)}, u32[]{:S(2)}) collective-permute-start(bf16[192,256]{1,0:T(8,128)(2,1)} %get-tuple-element.200), channel_id=1, source_target_pairs={{0,2},{1,3},{2,0},{3,1},{4,6},{5,7},{6,4},{7,5},{8,10},{9,11},{10,... | collective-permute-start | bytes 294920 | tf_op jit(solution)/shard_map/ppermute | solution.py:27
  460.2 21.8 %collective-permute-start.28 = (bf16[192,256]{1,0:T(8,128)(2,1)}, bf16[192,256]{1,0:T(8,128)(2,1)}, u32[]{:S(2)}, u32[]{:S(2)}) collective-permute-start(bf16[192,256]{1,0:T(8,128)(2,1)} %get-tuple-element.199), channel_id=1, source_target_pairs={{0,4},{1,5},{2,6},{3,7},{4,0},{5,1},{6,2},{7,3},{8,12},{9,13},{10,... | collective-permute-start | bytes 294920 | tf_op jit(solution)/shard_map/ppermute | solution.py:27
  462.4 53.3 %collective-permute-start.31 = (bf16[3072,384]{1,0:T(8,128)(2,1)}, bf16[3072,384]{1,0:T(8,128)(2,1)}, u32[]{:S(2)}, u32[]{:S(2)}) collective-permute-start(bf16[3072,384]{1,0:T(8,128)(2,1)} %convolution_convert_fusion), channel_id=1, source_target_pairs={{0,1},{1,0},{2,3},{3,2},{4,5},{5,4},{6,7},{7,6},{8,9},{9,8},{10,11... | collective-permute-start | bytes 7077896 | tf_op jit(solution)/shard_map/ppermute | solution.py:27
  465.9 12.8 %collective-permute-start.43 = (f32[24,384]{1,0:T(8,128)}, f32[24,384]{1,0:T(8,128)}, u32[]{:S(2)}, u32[]{:S(2)}) collective-permute-start(f32[24,384]{1,0:T(8,128)} %get-tuple-element.249), channel_id=1, source_target_pairs={{0,1},{1,0},{2,3},{3,2},{4,5},{5,4},{6,7},{7,6},{8,9},{9,8},{10,11... | collective-permute-start | bytes 110600 | tf_op jit(solution)/shard_map/ppermute | solution.py:27
  468.1 17.9 %collective-permute-start.45 = (f32[24,1536]{1,0:T(8,128)}, f32[24,1536]{1,0:T(8,128)S(1)}, u32[]{:S(2)}, u32[]{:S(2)}) collective-permute-start(f32[24,1536]{1,0:T(8,128)} %get-tuple-element.229), channel_id=1, source_target_pairs={{0,1},{1,0},{2,3},{3,2},{4,5},{5,4},{6,7},{7,6},{8,9},{9,8},{10,11... | collective-permute-start | bytes 442376 | tf_op jit(solution)/shard_map/ppermute | solution.py:27
  478.7 7.3 %collective-permute-start.29 = (bf16[192,256]{1,0:T(8,128)(2,1)}, bf16[192,256]{1,0:T(8,128)(2,1)S(1)}, u32[]{:S(2)}, u32[]{:S(2)}) collective-permute-start(bf16[192,256]{1,0:T(8,128)(2,1)} %get-tuple-element.198), channel_id=1, source_target_pairs={{0,6},{1,7},{2,4},{3,5},{4,2},{5,3},{6,0},{7,1},{8,14},{9,15},{10,... | collective-permute-start | bytes 294920 | tf_op jit(solution)/shard_map/ppermute | solution.py:27
  480.7 30.8 %collective-permute-start.34 = (bf16[768,1152]{1,0:T(8,128)(2,1)}, bf16[768,1152]{1,0:T(8,128)(2,1)}, u32[]{:S(2)}, u32[]{:S(2)}) collective-permute-start(bf16[768,1152]{1,0:T(8,128)(2,1)} %convolution_convert_fusion.3), channel_id=1, source_target_pairs={{0,1},{1,0},{2,3},{3,2},{4,5},{5,4},{6,7},{7,6},{8,9},{9,8},{10,11... | collective-permute-start | bytes 5308424 | tf_op jit(solution)/shard_map/ppermute | solution.py:27
  482.0 38.8 %collective-permute-start.32 = (bf16[768,1536]{1,0:T(8,128)(2,1)}, bf16[768,1536]{1,0:T(8,128)(2,1)}, u32[]{:S(2)}, u32[]{:S(2)}) collective-permute-start(bf16[768,1536]{1,0:T(8,128)(2,1)} %convolution_convert_fusion.4), channel_id=1, source_target_pairs={{0,1},{1,0},{2,3},{3,2},{4,5},{5,4},{6,7},{7,6},{8,9},{9,8},{10,11... | collective-permute-start | bytes 7077896 | tf_op jit(solution)/shard_map/ppermute | solution.py:27
  486.0 22.6 %collective-permute-start.33 = (bf16[768,384]{1,0:T(8,128)(2,1)}, bf16[768,384]{1,0:T(8,128)(2,1)}, u32[]{:S(2)}, u32[]{:S(2)}) collective-permute-start(bf16[768,384]{1,0:T(8,128)(2,1)} %convolution_convert_fusion.6), channel_id=1, source_target_pairs={{0,1},{1,0},{2,3},{3,2},{4,5},{5,4},{6,7},{7,6},{8,9},{9,8},{10,11... | collective-permute-start | bytes 1769480 | tf_op jit(solution)/shard_map/ppermute | solution.py:27
  486.0 15.2 %copy-start.31 = (f32[24,1536]{1,0:T(8,128)}, f32[24,1536]{1,0:T(8,128)S(1)}, u32[]{:S(2)}) copy-start(f32[24,1536]{1,0:T(8,128)S(1)} %collective-permute-done.45) | copy-start | bytes 442372
  486.0 15.2 %collective-permute-start.47 = (f32[96,384]{1,0:T(8,128)S(1)}, f32[96,384]{1,0:T(8,128)}, u32[]{:S(2)}, u32[]{:S(2)}) collective-permute-start(f32[96,384]{1,0:T(8,128)S(1)} %get-tuple-element.225), channel_id=1, source_target_pairs={{0,1},{1,0},{2,3},{3,2},{4,5},{5,4},{6,7},{7,6},{8,9},{9,8},{10,11... | collective-permute-start | bytes 442376 | tf_op jit(solution)/shard_map/ppermute | solution.py:27
  501.3 9.9 %collective-permute-start.30 = (bf16[4,384,256]{2,1,0:T(8,128)(2,1)}, bf16[4,384,256]{2,1,0:T(8,128)(2,1)S(1)}, u32[]{:S(2)}, u32[]{:S(2)}) collective-permute-start(bf16[4,384,256]{2,1,0:T(8,128)(2,1)} %bitcast.423), channel_id=1, source_target_pairs={{0,1},{1,0},{2,3},{3,2},{4,5},{5,4},{6,7},{7,6},{8,9},{9,8},{10,11... | collective-permute-start | bytes 2359304 | tf_op jit(solution)/shard_map/ppermute | solution.py:27
  525.0 79.7 %collective-permute-start.37 = (bf16[576,256]{1,0:T(8,128)(2,1)S(1)}, bf16[576,256]{1,0:T(8,128)(2,1)S(1)}, u32[]{:S(2)}, u32[]{:S(2)}) collective-permute-start(bf16[576,256]{1,0:T(8,128)(2,1)S(1)} %get-tuple-element.178), channel_id=1, source_target_pairs={{0,6},{1,7},{2,4},{3,5},{4,2},{5,3},{6,0},{7,1},{8,14},{9,15},{10,... | collective-permute-start | bytes 884744 | tf_op jit(solution)/shard_map/ppermute | solution.py:27
  526.9 77.8 %collective-permute-start.36 = (bf16[576,256]{1,0:T(8,128)(2,1)S(1)}, bf16[576,256]{1,0:T(8,128)(2,1)S(1)}, u32[]{:S(2)}, u32[]{:S(2)}) collective-permute-start(bf16[576,256]{1,0:T(8,128)(2,1)S(1)} %get-tuple-element.179), channel_id=1, source_target_pairs={{0,4},{1,5},{2,6},{3,7},{4,0},{5,1},{6,2},{7,3},{8,12},{9,13},{10,... | collective-permute-start | bytes 884744 | tf_op jit(solution)/shard_map/ppermute | solution.py:27
  527.4 77.4 %collective-permute-start.35 = (bf16[576,256]{1,0:T(8,128)(2,1)S(1)}, bf16[576,256]{1,0:T(8,128)(2,1)S(1)}, u32[]{:S(2)}, u32[]{:S(2)}) collective-permute-start(bf16[576,256]{1,0:T(8,128)(2,1)S(1)} %get-tuple-element.180), channel_id=1, source_target_pairs={{0,2},{1,3},{2,0},{3,1},{4,6},{5,7},{6,4},{7,5},{8,10},{9,11},{10,... | collective-permute-start | bytes 884744 | tf_op jit(solution)/shard_map/ppermute | solution.py:27
  610.1 12.7 %copy-start.3 = (f32[256,768]{1,0:T(8,128)S(1)}, f32[256,768]{1,0:T(8,128)}, u32[]{:S(2)}) copy-start(f32[256,768]{1,0:T(8,128)} %copy-done.2) | copy-start | bytes 2359300
  613.7 21.5 %collective-permute-start.38 = (bf16[768,1152]{1,0:T(8,128)(2,1)}, bf16[768,1152]{1,0:T(8,128)(2,1)}, u32[]{:S(2)}, u32[]{:S(2)}) collective-permute-start(bf16[768,1152]{1,0:T(8,128)(2,1)} %convolution_convert_fusion.2), channel_id=1, source_target_pairs={{0,1},{1,0},{2,3},{3,2},{4,5},{5,4},{6,7},{7,6},{8,9},{9,8},{10,11... | collective-permute-start | bytes 5308424 | tf_op jit(solution)/shard_map/ppermute | solution.py:27
  614.3 13.6 %copy-start.30 = (f32[1,24,768]{2,1,0:T(8,128)S(1)}, f32[1,24,768]{2,1,0:T(8,128)}, u32[]{:S(2)}) copy-start(f32[1,24,768]{2,1,0:T(8,128)} %maximum_select_fusion.10) | copy-start | bytes 221188
  617.1 11.4 %collective-permute-start.39 = (f32[16,8,128]{2,1,0:T(8,128)}, f32[16,8,128]{2,1,0:T(8,128)}, u32[]{:S(2)}, u32[]{:S(2)}) collective-permute-start(f32[16,8,128]{2,1,0:T(8,128)} %dynamic-slice_bitcast_fusion.40), channel_id=1, source_target_pairs={{0,1},{1,0},{2,3},{3,2},{4,5},{5,4},{6,7},{7,6},{8,9},{9,8},{10,11... | collective-permute-start | bytes 196616 | tf_op jit(solution)/shard_map/ppermute | solution.py:27
  619.2 10.7 %collective-permute-start.41 = (f32[24,1152]{1,0:T(8,128)}, f32[24,1152]{1,0:T(8,128)}, u32[]{:S(2)}, u32[]{:S(2)}) collective-permute-start(f32[24,1152]{1,0:T(8,128)} %get-tuple-element.237), channel_id=1, source_target_pairs={{0,1},{1,0},{2,3},{3,2},{4,5},{5,4},{6,7},{7,6},{8,9},{9,8},{10,11... | collective-permute-start | bytes 331784 | tf_op jit(solution)/shard_map/ppermute | solution.py:27
  620.6 6.6 collective-permute-start.42
  622.8 10.5 %collective-permute-start.44 = (f32[24,1536]{1,0:T(8,128)}, f32[24,1536]{1,0:T(8,128)}, u32[]{:S(2)}, u32[]{:S(2)}) collective-permute-start(f32[24,1536]{1,0:T(8,128)} %get-tuple-element.227), channel_id=1, source_target_pairs={{0,1},{1,0},{2,3},{3,2},{4,5},{5,4},{6,7},{7,6},{8,9},{9,8},{10,11... | collective-permute-start | bytes 442376 | tf_op jit(solution)/shard_map/ppermute | solution.py:27
  627.2 4.2 collective-permute-start.46
  670.9 2.1 collective-permute-start.40
  (106 other events, 509.2 us)
Sparse Core Ops, SparseCore 0:
  11.7 75.9 all-gather.7
  90.7 66.5 all-gather.9
  160.9 77.5 all-gather.11
  241.9 65.9 all-gather.13

commit v4 on v3

--- a/solution.py
+++ b/solution.py
@@ -100,8 +100,8 @@
         return [
             (slice(0, rows), slice(at, min(at + step, columns))) for at in range(0, columns, step)
         ]
-    step = max(16, most // columns // 16 * 16)
-    return [(slice(at, min(at + step, rows)), slice(0, columns)) for at in range(0, rows, step)]
+    step = rows // 2
+    return [(slice(at, at + step), slice(0, columns)) for at in (0, step)]
 
 
 def span(part, base=0):
@@ -198,10 +198,12 @@
     parts, outs = refs[:count], refs[count : 2 * count]
     items = len(pieces)
     refs = refs[2 * count :]
-    sums, landed = refs[:items], refs[items : 2 * items]
-    leave, arrive = refs[2 * items :]
+    joint, sums, landed = refs[:items], refs[items : 2 * items], refs[2 * items : 3 * items]
+    done = refs[3 * items : 3 * items + count]
+    give, take, leave, arrive, back_leave, back_arrive, place_sem = refs[3 * items + count :]
     route = Route(phases, chips)
-    route.meet(False)
+    route.meet(True)
+    core = route.core
     slots = 1 << phases
 
     def bit_of(s):
@@ -217,9 +219,15 @@
     def seat(p, s):
         return slots - (slots >> p) + (s >> (p + 1))
 
-    def term(n, s, k):
+    def mine(n, side, row):
         w, rows, columns = pieces[n]
-        return parts[w].at[route.row(s, k, route.core), span(rows), span(columns)]
+        if len(parts[w].shape) == 4:
+            return parts[w].at[row, side]
+        return parts[w].at[row, span(rows), span(columns, side * (parts[w].shape[-1] // 2))]
+
+    def chip_sum(n, s, k):
+        row = route.row(s, k, core)
+        return mine(n, core, row)[...].astype(jnp.float32) + joint[n][row].astype(jnp.float32)
 
     travels, waiting = {}, []
 
@@ -228,17 +236,27 @@
             n, p, s, k = waiting.pop()
             place = (seat(p, s ^ 1 << p), k) if p < phases else (slots - 1, k)
             travels[n, p, place] = send(
-                term(n, s, k) if p == 0 else sums[n].at[s >> 1, k],
+                joint[n].at[route.row(s, k, core)] if p == 0 else sums[n].at[s >> 1, k],
                 landed[n].at[place],
                 leave.at[(n, *place)],
                 arrive.at[(n, *place)],
                 route.phase_partner(p) if p < phases else route.chip_partner(k),
             )
 
+    gifts = [
+        send(
+            mine(n, 1 - core, slice(None)), joint[n], give.at[n], take.at[n], route.core_partner()
+        )
+        for n in range(items)
+    ]
     for n in range(items):
+        gifts[n].wait_recv()
         for s, k in order([s for s in range(slots) if s % 2 == 0]):
+            added = chip_sum(n, s ^ 1, k)
+            flush()
+            joint[n][route.row(s ^ 1, k, core)] = added.astype(joint[n].dtype)
             waiting.append((n, 0, s ^ 1, k))
-            flush()
+    flush()
     for n in range(items):
         for p in range(phases):
             for s, k in order([s for s in range(slots) if bit_of(s) > p]):
@@ -246,22 +264,51 @@
                 travels[n, p, place].wait_recv()
                 if p == phases - 1 and k == 0:
                     continue
-                before = term(n, s, k)[...] if p == 0 else sums[n][s >> 1, k]
-                added = before.astype(jnp.float32) + landed[n][place].astype(jnp.float32)
+                before = chip_sum(n, s, k) if p == 0 else sums[n][s >> 1, k].astype(jnp.float32)
+                added = before + landed[n][place].astype(jnp.float32)
                 flush()
-                sums[n][s >> 1, k] = added.astype(before.dtype)
+                sums[n][s >> 1, k] = added.astype(sums[n].dtype)
                 if bit_of(s) == p + 1 and (s or k):
                     waiting.append((n, p + 1, s, k))
             flush()
+    trades, placed = [], []
     for n, (w, rows, columns) in enumerate(pieces):
         last = (seat(phases - 1, 0), 0)
-        before = term(n, 0, 0)[...] if phases == 1 else sums[n][0, 0]
-        total = before.astype(jnp.float32) + landed[n][last].astype(jnp.float32)
+        before = chip_sum(n, 0, 0) if phases == 1 else sums[n][0, 0].astype(jnp.float32)
+        total = before + landed[n][last].astype(jnp.float32)
         for k in range(1, chips):
             place = (slots - 1, k)
             travels[n, phases, place].wait_recv()
             total = total + landed[n][place].astype(jnp.float32)
-        outs[w][rows, columns] = total
+        if len(parts[w].shape) == 4:
+            outs[w][...] = total
+            continue
+        own = outs[w].shape[0]
+        for side in range(2):
+            first, final = max(rows.start, side * own), min(rows.stop, (side + 1) * own)
+            if first < final:
+                done[w][side, first - side * own : final - side * own, columns] = total[
+                    first - rows.start : final - rows.start
+                ]
+    for w in range(count):
+        if len(parts[w].shape) == 4:
+            continue
+        half = done[w].shape[2]
+        target = outs[w].at[:, span(slice(0, half), core * half)]
+        trades.append(
+            send(
+                done[w].at[1 - core], target, back_leave.at[w], back_arrive.at[w], route.core_partner()
+            )
+        )
+        copy = pltpu.make_async_copy(done[w].at[core], target, place_sem.at[w])
+        copy.start()
+        placed.append(copy)
+    for copy in placed:
+        copy.wait()
+    for copy in trades:
+        copy.wait()
+    for copy in gifts:
+        copy.wait_send()
     for copy in travels.values():
         copy.wait_send()
 
@@ -270,19 +317,32 @@
     dp_size, chips = lax.axis_size("dp"), lax.axis_size("ctx") // 2
     phases, count = dp_size.bit_length() - 1, len(parts)
     slots = 1 << phases
-    pieces = [(w, *piece) for w, part in enumerate(parts) for piece in cut(part.shape[1:], 36864)]
+    pieces, outs, held = [], [], []
+    for w, part in enumerate(parts):
+        if part.ndim == 4:
+            shape, out = part.shape[2:], part.shape[2:]
+            held.append((1, 8, 128))
+        else:
+            shape, out = (part.shape[1], part.shape[2] // 2), (part.shape[1] // 2, part.shape[2])
+            held.append((2, out[0], shape[1]))
+        pieces += [(w, *piece) for piece in cut(shape, 36864)]
+        outs.append(jax.ShapeDtypeStruct(out, jnp.float32))
     sizes = [
         ((rows.stop - rows.start, columns.stop - columns.start), parts[w].dtype)
         for w, rows, columns in pieces
     ]
     return pl.pallas_call(
         functools.partial(reduce_kernel, phases, chips, count, pieces),
-        out_shape=tuple(jax.ShapeDtypeStruct(part.shape[1:], jnp.float32) for part in parts),
+        out_shape=tuple(outs),
         in_specs=[pl.BlockSpec(memory_space=pltpu.VMEM)] * count,
         out_specs=(pl.BlockSpec(memory_space=pltpu.VMEM),) * count,
-        scratch_shapes=[pltpu.VMEM((slots // 2, chips, *size), dtype) for size, dtype in sizes]
+        scratch_shapes=[pltpu.VMEM((slots * chips, *size), dtype) for size, dtype in sizes]
+        + [pltpu.VMEM((slots // 2, chips, *size), dtype) for size, dtype in sizes]
         + [pltpu.VMEM((slots, chips, *size), dtype) for size, dtype in sizes]
-        + [pltpu.SemaphoreType.DMA((len(pieces), slots, chips))] * 2,
+        + [pltpu.VMEM(shape, jnp.float32) for shape in held]
+        + [pltpu.SemaphoreType.DMA((len(pieces),))] * 2
+        + [pltpu.SemaphoreType.DMA((len(pieces), slots, chips))] * 2
+        + [pltpu.SemaphoreType.DMA((count,))] * 3,
         compiler_params=pltpu.CompilerParams(collective_id=collective_id, has_side_effects=True),
         cost_estimate=pl.CostEstimate(
             flops=15 * 10**9 * count, transcendentals=0, bytes_accessed=10**6 * count
@@ -300,29 +360,10 @@
     )
 
 
-def chip_part(left, right, left_dim=0, right_dim=0):
-    dp_size, chips = lax.axis_size("dp"), lax.axis_size("ctx") // 2
-    core = lax.axis_index("ctx") % 2
-    half = right.shape[1 - right_dim] // 2
-    own_side = lax.dynamic_slice_in_dim(right, core * half, half, 1 - right_dim)
-    far_side = lax.dynamic_slice_in_dim(right, (1 - core) * half, half, 1 - right_dim)
-    got = swap(contract(left, far_side, left_dim, right_dim).astype(jnp.bfloat16), 0, 1)
-    part = (contract(left, own_side, left_dim, right_dim) + got.astype(jnp.float32)).astype(
-        jnp.bfloat16
-    )
-    return part.reshape(dp_size * chips, -1, half)
-
-
-def device_rows(total):
-    core = lax.axis_index("ctx") % 2
-    total = total.reshape(2, -1, total.shape[1])
-    got = swap(pick(total, 1 - core, 0), 0, 1)
-    kept = pick(total, core, 0)
-    return jnp.where(
-        core == 0,
-        jnp.concatenate([kept, got], axis=1),
-        jnp.concatenate([got, kept], axis=1),
-    )
+def weight_term(left, right, left_dim=0, right_dim=0):
+    chips_in_all = lax.axis_size("dp") * lax.axis_size("ctx") // 2
+    term = contract(left, right, left_dim, right_dim).astype(jnp.bfloat16)
+    return term.reshape(chips_in_all, -1, term.shape[1])
 
 
 def layer_norm(residual, norm_gain, norm_bias):
@@ -367,6 +408,15 @@
     return lax.dot_general(
         left, right, (((left_dim,), (right_dim,)), ((), ())), preferred_element_type=jnp.float32
     )
+
+
+def starts_kernel(ids_ref, starts_ref):
+    ids = ids_ref[...]
+    starts = jnp.zeros_like(ids)
+    for number in range(1, DOCS):
+        before = jnp.sum(jnp.where(ids < number, 1.0, 0.0), axis=(0, 1), keepdims=True)
+        starts = jnp.where(ids == number, before, starts)
+    starts_ref[...] = starts.astype(jnp.int32)
 
 
 def allowed_keys(key_chunk, starts, length, own):
@@ -509,10 +559,12 @@
             far_ref[j - 1, k] = totals[chunk + (share ^ j)].astype(far_ref.dtype)
 
 
-def spread(grouped, parts, shares):
+def spread(grouped, parts, shares, axis=0):
     part = lax.axis_index("ctx") // shares
     return [
-        pick(grouped, part ^ k, 0) if k == 0 else swap(pick(grouped, part ^ k, 0), 0, shares * k)
+        pick(grouped, part ^ k, axis)
+        if k == 0
+        else swap(pick(grouped, part ^ k, axis), 0, shares * k)
         for k in range(parts)
     ]
 
@@ -520,7 +572,7 @@
 def collect(pieces, parts, shares):
     part = lax.axis_index("ctx") // shares
     held = jnp.stack([p if k == 0 else swap(p, 0, shares * k) for k, p in enumerate(pieces)])
-    return jnp.concatenate([pick(held, part ^ j, 0) for j in range(parts)])
+    return [pick(held, part ^ j, 0) for j in range(parts)]
 
 
 def attend(mine, theirs, starts, first, parts, shares):
@@ -586,30 +638,27 @@
     return grad_queries, own, far
 
 
-def forward_layer(residual, narrow, joined, held, plan, near):
+def forward_layer(residual, narrow, joined, held, plan, collective_id):
     starts, first, parts, shares, qkv_scale = plan
     width = residual.shape[1]
     normed_in, normed1, inv_std1 = layer_norm(residual, narrow["gain1"], narrow["bias1"])
     attn_in = normed_in.astype(jnp.bfloat16)
     qkv_weight, out_weight = joined
     projected = (contract(qkv_weight, attn_in, 0, 1) + narrow["qkv"][:, None]) * qkv_scale[:, None]
-    grouped = projected.astype(jnp.bfloat16).reshape(parts, -1, residual.shape[0])
-    if not near:
-        mine = spread(grouped, parts, shares)
-        fc_weight, proj_weight = held
-    else:
-        grouped, held = lax.optimization_barrier((grouped, held))
-        mine = spread(grouped, parts, shares)
-        fc_weight, proj_weight = gather_many(held, 2)
+    grouped = projected.astype(jnp.bfloat16).reshape(3, parts, -1, residual.shape[0])
+    own, here = held
+    grouped, here = lax.optimization_barrier((grouped, here))
+    mine = [
+        piece.reshape(-1, residual.shape[0]) for piece in spread(grouped, parts, shares, axis=1)
+    ]
+    gathered = gather_many(here, collective_id)
+    mine, gathered = lax.optimization_barrier((mine, gathered))
     joint = jnp.stack([piece[width // parts :] for piece in mine])
     theirs = jnp.stack([swap(joint, 0, j) for j in range(1, shares)])
-    if near:
-        mine, theirs, fc_weight, proj_weight = lax.optimization_barrier(
-            (mine, theirs, fc_weight, proj_weight)
-        )
+    fc_weight, proj_weight = (*gathered, *own)
     mixed, logs = attend(mine, theirs, starts, first, parts, shares)
     kept = (mixed, logs, mine, theirs)
-    mixed_columns = collect([mixed[k] for k in range(parts)], parts, shares)
+    mixed_columns = jnp.concatenate(collect([mixed[k] for k in range(parts)], parts, shares))
     fc_weight = fc_weight.reshape(width, -1)
     proj_weight = proj_weight.reshape(-1, width)
     middle = residual + contract(mixed_columns, out_weight, 0, 0) + narrow["out"]
@@ -632,19 +681,19 @@
     ) = saved
     starts, first, parts, shares, _ = plan
     grad_narrow = grad_residual.astype(jnp.bfloat16)
-    grad_proj_w = chip_part(hidden, grad_narrow)
+    grad_proj_w = weight_term(hidden, grad_narrow)
     grad_proj_b = jnp.sum(grad_residual, axis=0)
     grad_hidden = contract(grad_narrow, proj_weight, 1, 1)
     grad_pre = grad_hidden * gelu_slope(pre_act)
     pre_narrow = grad_pre.astype(jnp.bfloat16)
-    grad_fc_w = chip_part(ffn_in, pre_narrow)
+    grad_fc_w = weight_term(ffn_in, pre_narrow)
     grad_fc_b = jnp.sum(grad_pre, axis=0)
     grad_norm2 = contract(pre_narrow, fc_weight, 1, 1)
     grad_gain2 = jnp.sum(grad_norm2 * normed2, axis=0)
     grad_bias2 = jnp.sum(grad_norm2, axis=0)
     grad_middle = grad_residual + norm_back(grad_norm2, normed2, inv_std2, narrow["gain2"])
     middle_narrow = grad_middle.astype(jnp.bfloat16)
-    grad_out_w = chip_part(mixed_columns, middle_narrow, left_dim=1)
+    grad_out_w = weight_term(mixed_columns, middle_narrow, left_dim=1)
     grad_out_b = jnp.sum(grad_middle, axis=0)
     grad_mixed = contract(out_weight, middle_narrow, 1, 1).astype(jnp.bfloat16)
     grad_mixed = grad_mixed.reshape(parts, -1, grad_mixed.shape[1])
@@ -655,11 +704,14 @@
     joint = jnp.concatenate([grad_queries, own.astype(jnp.bfloat16)], axis=1)
     terms = [grad_proj_w, grad_fc_w, grad_out_w, *carried]
     joint, terms = lax.optimization_barrier((joint, terms))
-    grad_qkv = collect([joint[k] for k in range(parts)], parts, shares)
+    length = joint.shape[2]
+    pieces = collect([joint[k] for k in range(parts)], parts, shares)
+    grad_qkv = jnp.stack([piece.reshape(3, -1, length) for piece in pieces], axis=1)
+    grad_qkv = grad_qkv.reshape(-1, length)
     sums = reduce_many(terms, 4 + len(carried))
     grad_qkv, sums = lax.optimization_barrier((grad_qkv, sums))
-    grad_qkv_w = chip_part(attn_in, grad_qkv, right_dim=1)
-    grad_qkv_b = jnp.sum(grad_qkv.astype(jnp.float32), axis=1).reshape(parts, 3, -1)
+    grad_qkv_w = weight_term(attn_in, grad_qkv, right_dim=1)
+    grad_qkv_b = jnp.sum(grad_qkv.astype(jnp.float32), axis=1).reshape(3, -1)
     grad_norm1 = contract(grad_qkv, qkv_weight, 0, 1)
     grad_gain1 = jnp.sum(grad_norm1 * normed1, axis=0)
     grad_bias1 = jnp.sum(grad_norm1, axis=0)
@@ -667,24 +719,14 @@
     vectors = (
         grad_gain1,
         grad_bias1,
-        grad_qkv_b[:, 0].reshape(-1),
-        grad_qkv_b[:, 2].reshape(-1),
+        grad_qkv_b[0],
+        grad_qkv_b[2],
         grad_out_b,
         grad_gain2,
         grad_bias2,
         grad_proj_b,
     )
     return grad_before, grad_qkv_w, sums, vectors, grad_fc_b
-
-
-def by_part(columns, parts):
-    rows = columns.shape[0]
-    return jnp.swapaxes(columns.reshape(rows, 3, parts, -1), 1, 2).reshape(rows, -1)
-
-
-def by_kind(columns, parts):
-    rows = columns.shape[0]
-    return jnp.swapaxes(columns.reshape(rows, parts, 3, -1), 1, 2).reshape(rows, -1)
 
 
 def shards(
@@ -725,22 +767,22 @@
             jnp.zeros((packed_size - used - row_count,), jnp.bfloat16),
         ]
     )
-    joined_pieces = chip_rows(jnp.concatenate([by_part(w_qkv[0], parts), w_out[0]], axis=1)[None])[0]
-    fc_pieces, proj_pieces = chip_rows(w_fc[:1])[0], chip_rows(w_proj[:1])[0]
+    joined_pieces = chip_rows(jnp.concatenate([w_qkv[:1], w_out[:1]], axis=2))[0]
+    fc_pieces, proj_pieces = chip_rows(w_fc), chip_rows(w_proj[:1])[0]
     joined, small = gather_many([joined_pieces, packed.reshape(8, -1)], 1)
-    later_shards = (w_qkv[1:], w_out[1:], w_fc[1:], w_proj[1:])
     joined = joined.reshape(model_width, -1)
-    far_weights = [
+    weights = [
         (
-            (gather_far(by_part(qkv, parts)), gather_far(out)),
-            (gather_far(fc), gather_far(proj)),
-        )
-        for qkv, out, fc, proj in zip(*later_shards)
+            (joined[:, : 3 * model_width], joined[:, 3 * model_width :]),
+            ([], [fc_pieces[0], proj_pieces]),
+        )
+    ] + [
+        (
+            (gather_far(w_qkv[n]), gather_far(w_out[n])),
+            ([gather_far(w_proj[n])], [fc_pieces[n]]),
+        )
+        for n in range(1, LAYERS)
     ]
-    near_weights = (
-        (joined[:, : 3 * model_width], joined[:, 3 * model_width :]),
-        (fc_pieces, proj_pieces),
-    )
     small = small.reshape(devices, -1)
     narrow_all = (
         jnp.transpose(
@@ -761,22 +803,16 @@
         lax.axis_index("dp"),
         0,
     )
-    ids = lax.optimization_barrier(ids.astype(jnp.int32))
-    starts = jnp.zeros((ctx_size, row_count), jnp.int32)
-    for number in range(DOCS):
-        before = jnp.sum((ids < number).astype(jnp.int32))
-        starts = jnp.where(ids == number, before, starts)
+    starts = pl.pallas_call(
+        starts_kernel, out_shape=jax.ShapeDtypeStruct((ctx_size, row_count), jnp.int32)
+    )(ids.astype(jnp.float32))
     first = starts[:, 0] // row_count
-    qkv_scale = jnp.tile(
-        jnp.concatenate(
-            [
-                jnp.full((model_width // parts,), HEAD ** (-0.5), jnp.float32),
-                jnp.ones((2 * model_width // parts,), jnp.float32),
-            ]
-        ),
-        parts,
-    )
-
+    qkv_scale = jnp.concatenate(
+        [
+            jnp.full((model_width,), HEAD ** (-0.5), jnp.float32),
+            jnp.ones((2 * model_width,), jnp.float32),
+        ]
+    )
     plan = (starts.reshape(ctx_size, 1, row_count), first, parts, shares, qkv_scale)
 
     residual = block_input.reshape(row_count, model_width).astype(jnp.float32)
@@ -787,11 +823,9 @@
             zip(("gain1", "bias1", "query", "value", "out", "gain2", "bias2", "proj"), rows)
         )
         narrow["fc"] = fc_all[layer_idx]
-        narrow["qkv"] = by_part(
-            jnp.concatenate([rows[2], jnp.zeros_like(rows[2]), rows[3]])[None], parts
-        )[0]
+        narrow["qkv"] = jnp.concatenate([rows[2], jnp.zeros_like(rows[2]), rows[3]])
         residual, saved = forward_layer(
-            residual, narrow, *([near_weights] + far_weights)[layer_idx], plan, layer_idx == 0
+            residual, narrow, *weights[layer_idx], plan, 2 if layer_idx == 0 else 3
         )
         narrow_sets.append(narrow)
         saved_list.append(saved)
@@ -809,8 +843,9 @@
         carried = [part]
     grad_rows = grad_residual.astype(jnp.bfloat16).reshape(seq_count, local_len, model_width)
     term_size = -(-used // 1024) * 1024
-    narrow_terms = jnp.stack([vector for vectors in vector_sets for vector in vectors])
-    fc_terms = jnp.stack(fc_sets)
+    narrow_terms = jnp.concatenate([vector[None] for vectors in vector_sets for vector in vectors])
+    fc_terms = jnp.concatenate([vector[None] for vector in fc_sets])
+    narrow_terms, fc_terms = lax.optimization_barrier((narrow_terms, fc_terms))
     terms = jnp.concatenate(
         [
             jnp.transpose(narrow_terms.reshape(narrow_count, devices, slot), (1, 0, 2)).reshape(
@@ -824,15 +859,13 @@
         axis=1,
     )
     terms = terms.reshape(devices // 2, 2, 8, term_size // 8)
-    core = lax.axis_index("ctx") % 2
-    terms = pick(terms, core, 1) + swap(pick(terms, 1 - core, 1), 0, 1)
     qkv_sums[0], sums = reduce_many([*carried, terms], 6)
     sums = sums.reshape(-1)
     narrow_sums = sums[: narrow_count * slot].reshape(LAYERS, len(narrow_list), slot)
     grad_fc_b = sums[narrow_count * slot : used].reshape(LAYERS, fc_slot)
-    grad_w_qkv = jnp.stack([by_kind(device_rows(total), parts) for total in qkv_sums])
+    grad_w_qkv = jnp.stack([total for total in qkv_sums])
     grad_w_proj, grad_w_fc, grad_w_out = (
-        jnp.stack([device_rows(sums[n]) for sums in other_sums]) for n in range(3)
+        jnp.stack([sums[n] for sums in other_sums]) for n in range(3)
     )
     return (
         output_rows,

time: 689 us -> 659 us (0.956)
  Pallas kernels: 343 us -> 419 us
  waiting for transfers between devices: 78.9 us -> 25.5 us
  matrix products: 104 us -> 85.3 us
  local copies, waits for them, and re-layouts: 61.2 us -> 44.7 us
  other arithmetic: 29.5 us -> 18.6 us
    pallas_call x2 -> x3, Pallas kernels: 122 us -> 176 us  [gather_many(): pl.pallas_call(functools.partial(gather_kernel, phases, chips, count), ou...]
    ppermute x48 -> x31, waiting for transfers between devices: 55 us -> 25.4 us  [swap(): return lax.ppermute(value, ('dp', 'ctx'), pairs)]
    all_gather x4 -> x3, waiting for transfers between devices: 23.8 us -> 0.04 us  [gather_far(): return lax.all_gather(shard, ('dp', 'ctx'), axis=0, tiled=True)]
    dot_general x28 -> x20, matrix products: 87.8 us -> 69.3 us  [contract(): lax.dot_general(left, right, (((left_dim,), (right_dim,)), ((), ())), pre...]
    another operation x29 -> x1, local copies, waits for them, and re-layouts: 13.1 us -> 0.01 us  [the longest x17 11.3 us: shards(): jnp.stack([vector for vectors in vector_sets for vector in vectors])]
    select_n x7 -> x0, other arithmetic: 10.8 us -> none  [the longest x6 5.59 us: device_rows(): jnp.where(core == 0, jnp.concatenate([kept, got], axis=1), jnp.concatenat...]
    pallas_call x3, Pallas kernels: 165 us -> 176 us  [reduce_many(): pl.pallas_call(functools.partial(reduce_kernel, phases, chips, count, pie...]
    dynamic_slice x8 -> x3, local copies, waits for them, and re-layouts: 9.96 us -> 0.21 us  [pick(): return lax.dynamic_index_in_dim(value, place, axis, keepdims=False)]
  transfers between devices with their start and end apart: 52 -> 34, of which waited for: 9 -> 8; matrix products, arithmetic and copies ran while one was open for 19% -> 12% of each run, Pallas kernels for 46% -> 54%
where the time goes in v4:
time: 659 us; the launch traced here: 652 us
  Pallas kernels  419 us (64%)
  matrix products  85.3 us (13%)
  local copies, waits for them, and re-layouts  44.7 us (7%)
  starting transfers between devices  43.4 us (7%)
  waiting for transfers between devices  25.5 us (4%)
  other arithmetic  18.6 us (3%)
  between operations  15.9 us (2%)
    pallas_call x3, Pallas kernels, reduce_many(): pl.pallas_call(functools.partial(reduce_kernel, phases, chips, count, pie...  176 us
    pallas_call x3, Pallas kernels, gather_many(): pl.pallas_call(functools.partial(gather_kernel, phases, chips, count), ou...  176 us
    dot_general x20, matrix products, contract(): lax.dot_general(left, right, (((left_dim,), (right_dim,)), ((), ())), pre...  69.3 us
    ppermute x31, starting transfers between devices, swap(): return lax.ppermute(value, ('dp', 'ctx'), pairs)  43.3 us
    pallas_call x2, Pallas kernels, attend_back(): pl.pallas_call(functools.partial(mix_back_kernel, parts, shares), out_sha...  34.6 us
    pallas_call x2, Pallas kernels, attend(): pl.pallas_call(functools.partial(mix_kernel, parts, shares), out_shape=(j...  31.3 us
    ppermute x31, waiting for transfers between devices, swap(): return lax.ppermute(value, ('dp', 'ctx'), pairs)  25.4 us
    unnamed x193, local copies, waits for them, and re-layouts  14.8 us
  transfers between devices with their start and end apart: 34, of which 8 were waited for; matrix products, arithmetic and copies ran while one was open for 12% of the time, Pallas kernels for 54%

profile of v4, /device:TPU:0, one launch (start us, length us, event | category | flops | bytes accessed | tf_op | source)
XLA Modules:
  0.0 652.2 jit_solution(13117070195609007249)
XLA Ops:
  7.2 1.7 fusion.100
  9.0 1.4 fusion.101
  12.3 1.7 fusion.99
  24.2 40.6 %shard_map.271 = (bf16[16,48,3072]{2,1,0:T(8,128)(2,1)}, bf16[16,2,8,128]{3,2,1,0:T(8,128)(2,1)}) custom-call(bf16[48,1536]{1,0:T(8,128)(2,1)} %maximum_select_fusion.1.refs_0_, bf16[8,128]{1,0:T(8,128)(2,1)} %maximum_bitcast_fusion.1.refs_1_), custom_call_target="tpu_custom_call" | custom-call | flops 30000001024 | bytes 2000000 | tf_op jit(solution)/shard_map/pallas_call | solution.py:179
  67.4 3.7 fusion.9
  72.8 2.0 collective-permute-start.4
  74.9 2.3 collective-permute-start.5
  77.2 77.4 %shard_map.273 = (bf16[16,48,3072]{2,1,0:T(8,128)(2,1)}, bf16[16,192,768]{2,1,0:T(8,128)(2,1)}) custom-call(bf16[48,1536]{1,0:T(8,128)(2,1)} %get-tuple-element.77.refs_0_, bf16[192,384]{1,0:T(8,128)(2,1)} %maximum_select_fusion.2.refs_1_), custom_call_target="tpu_custom_call" | custom-call | flops 30000001024 | bytes 2000000 | tf_op jit(solution)/shard_map/pallas_call | solution.py:179
  157.0 1.4 shard_map.272
  162.1 15.6 %shard_map.274 = (bf16[4,192,256]{2,1,0:T(8,128)(2,1)}, f32[4,8,256]{2,1,0:T(8,128)}) custom-call(s32[8]{0:T(128)} %and_select_fusion.refs_0_, s32[8,1,256]{2,1,0:T(1,128)} %reshape.359.refs_1_, bf16[576,256]{1,0:T(8,128)(2,1)} %bitcast.347, bf16[576,256]{1,0:T(8,128)(2,1)} %bitcast.379, bf16[576,256]{1,0:T(8,128)(2,1)} %bitcast.382, ...), custom_call_target="tpu_custom_call" | custom-call | flops 1610612736 | bytes 1572864 | tf_op jit(solution)/shard_map/pallas_call | solution.py:580
  179.8 3.3 collective-permute-start.7
  183.3 3.7 collective-permute-done.9
  187.0 4.9 collective-permute-done.8
  192.1 2.0 fusion.105
  194.4 4.0 convolution_add_fusion.3
  198.5 2.1 fusion.106
  200.8 4.9 fusion.11
  205.8 1.6 copy.65
  208.7 4.3 collective-permute-start.11
  212.9 57.5 %shard_map.275 = bf16[16,48,3072]{2,1,0:T(8,128)(2,1)} custom-call(bf16[48,1536]{1,0:T(8,128)(2,1)} %get-tuple-element.89.refs_0_), custom_call_target="tpu_custom_call" | custom-call | flops 15000000512 | bytes 1000000 | tf_op jit(solution)/shard_map/pallas_call | solution.py:179
  271.2 1.9 collective-permute-done.13
  274.0 15.8 %shard_map.276 = (bf16[4,192,256]{2,1,0:T(8,128)(2,1)}, f32[4,8,256]{2,1,0:T(8,128)}) custom-call(s32[8]{0:T(128)} %and_select_fusion.refs_0_, s32[8,1,256]{2,1,0:T(1,128)} %reshape.359.refs_1_, bf16[576,256]{1,0:T(8,128)(2,1)} %bitcast.350, bf16[576,256]{1,0:T(8,128)(2,1)} %bitcast.367, bf16[576,256]{1,0:T(8,128)(2,1)} %bitcast.370, ...), custom_call_target="tpu_custom_call" | custom-call | flops 1610612736 | bytes 1572864 | tf_op jit(solution)/shard_map/pallas_call | solution.py:580
  290.9 1.5 collective-permute-start.16
  293.0 2.4 collective-permute-start.14
  296.1 1.4 collective-permute-done.16
  297.5 5.1 collective-permute-done.15
  302.7 1.9 fusion.107
  305.0 3.9 convolution_add_fusion.2
  308.9 1.6 copy-done.87
  310.5 4.4 convolution_convert_fusion.5
  314.9 7.1 %fusion.108 = (f32[3072]{0:T(1024)}, bf16[256,3072]{1,0:T(8,128)(2,1)S(1)}) fusion(f32[256,3072]{1,0:T(8,128)} %copy-done.87, bf16[1,3072,768]{2,1,0:T(8,128)(2,1)} %all-gather.11.cloned.1.call-done, bf16[1,256,768]{2,1,0:T(8,128)(2,1)S(1)} %copy-done.26), kind=kOutput, calls=%fused_computation.288 | convolution fusion | flops 1223685120 | bytes 9842688 | tf_op jit(solution)/shard_map/dot_general | solution.py:408
  322.0 5.2 multiply_reduce_fusion
  327.2 1.8 fusion.92
  332.1 2.1 collective-permute-start.18
  334.2 2.2 collective-permute-start.19
  336.5 5.1 convolution_convert_fusion.4
  343.6 17.2 %shard_map.277 = (bf16[4,192,256]{2,1,0:T(8,128)(2,1)}, f32[4,384,256]{2,1,0:T(8,128)}, bf16[1,4,384,256]{3,2,1,0:T(8,128)(2,1)}) custom-call(s32[8]{0:T(128)} %and_select_fusion.refs_0_, s32[8,1,256]{2,1,0:T(1,128)} %reshape.359.refs_1_, bf16[4,192,256]{2,1,0:T(8,128)(2,1)} %get-tuple-element.94.refs_2_, f32[4,8,256]{2,1,0:T(8,128)} %get-tuple-element.96.refs_3_, ...), custom_call_target="tpu_custom_call" | custom-call | flops 4026531840 | bytes 3145728 | tf_op jit(solution)/shard_map/pallas_call | solution.py:610
  360.8 3.9 collective-permute-start.20
  364.7 1.5 convolution_convert_fusion.7
  370.6 6.1 fusion.41
  378.7 1.4 collective-permute-start.23
  380.1 2.7 collective-permute-start.22
  383.1 62.8 %shard_map.278 = (f32[96,768]{1,0:T(8,128)}, f32[24,3072]{1,0:T(8,128)}, f32[24,768]{1,0:T(8,128)}) custom-call(bf16[16,192,768]{2,1,0:T(8,128)(2,1)} %bitcast.424, bf16[16,48,3072]{2,1,0:T(8,128)(2,1)} %bitcast.329, bf16[16,48,768]{2,1,0:T(8,128)(2,1)} %bitcast.342), custom_call_target="tpu_custom_call" | custom-call | flops 44999999488 | bytes 3000000 | tf_op jit(solution)/shard_map/pallas_call | solution.py:334
  448.2 1.9 multiply_reduce_fusion.1
  452.0 5.0 fusion.109
  457.0 2.3 multiply_reduce_fusion.2
  459.3 3.7 convolution_convert_fusion.2
  463.0 3.0 convolution_convert_fusion.1
  466.4 1.8 convolution_convert_fusion.8
  469.9 1.6 collective-permute-start.25
  471.5 1.7 collective-permute-start.26
  473.6 1.5 collective-permute-done.24.refs_9_
  475.1 5.5 collective-permute-done.25.refs_10_
  481.4 17.4 %shard_map.279 = (bf16[4,192,256]{2,1,0:T(8,128)(2,1)}, f32[4,384,256]{2,1,0:T(8,128)}, bf16[1,4,384,256]{3,2,1,0:T(8,128)(2,1)}) custom-call(s32[8]{0:T(128)} %and_select_fusion.refs_0_, s32[8,1,256]{2,1,0:T(1,128)} %reshape.359.refs_1_, bf16[4,192,256]{2,1,0:T(8,128)(2,1)} %get-tuple-element.85.refs_2_, f32[4,8,256]{2,1,0:T(8,128)} %get-tuple-element.108.refs_3_, ...), custom_call_target="tpu_custom_call" | custom-call | flops 4026531840 | bytes 3145728 | tf_op jit(solution)/shard_map/pallas_call | solution.py:610
  498.8 1.8 collective-permute-start.27
  500.8 1.5 convolution_convert_fusion.6
  502.2 6.5 convolution_convert_fusion.3
  509.8 1.9 collective-permute-start.30
  511.8 2.7 collective-permute-start.29
  514.4 80.6 %shard_map.280 = (f32[96,768]{1,0:T(8,128)}, f32[24,3072]{1,0:T(8,128)}, f32[24,768]{1,0:T(8,128)}, f32[24,2304]{1,0:T(8,128)}) custom-call(bf16[16,192,768]{2,1,0:T(8,128)(2,1)} %bitcast.427, bf16[16,48,3072]{2,1,0:T(8,128)(2,1)} %bitcast.328, bf16[16,48,768]{2,1,0:T(8,128)(2,1)} %bitcast.343, bf16[16,48,2304]{2,1,0:T(8,128)(2,1)} %bitcast.327), custom_call_target="tpu_custom_call" | custom-call | flops 60000002048 | bytes 4000000 | tf_op jit(solution)/shard_map/pallas_call | solution.py:334
  596.0 3.4 fusion.62
  599.5 3.2 convolution_convert_fusion
  604.7 32.6 %shard_map.281 = (f32[24,2304]{1,0:T(8,128)}, f32[8,128]{1,0:T(8,128)}) custom-call(bf16[16,48,2304]{2,1,0:T(8,128)(2,1)} %bitcast.326, f32[16,2,8,128]{3,2,1,0:T(8,128)} %bitcast.376), custom_call_target="tpu_custom_call" | custom-call | flops 30000001024 | bytes 2000000 | tf_op jit(solution)/shard_map/pallas_call | solution.py:334
  640.0 1.8 pad_maximum_fusion.10
  (369 shorter events, 59.9 us)
Async XLA Ops:
  7.2 15.4 %copy-start = (bf16[1,256,768]{2,1,0:T(8,128)(2,1)S(1)}, bf16[1,256,768]{2,1,0:T(8,128)(2,1)}, u32[]{:S(2)}) copy-start(bf16[1,256,768]{2,1,0:T(8,128)(2,1)} %param.16) | copy-start | bytes 1179652
  7.2 193.6 %all-gather.7.cloned.1.call-start = ((), (), s32[]{:S(2)}) async-start(), calls=%async_computation | async-start | bytes 3649536 | tf_op jit(solution)/shard_map/all_gather | solution.py:194
  8.9 293.8 %all-gather.9.cloned.1.call-start = ((), (), s32[]{:S(2)}) async-start(), calls=%async_computation.1 | async-start | bytes 1216512 | tf_op jit(solution)/shard_map/all_gather | solution.py:194
  10.4 304.5 %all-gather.11.cloned.1.call-start = ((), (), s32[]{:S(2)}) async-start(), calls=%async_computation.2 | async-start | bytes 4866048 | tf_op jit(solution)/shard_map/all_gather | solution.py:194
  10.6 12.9 %collective-permute-start = (bf16[1,24,1536]{2,1,0:T(8,128)(2,1)S(1)}, bf16[1,24,1536]{2,1,0:T(8,128)(2,1)S(1)}, u32[]{:S(2)}, u32[]{:S(2)}) collective-permute-start(bf16[1,24,1536]{2,1,0:T(8,128)(2,1)S(1)} %get-tuple-element.232), channel_id=1, source_target_pairs={{0,1},{1,0},{2,3},{3,2},{4,5},{5,4},{6,7},{7,6},{8,9},{9,8},{10,11... | collective-permute-start | bytes 221192 | tf_op jit(solution)/shard_map/ppermute | solution.py:27
  12.2 59.7 %collective-permute-start.1 = (bf16[2,24,1536]{2,1,0:T(8,128)(2,1)S(1)}, bf16[2,24,1536]{2,1,0:T(8,128)(2,1)S(1)}, u32[]{:S(2)}, u32[]{:S(2)}) collective-permute-start(bf16[2,24,1536]{2,1,0:T(8,128)(2,1)S(1)} %get-tuple-element.226), channel_id=1, source_target_pairs={{0,1},{1,0},{2,3},{3,2},{4,5},{5,4},{6,7},{7,6},{8,9},{9,8},{10,11... | collective-permute-start | bytes 442376 | tf_op jit(solution)/shard_map/ppermute | solution.py:27
  13.9 57.3 %collective-permute-start.2 = (bf16[1,96,384]{2,1,0:T(8,128)(2,1)S(1)}, bf16[1,96,384]{2,1,0:T(8,128)(2,1)S(1)}, u32[]{:S(2)}, u32[]{:S(2)}) collective-permute-start(bf16[1,96,384]{2,1,0:T(8,128)(2,1)S(1)} %get-tuple-element.230), channel_id=1, source_target_pairs={{0,1},{1,0},{2,3},{3,2},{4,5},{5,4},{6,7},{7,6},{8,9},{9,8},{10,11... | collective-permute-start | bytes 221192 | tf_op jit(solution)/shard_map/ppermute | solution.py:27
  22.6 44.9 %copy-start.46 = (f32[256]{0:T(256)}, f32[256]{0:T(256)S(1)}, u32[]{:S(2)}) copy-start(f32[256]{0:T(256)S(1)} %broadcast_multiply_fusion.11) | copy-start | bytes 3076
  22.8 44.6 %copy-start.53 = (f32[256]{0:T(256)}, f32[256]{0:T(256)S(1)}, u32[]{:S(2)}) copy-start(f32[256]{0:T(256)S(1)} %add_rsqrt_fusion.3) | copy-start | bytes 3076
  24.2 43.2 %copy-start.83 = (f32[2304]{0:T(1024)S(1)}, f32[2304]{0:T(1024)}, u32[]{:S(2)}) copy-start(f32[2304]{0:T(1024)} %constant.180.clone.1) | copy-start | bytes 27652
  66.8 127.6 %copy-start.41 = (f32[768]{0:T(1024)}, f32[768]{0:T(1024)S(1)}, u32[]{:S(2)}) copy-start(f32[768]{0:T(1024)S(1)} %get-tuple-element.158) | copy-start | bytes 9220
  72.8 81.9 %collective-permute-start.3 = (bf16[3,192,256]{2,1,0:T(8,128)(2,1)S(1)}, bf16[3,192,256]{2,1,0:T(8,128)(2,1)S(1)}, u32[]{:S(2)}, u32[]{:S(2)}) collective-permute-start(bf16[3,192,256]{2,1,0:T(8,128)(2,1)S(1)} %get-tuple-element.195), channel_id=1, source_target_pairs={{0,2},{1,3},{2,0},{3,1},{4,6},{5,7},{6,4},{7,5},{8,10},{9,11},{10,... | collective-permute-start | bytes 884744 | tf_op jit(solution)/shard_map/ppermute | solution.py:27
  72.8 81.9 %collective-permute-start.4 = (bf16[3,192,256]{2,1,0:T(8,128)(2,1)S(1)}, bf16[3,192,256]{2,1,0:T(8,128)(2,1)S(1)}, u32[]{:S(2)}, u32[]{:S(2)}) collective-permute-start(bf16[3,192,256]{2,1,0:T(8,128)(2,1)S(1)} %get-tuple-element.194), channel_id=1, source_target_pairs={{0,4},{1,5},{2,6},{3,7},{4,0},{5,1},{6,2},{7,3},{8,12},{9,13},{10,... | collective-permute-start | bytes 884744 | tf_op jit(solution)/shard_map/ppermute | solution.py:27
  74.9 79.9 %collective-permute-start.5 = (bf16[3,192,256]{2,1,0:T(8,128)(2,1)S(1)}, bf16[3,192,256]{2,1,0:T(8,128)(2,1)}, u32[]{:S(2)}, u32[]{:S(2)}) collective-permute-start(bf16[3,192,256]{2,1,0:T(8,128)(2,1)S(1)} %get-tuple-element.193), channel_id=1, source_target_pairs={{0,6},{1,7},{2,4},{3,5},{4,2},{5,3},{6,0},{7,1},{8,14},{9,15},{10,... | collective-permute-start | bytes 884744 | tf_op jit(solution)/shard_map/ppermute | solution.py:27
  156.1 5.0 collective-permute-start.6
  178.7 8.3 %collective-permute-start.9 = (bf16[192,256]{1,0:T(8,128)(2,1)S(1)}, bf16[192,256]{1,0:T(8,128)(2,1)S(1)}, u32[]{:S(2)}, u32[]{:S(2)}) collective-permute-start(bf16[192,256]{1,0:T(8,128)(2,1)S(1)} %get-tuple-element.218), channel_id=1, source_target_pairs={{0,6},{1,7},{2,4},{3,5},{4,2},{5,3},{6,0},{7,1},{8,14},{9,15},{10,... | collective-permute-start | bytes 294920 | tf_op jit(solution)/shard_map/ppermute | solution.py:27
  179.8 12.1 %collective-permute-start.8 = (bf16[192,256]{1,0:T(8,128)(2,1)S(1)}, bf16[192,256]{1,0:T(8,128)(2,1)S(1)}, u32[]{:S(2)}, u32[]{:S(2)}) collective-permute-start(bf16[192,256]{1,0:T(8,128)(2,1)S(1)} %get-tuple-element.219), channel_id=1, source_target_pairs={{0,4},{1,5},{2,6},{3,7},{4,0},{5,1},{6,2},{7,3},{8,12},{9,13},{10,... | collective-permute-start | bytes 294920 | tf_op jit(solution)/shard_map/ppermute | solution.py:27
  179.8 12.1 %collective-permute-start.7 = (bf16[192,256]{1,0:T(8,128)(2,1)S(1)}, bf16[192,256]{1,0:T(8,128)(2,1)S(1)}, u32[]{:S(2)}, u32[]{:S(2)}) collective-permute-start(bf16[192,256]{1,0:T(8,128)(2,1)S(1)} %get-tuple-element.220), channel_id=1, source_target_pairs={{0,2},{1,3},{2,0},{3,1},{4,6},{5,7},{6,4},{7,5},{8,10},{9,11},{10,... | collective-permute-start | bytes 294920 | tf_op jit(solution)/shard_map/ppermute | solution.py:27
  208.2 62.4 %copy-start.15 = (bf16[3,1,192,256]{3,2,1,0:T(8,128)(2,1)}, bf16[3,1,192,256]{3,2,1,0:T(8,128)(2,1)S(1)}, u32[]{:S(2)}) copy-start(bf16[3,1,192,256]{3,2,1,0:T(8,128)(2,1)S(1)} %get-tuple-element.192) | copy-start | bytes 884740
  208.2 62.3 %collective-permute-start.10 = (bf16[3,192,256]{2,1,0:T(8,128)(2,1)}, bf16[3,192,256]{2,1,0:T(8,128)(2,1)S(1)}, u32[]{:S(2)}, u32[]{:S(2)}) collective-permute-start(bf16[3,192,256]{2,1,0:T(8,128)(2,1)} %get-tuple-element.191), channel_id=1, source_target_pairs={{0,2},{1,3},{2,0},{3,1},{4,6},{5,7},{6,4},{7,5},{8,10},{9,11},{10,... | collective-permute-start | bytes 884744 | tf_op jit(solution)/shard_map/ppermute | solution.py:27
  208.7 61.9 %collective-permute-start.11 = (bf16[3,192,256]{2,1,0:T(8,128)(2,1)}, bf16[3,192,256]{2,1,0:T(8,128)(2,1)S(1)}, u32[]{:S(2)}, u32[]{:S(2)}) collective-permute-start(bf16[3,192,256]{2,1,0:T(8,128)(2,1)} %get-tuple-element.190), channel_id=1, source_target_pairs={{0,4},{1,5},{2,6},{3,7},{4,0},{5,1},{6,2},{7,3},{8,12},{9,13},{10,... | collective-permute-start | bytes 884744 | tf_op jit(solution)/shard_map/ppermute | solution.py:27
  212.9 57.6 %collective-permute-start.12 = (bf16[3,192,256]{2,1,0:T(8,128)(2,1)S(1)}, bf16[3,192,256]{2,1,0:T(8,128)(2,1)S(1)}, u32[]{:S(2)}, u32[]{:S(2)}) collective-permute-start(bf16[3,192,256]{2,1,0:T(8,128)(2,1)S(1)} %get-tuple-element.189), channel_id=1, source_target_pairs={{0,6},{1,7},{2,4},{3,5},{4,2},{5,3},{6,0},{7,1},{8,14},{9,15},{10,... | collective-permute-start | bytes 884744 | tf_op jit(solution)/shard_map/ppermute | solution.py:27
  270.8 2.4 collective-permute-start.13
  289.8 15.1 %copy-start.43 = (f32[768]{0:T(1024)S(1)}, f32[768]{0:T(1024)}, u32[]{:S(2)}) copy-start(f32[768]{0:T(1024)} %get-tuple-element.151) | copy-start | bytes 9220
  290.9 6.6 %collective-permute-start.16 = (bf16[192,256]{1,0:T(8,128)(2,1)S(1)}, bf16[192,256]{1,0:T(8,128)(2,1)S(1)}, u32[]{:S(2)}, u32[]{:S(2)}) collective-permute-start(bf16[192,256]{1,0:T(8,128)(2,1)S(1)} %get-tuple-element.210), channel_id=1, source_target_pairs={{0,6},{1,7},{2,4},{3,5},{4,2},{5,3},{6,0},{7,1},{8,14},{9,15},{10,... | collective-permute-start | bytes 294920 | tf_op jit(solution)/shard_map/ppermute | solution.py:27
  292.4 10.1 %collective-permute-start.15 = (bf16[192,256]{1,0:T(8,128)(2,1)S(1)}, bf16[192,256]{1,0:T(8,128)(2,1)S(1)}, u32[]{:S(2)}, u32[]{:S(2)}) collective-permute-start(bf16[192,256]{1,0:T(8,128)(2,1)S(1)} %get-tuple-element.211), channel_id=1, source_target_pairs={{0,4},{1,5},{2,6},{3,7},{4,0},{5,1},{6,2},{7,3},{8,12},{9,13},{10,... | collective-permute-start | bytes 294920 | tf_op jit(solution)/shard_map/ppermute | solution.py:27
  293.0 9.6 %collective-permute-start.14 = (bf16[192,256]{1,0:T(8,128)(2,1)S(1)}, bf16[192,256]{1,0:T(8,128)(2,1)S(1)}, u32[]{:S(2)}, u32[]{:S(2)}) collective-permute-start(bf16[192,256]{1,0:T(8,128)(2,1)S(1)} %get-tuple-element.212), channel_id=1, source_target_pairs={{0,2},{1,3},{2,0},{3,1},{4,6},{5,7},{6,4},{7,5},{8,10},{9,11},{10,... | collective-permute-start | bytes 294920 | tf_op jit(solution)/shard_map/ppermute | solution.py:27
  304.7 17.3 %copy-start.52 = (f32[256]{0:T(256)}, f32[256]{0:T(256)S(1)}, u32[]{:S(2)}) copy-start(f32[256]{0:T(256)S(1)} %broadcast_multiply_fusion.8) | copy-start | bytes 3076
  304.9 17.1 %copy-start.62 = (f32[256]{0:T(256)}, f32[256]{0:T(256)S(1)}, u32[]{:S(2)}) copy-start(f32[256]{0:T(256)S(1)} %add_rsqrt_fusion) | copy-start | bytes 3076
  332.1 9.5 %collective-permute-start.17 = (bf16[192,256]{1,0:T(8,128)(2,1)S(1)}, bf16[192,256]{1,0:T(8,128)(2,1)S(1)}, u32[]{:S(2)}, u32[]{:S(2)}) collective-permute-start(bf16[192,256]{1,0:T(8,128)(2,1)S(1)} %get-tuple-element.203), channel_id=1, source_target_pairs={{0,2},{1,3},{2,0},{3,1},{4,6},{5,7},{6,4},{7,5},{8,10},{9,11},{10,... | collective-permute-start | bytes 294920 | tf_op jit(solution)/shard_map/ppermute | solution.py:27
  332.1 10.8 %collective-permute-start.18 = (bf16[192,256]{1,0:T(8,128)(2,1)S(1)}, bf16[192,256]{1,0:T(8,128)(2,1)S(1)}, u32[]{:S(2)}, u32[]{:S(2)}) collective-permute-start(bf16[192,256]{1,0:T(8,128)(2,1)S(1)} %get-tuple-element.202), channel_id=1, source_target_pairs={{0,4},{1,5},{2,6},{3,7},{4,0},{5,1},{6,2},{7,3},{8,12},{9,13},{10,... | collective-permute-start | bytes 294920 | tf_op jit(solution)/shard_map/ppermute | solution.py:27
  334.2 8.7 %collective-permute-start.19 = (bf16[192,256]{1,0:T(8,128)(2,1)S(1)}, bf16[192,256]{1,0:T(8,128)(2,1)S(1)}, u32[]{:S(2)}, u32[]{:S(2)}) collective-permute-start(bf16[192,256]{1,0:T(8,128)(2,1)S(1)} %get-tuple-element.201), channel_id=1, source_target_pairs={{0,6},{1,7},{2,4},{3,5},{4,2},{5,3},{6,0},{7,1},{8,14},{9,15},{10,... | collective-permute-start | bytes 294920 | tf_op jit(solution)/shard_map/ppermute | solution.py:27
  343.6 21.1 %copy-start.7 = (bf16[192,256]{1,0:T(8,128)(2,1)S(1)}, bf16[192,256]{1,0:T(8,128)(2,1)}, u32[]{:S(2)}) copy-start(bf16[192,256]{1,0:T(8,128)(2,1)} %copy-done.6) | copy-start | bytes 294916
  343.6 21.1 %copy-start.9 = (bf16[192,256]{1,0:T(8,128)(2,1)S(1)}, bf16[192,256]{1,0:T(8,128)(2,1)}, u32[]{:S(2)}) copy-start(bf16[192,256]{1,0:T(8,128)(2,1)} %copy-done.8) | copy-start | bytes 294916
  343.6 21.1 %copy-start.11 = (bf16[192,256]{1,0:T(8,128)(2,1)S(1)}, bf16[192,256]{1,0:T(8,128)(2,1)}, u32[]{:S(2)}) copy-start(bf16[192,256]{1,0:T(8,128)(2,1)} %copy-done.10) | copy-start | bytes 294916
  343.6 21.1 %copy-start.13 = (bf16[192,256]{1,0:T(8,128)(2,1)S(1)}, bf16[192,256]{1,0:T(8,128)(2,1)}, u32[]{:S(2)}) copy-start(bf16[192,256]{1,0:T(8,128)(2,1)} %copy-done.12) | copy-start | bytes 294916
  343.6 26.4 %copy-start.56 = (f32[768]{0:T(1024)S(1)}, f32[768]{0:T(1024)}, u32[]{:S(2)}) copy-start(f32[768]{0:T(1024)} %get-tuple-element.196) | copy-start | bytes 9220
  360.8 15.9 %collective-permute-start.20 = (bf16[4,384,256]{2,1,0:T(8,128)(2,1)}, bf16[4,384,256]{2,1,0:T(8,128)(2,1)S(1)}, u32[]{:S(2)}, u32[]{:S(2)}) collective-permute-start(bf16[4,384,256]{2,1,0:T(8,128)(2,1)} %bitcast.411), channel_id=1, source_target_pairs={{0,1},{1,0},{2,3},{3,2},{4,5},{5,4},{6,7},{7,6},{8,9},{9,8},{10,11... | collective-permute-start | bytes 2359304 | tf_op jit(solution)/shard_map/ppermute | solution.py:27
  378.7 67.2 %collective-permute-start.23 = (bf16[576,256]{1,0:T(8,128)(2,1)}, bf16[576,256]{1,0:T(8,128)(2,1)S(1)}, u32[]{:S(2)}, u32[]{:S(2)}) collective-permute-start(bf16[576,256]{1,0:T(8,128)(2,1)} %get-tuple-element.186), channel_id=1, source_target_pairs={{0,6},{1,7},{2,4},{3,5},{4,2},{5,3},{6,0},{7,1},{8,14},{9,15},{10,... | collective-permute-start | bytes 884744 | tf_op jit(solution)/shard_map/ppermute | solution.py:27
  380.1 65.9 %collective-permute-start.22 = (bf16[576,256]{1,0:T(8,128)(2,1)}, bf16[576,256]{1,0:T(8,128)(2,1)}, u32[]{:S(2)}, u32[]{:S(2)}) collective-permute-start(bf16[576,256]{1,0:T(8,128)(2,1)} %get-tuple-element.187), channel_id=1, source_target_pairs={{0,4},{1,5},{2,6},{3,7},{4,0},{5,1},{6,2},{7,3},{8,12},{9,13},{10,... | collective-permute-start | bytes 884744 | tf_op jit(solution)/shard_map/ppermute | solution.py:27
  382.8 63.2 %collective-permute-start.21 = (bf16[576,256]{1,0:T(8,128)(2,1)S(1)}, bf16[576,256]{1,0:T(8,128)(2,1)}, u32[]{:S(2)}, u32[]{:S(2)}) collective-permute-start(bf16[576,256]{1,0:T(8,128)(2,1)S(1)} %get-tuple-element.188), channel_id=1, source_target_pairs={{0,2},{1,3},{2,0},{3,1},{4,6},{5,7},{6,4},{7,5},{8,10},{9,11},{10,... | collective-permute-start | bytes 884744 | tf_op jit(solution)/shard_map/ppermute | solution.py:27
  448.2 8.8 %slice-start = ((s8[4718592]{0:T(1024)(128)(4,1)}), s8[4194304]{0:T(1024)(128)(4,1)S(1)}, s32[]{:S(2)}) async-start(s8[4718592]{0:T(1024)(128)(4,1)} %bitcast.417), calls=%async_computation.3 | async-start | bytes 8388608
  468.8 6.3 collective-permute-start.24
  469.9 10.8 %collective-permute-start.25 = (bf16[192,256]{1,0:T(8,128)(2,1)S(1)}, bf16[192,256]{1,0:T(8,128)(2,1)S(1)}, u32[]{:S(2)}, u32[]{:S(2)}) collective-permute-start(bf16[192,256]{1,0:T(8,128)(2,1)S(1)} %get-tuple-element.198), channel_id=1, source_target_pairs={{0,4},{1,5},{2,6},{3,7},{4,0},{5,1},{6,2},{7,3},{8,12},{9,13},{10,... | collective-permute-start | bytes 294920 | tf_op jit(solution)/shard_map/ppermute | solution.py:27
  471.5 9.2 %collective-permute-start.26 = (bf16[192,256]{1,0:T(8,128)(2,1)S(1)}, bf16[192,256]{1,0:T(8,128)(2,1)S(1)}, u32[]{:S(2)}, u32[]{:S(2)}) collective-permute-start(bf16[192,256]{1,0:T(8,128)(2,1)S(1)} %get-tuple-element.197), channel_id=1, source_target_pairs={{0,6},{1,7},{2,4},{3,5},{4,2},{5,3},{6,0},{7,1},{8,14},{9,15},{10,... | collective-permute-start | bytes 294920 | tf_op jit(solution)/shard_map/ppermute | solution.py:27
  481.3 19.3 %copy-start.73 = (f32[768]{0:T(1024)S(1)}, f32[768]{0:T(1024)}, u32[]{:S(2)}) copy-start(f32[768]{0:T(1024)} %get-tuple-element.137) | copy-start | bytes 9220
  481.3 19.3 %copy-start.72 = (f32[768]{0:T(1024)S(1)}, f32[768]{0:T(1024)}, u32[]{:S(2)}) copy-start(f32[768]{0:T(1024)} %get-tuple-element.147) | copy-start | bytes 9220
  481.3 19.3 %copy-start.55 = (f32[768]{0:T(1024)S(1)}, f32[768]{0:T(1024)}, u32[]{:S(2)}) copy-start(f32[768]{0:T(1024)} %get-tuple-element.169) | copy-start | bytes 9220
  481.3 19.3 %copy-start.71 = (f32[768]{0:T(1024)S(1)}, f32[768]{0:T(1024)}, u32[]{:S(2)}) copy-start(f32[768]{0:T(1024)} %get-tuple-element.135) | copy-start | bytes 9220
  481.3 19.3 %copy-start.70 = (f32[768]{0:T(1024)S(1)}, f32[768]{0:T(1024)}, u32[]{:S(2)}) copy-start(f32[768]{0:T(1024)} %get-tuple-element.146) | copy-start | bytes 9220
  481.3 19.4 %copy-start.17 = (bf16[192,256]{1,0:T(8,128)(2,1)S(1)}, bf16[192,256]{1,0:T(8,128)(2,1)}, u32[]{:S(2)}) copy-start(bf16[192,256]{1,0:T(8,128)(2,1)} %copy-done.16) | copy-start | bytes 294916
  481.4 19.4 %copy-start.19 = (bf16[192,256]{1,0:T(8,128)(2,1)S(1)}, bf16[192,256]{1,0:T(8,128)(2,1)}, u32[]{:S(2)}) copy-start(bf16[192,256]{1,0:T(8,128)(2,1)} %copy-done.18) | copy-start | bytes 294916
  481.4 19.4 %copy-start.21 = (bf16[192,256]{1,0:T(8,128)(2,1)S(1)}, bf16[192,256]{1,0:T(8,128)(2,1)}, u32[]{:S(2)}) copy-start(bf16[192,256]{1,0:T(8,128)(2,1)} %copy-done.20) | copy-start | bytes 294916
  481.4 19.4 %copy-start.23 = (bf16[192,256]{1,0:T(8,128)(2,1)S(1)}, bf16[192,256]{1,0:T(8,128)(2,1)}, u32[]{:S(2)}) copy-start(bf16[192,256]{1,0:T(8,128)(2,1)} %copy-done.22) | copy-start | bytes 294916
  498.8 9.9 %collective-permute-start.27 = (bf16[4,384,256]{2,1,0:T(8,128)(2,1)}, bf16[4,384,256]{2,1,0:T(8,128)(2,1)S(1)}, u32[]{:S(2)}, u32[]{:S(2)}) collective-permute-start(bf16[4,384,256]{2,1,0:T(8,128)(2,1)} %bitcast.410), channel_id=1, source_target_pairs={{0,1},{1,0},{2,3},{3,2},{4,5},{5,4},{6,7},{7,6},{8,9},{9,8},{10,11... | collective-permute-start | bytes 2359304 | tf_op jit(solution)/shard_map/ppermute | solution.py:27
  509.8 85.1 %collective-permute-start.30 = (bf16[576,256]{1,0:T(8,128)(2,1)S(1)}, bf16[576,256]{1,0:T(8,128)(2,1)S(1)}, u32[]{:S(2)}, u32[]{:S(2)}) collective-permute-start(bf16[576,256]{1,0:T(8,128)(2,1)S(1)} %get-tuple-element.178), channel_id=1, source_target_pairs={{0,6},{1,7},{2,4},{3,5},{4,2},{5,3},{6,0},{7,1},{8,14},{9,15},{10,... | collective-permute-start | bytes 884744 | tf_op jit(solution)/shard_map/ppermute | solution.py:27
  511.8 83.2 %collective-permute-start.29 = (bf16[576,256]{1,0:T(8,128)(2,1)S(1)}, bf16[576,256]{1,0:T(8,128)(2,1)S(1)}, u32[]{:S(2)}, u32[]{:S(2)}) collective-permute-start(bf16[576,256]{1,0:T(8,128)(2,1)S(1)} %get-tuple-element.179), channel_id=1, source_target_pairs={{0,4},{1,5},{2,6},{3,7},{4,0},{5,1},{6,2},{7,3},{8,12},{9,13},{10,... | collective-permute-start | bytes 884744 | tf_op jit(solution)/shard_map/ppermute | solution.py:27
  514.4 80.6 %collective-permute-start.28 = (bf16[576,256]{1,0:T(8,128)(2,1)S(1)}, bf16[576,256]{1,0:T(8,128)(2,1)S(1)}, u32[]{:S(2)}, u32[]{:S(2)}) collective-permute-start(bf16[576,256]{1,0:T(8,128)(2,1)S(1)} %get-tuple-element.180), channel_id=1, source_target_pairs={{0,2},{1,3},{2,0},{3,1},{4,6},{5,7},{6,4},{7,5},{8,10},{9,11},{10,... | collective-permute-start | bytes 884744 | tf_op jit(solution)/shard_map/ppermute | solution.py:27
  604.7 37.1 %copy-start.44 = (f32[24,768]{1,0:T(8,128)S(1)}, f32[24,768]{1,0:T(8,128)}, u32[]{:S(2)}) copy-start(f32[24,768]{1,0:T(8,128)} %get-tuple-element.128) | copy-start | bytes 221188
  604.7 37.1 %copy-start.45 = (f32[24,768]{1,0:T(8,128)S(1)}, f32[24,768]{1,0:T(8,128)}, u32[]{:S(2)}) copy-start(f32[24,768]{1,0:T(8,128)} %get-tuple-element.127) | copy-start | bytes 221188
  604.7 37.8 %copy-start.29 = (f32[24,3072]{1,0:T(8,128)S(1)}, f32[24,3072]{1,0:T(8,128)}, u32[]{:S(2)}) copy-start(f32[24,3072]{1,0:T(8,128)} %get-tuple-element.130) | copy-start | bytes 884740
  604.7 37.8 %copy-start.31 = (f32[24,3072]{1,0:T(8,128)S(1)}, f32[24,3072]{1,0:T(8,128)}, u32[]{:S(2)}) copy-start(f32[24,3072]{1,0:T(8,128)} %get-tuple-element.129) | copy-start | bytes 884740
  604.7 38.7 %copy-start.28 = (f32[96,768]{1,0:T(8,128)S(1)}, f32[96,768]{1,0:T(8,128)}, u32[]{:S(2)}) copy-start(f32[96,768]{1,0:T(8,128)} %get-tuple-element.132) | copy-start | bytes 884740
  604.7 38.7 %copy-start.30 = (f32[96,768]{1,0:T(8,128)S(1)}, f32[96,768]{1,0:T(8,128)}, u32[]{:S(2)}) copy-start(f32[96,768]{1,0:T(8,128)} %get-tuple-element.131) | copy-start | bytes 884740
  (62 other events, 212.6 us)
Sparse Core Ops, SparseCore 0:
  11.6 70.0 all-gather.6
  84.7 67.5 all-gather.8
  155.4 74.4 all-gather.10
